TPU v7x, 32 devices: a whole 2x2x4 slice. The times are simulated.
32 devices in a mesh: fsdp: 8 (over y, x, core), tensor: 4 (over z).
Axes of the slice: x: 2, y: 2, z: 4, core: 2. Of those that a mesh axis runs over, the one named last changes fastest.
Arguments:
- tokens: bfloat16 [2, 8, 1024, 768], P(None, 'fsdp', 'tensor'), may hold values from -6 to 6
- lengths: int32 [2, 8], P(None, 'fsdp'), may hold values from 256 to 1024, as said below
- cotangent: bfloat16 [2, 8, 1024, 768], P(None, 'fsdp', 'tensor'), may hold values from -6 to 6
- query_proj: bfloat16 [768, 768], P('fsdp', 'tensor'), may hold values from -0.3125 to 0.3125
- key_proj: bfloat16 [768, 768], P('fsdp', 'tensor'), may hold values from -0.3125 to 0.3125
- value_proj: bfloat16 [768, 768], P('fsdp', 'tensor'), may hold values from -0.21875 to 0.21875
- output_proj: bfloat16 [768, 768], P('tensor', 'fsdp'), may hold values from -1.25 to 1.25
- expand_proj: bfloat16 [768, 3072], P('fsdp', 'tensor'), may hold values from -0.21875 to 0.21875
- shrink_proj: bfloat16 [3072, 768], P('tensor', 'fsdp'), may hold values from -0.109375 to 0.109375
- query_bias: bfloat16 [768], P(('tensor', 'fsdp')), may hold values from -3 to 3
- value_bias: bfloat16 [768], P(('tensor', 'fsdp')), may hold values from -3 to 3
- expand_bias: bfloat16 [3072], P(('tensor', 'fsdp')), may hold values from -3 to 3
- output_bias: bfloat16 [768], P('fsdp'), may hold values from -3 to 3
- attn_gain: bfloat16 [768], P('fsdp'), may hold values from 0.25 to 1.75
- attn_shift: bfloat16 [768], P('fsdp'), may hold values from -2 to 2
- shrink_bias: bfloat16 [768], P('fsdp'), may hold values from -3 to 3
- ffn_gain: bfloat16 [768], P('fsdp'), may hold values from 0.25 to 1.75
- ffn_shift: bfloat16 [768], P('fsdp'), may hold values from -2 to 2
Outputs:
- layer_out: bfloat16 [2, 8, 1024, 768], P(None, 'fsdp', 'tensor')
- input_grad: float32 [2, 8, 1024, 768], P(None, 'fsdp', 'tensor')
- grad_query: float32 [768, 768], P('fsdp', 'tensor')
- grad_key: float32 [768, 768], P('fsdp', 'tensor')
- grad_value: float32 [768, 768], P('fsdp', 'tensor')
- grad_output: float32 [768, 768], P('tensor', 'fsdp')
- grad_expand: float32 [768, 3072], P('fsdp', 'tensor')
- grad_shrink: float32 [3072, 768], P('tensor', 'fsdp')
- bgrad_query: float32 [768], P(('tensor', 'fsdp'))
- bgrad_value: float32 [768], P(('tensor', 'fsdp'))
- bgrad_expand: float32 [3072], P(('tensor', 'fsdp'))
- bgrad_output: float32 [768], P(('fsdp', 'tensor'))
- ggrad_attn: float32 [768], P(('fsdp', 'tensor'))
- sgrad_attn: float32 [768], P(('fsdp', 'tensor'))
- bgrad_shrink: float32 [768], P(('fsdp', 'tensor'))
- ggrad_ffn: float32 [768], P(('fsdp', 'tensor'))
- sgrad_ffn: float32 [768], P(('fsdp', 'tensor'))
Inputs may be any that keep to these rules, and one draw needn't show every extreme that they name: Sequence (m, s) holds live tokens in its first lengths[m, s] slots and padding after them. Some sequence fills all 1024 slots and some has exactly 256.
All inputs are finite; a program needn't handle non-finite values.
Results may differ from a plain program's by a relative error of at most 0.015.
Values may be sent and summed in bfloat16 or wider, within the bound.
No kernel may reach another device: no remote copies, remote signals or barrier semaphores. Data moves between devices by JAX's collectives and lax.ppermute only.
A program may use at most 128 MiB of HBM per device.

v0:
```python
import jax
import jax.numpy as jnp
from jax import lax
from jax.sharding import PartitionSpec as P

D = 768
HD = 64


EPS = 1e-05
NEG = -1000000000.0
ROOT_HALF = 0.7071067811865476
DENSITY = 0.3989422804014327


def contract(left, right, form):
    return jnp.einsum(form, left, right, preferred_element_type=jnp.float32)


def normalize(summed):
    center = summed - jnp.mean(summed, axis=-1, keepdims=True)
    spread = jnp.mean(center * center, axis=-1, keepdims=True)
    inv_scale = lax.rsqrt(spread + EPS)
    return (center * inv_scale, inv_scale)


def norm_back(grad, gain, unit, inv_scale):
    scaled = grad * gain
    return inv_scale * (
        scaled
        - jnp.mean(scaled, axis=-1, keepdims=True)
        - unit * jnp.mean(scaled * unit, axis=-1, keepdims=True)
    )


def gelu_slope(upper):
    return (
        0.5 * (1.0 + lax.erf(upper * ROOT_HALF)) + upper * jnp.exp(-0.5 * upper * upper) * DENSITY
    )


def attend_forward(query, keys, values, live):
    rows, width = query.shape
    heads_here = width // HD
    block = min(512, rows)
    number = rows // block
    key_heads = keys.reshape(rows, heads_here, HD)
    value_heads = values.reshape(rows, heads_here, HD)

    def one_block(query_block):
        query_heads = query_block.reshape(block, heads_here, HD)
        scores = contract(query_heads, key_heads, "qhd,khd->hqk") * 0.125
        scores = jnp.where(live[None, None, :], scores, NEG)
        top = jnp.max(scores, axis=-1, keepdims=True)
        raised = jnp.exp(scores - top)
        denom = jnp.sum(raised, axis=-1, keepdims=True)
        probs_low = (raised / denom).astype(jnp.bfloat16)
        attended = contract(probs_low, value_heads, "hqk,khd->qhd").astype(jnp.bfloat16)
        return (attended.reshape(block, width), (top + jnp.log(denom))[..., 0])

    attended, log_total = lax.map(one_block, query.reshape(number, block, width))
    return (attended.reshape(rows, width), log_total)


def attend_backward(query, keys, values, live, log_total, attended_grad):
    rows, width = query.shape
    heads_here = width // HD
    block = min(512, rows)
    number = rows // block
    key_heads = keys.reshape(rows, heads_here, HD)
    value_heads = values.reshape(rows, heads_here, HD)

    def one_block(carry, item):
        key_grad, value_grad = carry
        query_block, log_block, grad_block = item
        query_heads = query_block.reshape(block, heads_here, HD)
        grad_heads = grad_block.reshape(block, heads_here, HD)
        scores = contract(query_heads, key_heads, "qhd,khd->hqk") * 0.125
        scores = jnp.where(live[None, None, :], scores, NEG)
        probs = jnp.exp(scores - log_block[..., None])
        prob_grad = contract(grad_heads, value_heads, "qhd,khd->hqk")
        inner = jnp.sum(probs * prob_grad, axis=-1, keepdims=True)
        score_grad = (probs * (prob_grad - inner)).astype(jnp.bfloat16)
        query_grad = contract(score_grad, key_heads, "hqk,khd->qhd") * 0.125
        key_grad = key_grad + contract(score_grad, query_heads, "hqk,qhd->khd") * 0.125
        value_grad = value_grad + contract(probs.astype(jnp.bfloat16), grad_heads, "hqk,qhd->khd")
        return ((key_grad, value_grad), query_grad.reshape(block, width))

    start = jnp.zeros((rows, heads_here, HD), jnp.float32)
    (key_grad, value_grad), query_grad = lax.scan(
        one_block,
        (start, start),
        (
            query.reshape(number, block, width),
            log_total,
            attended_grad.reshape(number, block, width),
        ),
    )
    return (
        query_grad.reshape(rows, width),
        key_grad.reshape(rows, width),
        value_grad.reshape(rows, width),
    )


def shards(
    tokens,
    lengths,
    cotangent,
    query_proj,
    key_proj,
    value_proj,
    output_proj,
    expand_proj,
    shrink_proj,
    query_bias,
    value_bias,
    expand_bias,
    output_bias,
    attn_gain,
    attn_shift,
    shrink_bias,
    ffn_gain,
    ffn_shift,
):
    parts = lax.axis_size("tensor")
    place = lax.axis_index("tensor")
    local_rows = tokens.shape[2]
    rows = local_rows * parts
    width = query_proj.shape[1]
    hidden = expand_proj.shape[1]
    floating = jnp.float32

    def micro_step(carry, item):
        big_sums, small_sums = carry
        rows_local, length, cot_local = item
        gathered = (
            lax.all_gather(query_proj, "fsdp", axis=0, tiled=True),
            lax.all_gather(key_proj, "fsdp", axis=0, tiled=True),
            lax.all_gather(value_proj, "fsdp", axis=0, tiled=True),
            lax.all_gather(output_proj, "fsdp", axis=1, tiled=True),
            lax.all_gather(query_bias, "fsdp", axis=0, tiled=True),
            lax.all_gather(value_bias, "fsdp", axis=0, tiled=True),
            lax.all_gather(output_bias, "fsdp", axis=0, tiled=True),
            lax.all_gather(attn_gain, "fsdp", axis=0, tiled=True),
            lax.all_gather(attn_shift, "fsdp", axis=0, tiled=True),
            lax.all_gather(shrink_bias, "fsdp", axis=0, tiled=True),
            lax.all_gather(ffn_gain, "fsdp", axis=0, tiled=True),
            lax.all_gather(ffn_shift, "fsdp", axis=0, tiled=True),
        )
        (
            query_w,
            key_w,
            value_w,
            output_w,
            query_b,
            value_b,
            output_b,
            gain_one,
            shift_one,
            shrink_b,
            gain_two,
            shift_two,
        ) = gathered
        expand_w, shrink_w, expand_b = (
            lax.all_gather(expand_proj, "fsdp", axis=0, tiled=True),
            lax.all_gather(shrink_proj, "fsdp", axis=1, tiled=True),
            lax.all_gather(expand_bias, "fsdp", axis=0, tiled=True),
        )
        slot_index = place * local_rows + jnp.arange(local_rows)
        live_rows = (slot_index < length).astype(floating)
        live = jnp.arange(rows) < length
        rows_all = lax.all_gather(rows_local, "tensor", axis=0, tiled=True)
        query = (contract(rows_all, query_w, "rd,dk->rk") + query_b.astype(floating)).astype(
            jnp.bfloat16
        )
        keys = contract(rows_all, key_w, "rd,dk->rk").astype(jnp.bfloat16)
        values = (contract(rows_all, value_w, "rd,dk->rk") + value_b.astype(floating)).astype(
            jnp.bfloat16
        )
        attended, log_total = attend_forward(query, keys, values, live)
        attn_part = contract(attended, output_w, "rk,kd->rd")
        attn_sum = lax.psum_scatter(attn_part, "tensor", scatter_dimension=0, tiled=True)
        first_sum = rows_local.astype(floating) + attn_sum + output_b.astype(floating)
        first_unit, first_scale = normalize(first_sum)
        normed = first_unit * gain_one.astype(floating) + shift_one.astype(floating)
        ffn_in = lax.all_gather(normed.astype(jnp.bfloat16), "tensor", axis=0, tiled=True)
        upper = contract(ffn_in, expand_w, "rd,dk->rk") + expand_b.astype(floating)
        active = jax.nn.gelu(upper, approximate=False).astype(jnp.bfloat16)
        ffn_part = contract(active, shrink_w, "rk,kd->rd")
        ffn_sum = lax.psum_scatter(ffn_part, "tensor", scatter_dimension=0, tiled=True)
        second_sum = normed + ffn_sum + shrink_b.astype(floating)
        second_unit, second_scale = normalize(second_sum)
        layer_rows = (second_unit * gain_two.astype(floating) + shift_two.astype(floating)).astype(
            jnp.bfloat16
        )
        back = (
            lax.all_gather(query_proj, "fsdp", axis=0, tiled=True),
            lax.all_gather(key_proj, "fsdp", axis=0, tiled=True),
            lax.all_gather(value_proj, "fsdp", axis=0, tiled=True),
            lax.all_gather(output_proj, "fsdp", axis=1, tiled=True),
            lax.all_gather(attn_gain, "fsdp", axis=0, tiled=True),
            lax.all_gather(ffn_gain, "fsdp", axis=0, tiled=True),
        )
        ffn_back = (
            lax.all_gather(expand_proj, "fsdp", axis=0, tiled=True),
            lax.all_gather(shrink_proj, "fsdp", axis=1, tiled=True),
        )
        out_grad = cot_local.astype(floating) * live_rows[:, None]
        grad_gain_two = jnp.sum(out_grad * second_unit, axis=0)
        grad_shift_two = jnp.sum(out_grad, axis=0)
        second_grad = norm_back(out_grad, back[5].astype(floating), second_unit, second_scale)
        grad_shrink_b = jnp.sum(second_grad, axis=0)
        second_all = lax.all_gather(second_grad.astype(jnp.bfloat16), "tensor", axis=0, tiled=True)
        grad_shrink_w = contract(active, second_all, "rk,rd->kd")
        upper_grad = contract(second_all, ffn_back[1], "rd,kd->rk") * gelu_slope(upper)
        grad_expand_b = jnp.sum(upper_grad, axis=0)
        upper_low = upper_grad.astype(jnp.bfloat16)
        grad_expand_w = contract(ffn_in, upper_low, "rd,rk->dk")
        normed_part = contract(upper_low, ffn_back[0], "rk,dk->rd")
        normed_grad = (
            lax.psum_scatter(normed_part, "tensor", scatter_dimension=0, tiled=True) + second_grad
        )
        grad_gain_one = jnp.sum(normed_grad * first_unit, axis=0)
        grad_shift_one = jnp.sum(normed_grad, axis=0)
        first_grad = norm_back(normed_grad, back[4].astype(floating), first_unit, first_scale)
        grad_output_b = jnp.sum(first_grad, axis=0)
        first_all = lax.all_gather(first_grad.astype(jnp.bfloat16), "tensor", axis=0, tiled=True)
        grad_output_w = contract(attended, first_all, "rk,rd->kd")
        attended_grad = contract(first_all, back[3], "rd,kd->rk").astype(jnp.bfloat16)
        query_grad, key_grad, value_grad = attend_backward(
            query, keys, values, live, log_total, attended_grad
        )
        grad_query_b = jnp.sum(query_grad, axis=0)
        grad_value_b = jnp.sum(value_grad, axis=0)
        query_low = query_grad.astype(jnp.bfloat16)
        key_low = key_grad.astype(jnp.bfloat16)
        value_low = value_grad.astype(jnp.bfloat16)
        grad_query_w = contract(rows_all, query_low, "rd,rk->dk")
        grad_key_w = contract(rows_all, key_low, "rd,rk->dk")
        grad_value_w = contract(rows_all, value_low, "rd,rk->dk")
        input_part = (
            contract(query_low, back[0], "rk,dk->rd")
            + contract(key_low, back[1], "rk,dk->rd")
            + contract(value_low, back[2], "rk,dk->rd")
        )
        rows_grad = (
            lax.psum_scatter(
                input_part.astype(jnp.bfloat16), "tensor", scatter_dimension=0, tiled=True
            ).astype(jnp.float32)
            + first_grad
        )
        big_terms = (
            grad_query_w,
            grad_key_w,
            grad_value_w,
            grad_output_w,
            grad_expand_w,
            grad_shrink_w,
            grad_query_b,
            grad_value_b,
            grad_expand_b,
        )
        small_terms = (
            grad_output_b,
            grad_gain_one,
            grad_shift_one,
            grad_shrink_b,
            grad_gain_two,
            grad_shift_two,
        )
        carry = (
            jax.tree.map(jnp.add, big_sums, big_terms),
            jax.tree.map(jnp.add, small_sums, small_terms),
        )
        return (carry, (layer_rows, rows_grad))

    big_start = (
        jnp.zeros((D, width), floating),
        jnp.zeros((D, width), floating),
        jnp.zeros((D, width), floating),
        jnp.zeros((width, D), floating),
        jnp.zeros((D, hidden), floating),
        jnp.zeros((hidden, D), floating),
        jnp.zeros((width,), floating),
        jnp.zeros((width,), floating),
        jnp.zeros((hidden,), floating),
    )
    small_start = tuple((jnp.zeros((D,), floating) for place_holder in range(6)))
    (big_total, small_total), (layer_rows, rows_grads) = lax.scan(
        micro_step, (big_start, small_start), (tokens[:, 0], lengths[:, 0], cotangent[:, 0])
    )
    ffn_grads = (big_total[4], big_total[5], big_total[8])
    reduced = (
        lax.psum_scatter(big_total[0], "fsdp", scatter_dimension=0, tiled=True),
        lax.psum_scatter(big_total[1], "fsdp", scatter_dimension=0, tiled=True),
        lax.psum_scatter(big_total[2], "fsdp", scatter_dimension=0, tiled=True),
        lax.psum_scatter(big_total[3], "fsdp", scatter_dimension=1, tiled=True),
        lax.psum_scatter(ffn_grads[0], "fsdp", scatter_dimension=0, tiled=True),
        lax.psum_scatter(ffn_grads[1], "fsdp", scatter_dimension=1, tiled=True),
        lax.psum_scatter(big_total[6], "fsdp", scatter_dimension=0, tiled=True),
        lax.psum_scatter(big_total[7], "fsdp", scatter_dimension=0, tiled=True),
        lax.psum_scatter(ffn_grads[2], "fsdp", scatter_dimension=0, tiled=True),
    )
    norms = (
        lax.psum_scatter(small_total[0], ("fsdp", "tensor"), scatter_dimension=0, tiled=True),
        lax.psum_scatter(small_total[1], ("fsdp", "tensor"), scatter_dimension=0, tiled=True),
        lax.psum_scatter(small_total[2], ("fsdp", "tensor"), scatter_dimension=0, tiled=True),
        lax.psum_scatter(small_total[3], ("fsdp", "tensor"), scatter_dimension=0, tiled=True),
        lax.psum_scatter(small_total[4], ("fsdp", "tensor"), scatter_dimension=0, tiled=True),
        lax.psum_scatter(small_total[5], ("fsdp", "tensor"), scatter_dimension=0, tiled=True),
    )
    return (
        layer_rows[:, None],
        rows_grads[:, None],
        reduced[0],
        reduced[1],
        reduced[2],
        reduced[3],
        reduced[4],
        reduced[5],
        reduced[6],
        reduced[7],
        reduced[8],
        norms[0],
        norms[1],
        norms[2],
        norms[3],
        norms[4],
        norms[5],
    )


def solution(mesh):
    placed = (
        P(None, "fsdp", "tensor", None),
        P(None, "fsdp"),
        P(None, "fsdp", "tensor", None),
        P("fsdp", "tensor"),
        P("fsdp", "tensor"),
        P("fsdp", "tensor"),
        P("tensor", "fsdp"),
        P("fsdp", "tensor"),
        P("tensor", "fsdp"),
        P(("tensor", "fsdp")),
        P(("tensor", "fsdp")),
        P(("tensor", "fsdp")),
        P("fsdp"),
        P("fsdp"),
        P("fsdp"),
        P("fsdp"),
        P("fsdp"),
        P("fsdp"),
    )
    return jax.shard_map(
        shards,
        mesh=mesh,
        in_specs=placed,
        out_specs=(
            P(None, "fsdp", "tensor", None),
            P(None, "fsdp", "tensor", None),
            P("fsdp", "tensor"),
            P("fsdp", "tensor"),
            P("fsdp", "tensor"),
            P("tensor", "fsdp"),
            P("fsdp", "tensor"),
            P("tensor", "fsdp"),
            P(("tensor", "fsdp")),
            P(("tensor", "fsdp")),
            P(("tensor", "fsdp")),
            P(("fsdp", "tensor")),
            P(("fsdp", "tensor")),
            P(("fsdp", "tensor")),
            P(("fsdp", "tensor")),
            P(("fsdp", "tensor")),
            P(("fsdp", "tensor")),
        ),
        check_vma=False,
    )
```

profile of v0, /device:TPU:0, one launch (start us, length us, event | category | flops | bytes accessed | tf_op | source)
XLA Modules:
  0.0 1267.7 jit_solution(17105940230689582696)
XLA Ops:
  9.7 1003.4 %while.95 = (s32[]{:T(128)}, f32[768,192]{0,1:T(8,128)}, f32[768,192]{0,1:T(8,128)}, f32[768,192]{0,1:T(8,128)}, f32[192,768]{1,0:T(8,128)}, /*index=5*/f32[768,...) while((s32[]{:T(128)}, f32[768,192]{0,1:T(8,128)}, ...), condition=%wide.region_29.30_spmd.clone, body=%wide.region_0.29_spmd.clone.sunk | while | flops 12407750656 | bytes 348198464 | solution.py:290
  22.9 27.7 %all-reduce.31 = (bf16[192]{0:T(256)(128)(2,1)S(1)}, bf16[192]{0:T(256)(128)(2,1)S(1)}, bf16[768]{0:T(1024)(128)(2,1)S(1)}, bf16[768]{0:T(1024)(128)(2,1)S(1)}, ...) all-reduce(bf16[192]{0:T(256)(128)(2,1)S(1)} %dynamic-update-slice., ...), channel_id=1, replica_groups=mesh['fsdp'=8,'tensor'=4] {'fsdp'}, use_global_device_ids=true, to_apply=%add | all-reduce | flops 5760 | bytes 23040 | tf_op jit(solution)/shard_map/while
  50.6 8.8 all_gather.124
  59.4 9.3 all_gather.123
  68.7 8.8 all_gather.122
  77.6 9.3 all_gather.121
  86.9 2.3 fusion.261
  90.6 10.9 while.96
  101.6 2.3 fusion.264
  104.6 60.0 %reduce-scatter.25.cloned.1.call-done = f32[256,768]{1,0:T(8,128)} async-done(((f32[1024,768]{1,0:T(8,128)}), f32[256,768]{1,0:T(8,128)}) %reduce-scatter.25.cloned.1.call-update) | async-done | bytes 786448 | tf_op jit(solution)/shard_map/while/body/eval_jaxpr/reduce_scatter | solution.py:183
  167.9 36.4 %all-gather.15.cloned.1.call-done = bf16[1024,768]{1,0:T(8,128)(2,1)} async-done(((bf16[256,768]{1,0:T(8,128)(2,1)}), bf16[1024,768]{1,0:T(8,128)(2,1)}) %all-gather.15.cloned.1.call-update) | async-done | bytes 1572880 | tf_op jit(solution)/shard_map/while/body/eval_jaxpr/all_gather | solution.py:187
  204.3 10.6 fusion.267
  214.9 13.9 %all-gather.17.cloned.1.call-done = bf16[768,768]{0,1:T(8,128)(2,1)} async-done(((bf16[768,96]{0,1:T(8,128)(2,1)}), bf16[768,768]{0,1:T(8,128)(2,1)}) %all-gather.17.cloned.1.call-update) | async-done | bytes 1179664 | tf_op jit(solution)/shard_map/while/body/eval_jaxpr/all_gather | solution.py:167
  228.8 4.8 fusion.268
  236.1 57.9 %reduce-scatter.27.cloned.1.call-done = f32[256,768]{1,0:T(8,128)} async-done(((f32[1024,768]{1,0:T(8,128)}), f32[256,768]{1,0:T(8,128)}) %reduce-scatter.27.cloned.1.call-update) | async-done | bytes 786448 | tf_op jit(solution)/shard_map/while/body/eval_jaxpr/reduce_scatter | solution.py:191
  299.6 37.1 %all-gather.19.cloned.1.call-done = bf16[1024,768]{1,0:T(8,128)(2,1)} async-done(((bf16[256,768]{1,0:T(8,128)(2,1)}), bf16[1024,768]{1,0:T(8,128)(2,1)}) %all-gather.19.cloned.1.call-update) | async-done | bytes 1572880 | tf_op jit(solution)/shard_map/while/body/eval_jaxpr/all_gather | solution.py:214
  336.7 5.5 fusion.272
  343.4 3.1 fusion.273
  346.6 59.2 %reduce-scatter.29.cloned.1.call-done = f32[256,768]{1,0:T(8,128)} async-done(((f32[1024,768]{1,0:T(8,128)}), f32[256,768]{1,0:T(8,128)}) %reduce-scatter.29.cloned.1.call-update) | async-done | bytes 786448 | tf_op jit(solution)/shard_map/while/body/eval_jaxpr/reduce_scatter | solution.py:222
  405.8 2.2 multiply_reduce_fusion.12
  413.4 33.4 %all-gather.21.cloned.1.call-done = bf16[1024,768]{1,0:T(8,128)(2,1)} async-done(((bf16[256,768]{1,0:T(8,128)(2,1)}), bf16[1024,768]{1,0:T(8,128)(2,1)}) %all-gather.21.cloned.1.call-update) | async-done | bytes 1572880 | tf_op jit(solution)/shard_map/while/body/eval_jaxpr/all_gather | solution.py:228
  448.9 20.7 %while.97 = (s32[]{:T(128)}, f32[1024,3,64]{0,2,1:T(8,128)S(1)}, f32[1024,3,64]{0,2,1:T(8,128)}, f32[2,512,192]{1,2,0:T(8,128)}, bf16[2,512,192]{1,2,0:T(8,128)(...) while((s32[]{:T(128)}, f32[1024,3,64]{0,2,1:T(8,128)S(1)}, ...), condition=%wide.region_18.18_spmd.clone, body=%wide.region_16.17_spmd.clone.sunk | while | flops 1031306752 | bytes 66894084 | solution.py:90
  469.7 2.2 fusion.275
  475.8 4.9 select_add_fusion.20
  480.8 2.9 select_add_fusion.19
  485.1 2.8 convolution_add_fusion.2
  491.4 18.5 %reduce-scatter.31.cloned.1.call-done = bf16[256,768]{1,0:T(8,128)(2,1)} async-done(((bf16[1024,768]{1,0:T(8,128)(2,1)}), bf16[256,768]{1,0:T(8,128)(2,1)}) %reduce-scatter.31.cloned.1.call-update) | async-done | bytes 393232 | tf_op jit(solution)/shard_map/while/body/eval_jaxpr/reduce_scatter | solution.py:248
  525.1 25.8 %all-reduce.31 = (bf16[192]{0:T(256)(128)(2,1)S(1)}, bf16[192]{0:T(256)(128)(2,1)S(1)}, bf16[768]{0:T(1024)(128)(2,1)S(1)}, bf16[768]{0:T(1024)(128)(2,1)S(1)}, ...) all-reduce(bf16[192]{0:T(256)(128)(2,1)S(1)} %dynamic-update-slice., ...), channel_id=1, replica_groups=mesh['fsdp'=8,'tensor'=4] {'fsdp'}, use_global_device_ids=true, to_apply=%add | all-reduce | flops 5760 | bytes 23040 | tf_op jit(solution)/shard_map/while
  551.0 8.8 all_gather.124
  559.8 9.3 all_gather.123
  569.1 8.8 all_gather.122
  577.9 9.3 all_gather.121
  587.3 2.3 fusion.261
  591.0 10.9 while.96
  602.0 2.3 fusion.264
  605.0 57.9 %reduce-scatter.25.cloned.1.call-done = f32[256,768]{1,0:T(8,128)} async-done(((f32[1024,768]{1,0:T(8,128)}), f32[256,768]{1,0:T(8,128)}) %reduce-scatter.25.cloned.1.call-update) | async-done | bytes 786448 | tf_op jit(solution)/shard_map/while/body/eval_jaxpr/reduce_scatter | solution.py:183
  666.2 36.4 %all-gather.15.cloned.1.call-done = bf16[1024,768]{1,0:T(8,128)(2,1)} async-done(((bf16[256,768]{1,0:T(8,128)(2,1)}), bf16[1024,768]{1,0:T(8,128)(2,1)}) %all-gather.15.cloned.1.call-update) | async-done | bytes 1572880 | tf_op jit(solution)/shard_map/while/body/eval_jaxpr/all_gather | solution.py:187
  702.5 10.6 fusion.267
  713.2 13.9 %all-gather.17.cloned.1.call-done = bf16[768,768]{0,1:T(8,128)(2,1)} async-done(((bf16[768,96]{0,1:T(8,128)(2,1)}), bf16[768,768]{0,1:T(8,128)(2,1)}) %all-gather.17.cloned.1.call-update) | async-done | bytes 1179664 | tf_op jit(solution)/shard_map/while/body/eval_jaxpr/all_gather | solution.py:167
  727.1 4.8 fusion.268
  734.4 57.9 %reduce-scatter.27.cloned.1.call-done = f32[256,768]{1,0:T(8,128)} async-done(((f32[1024,768]{1,0:T(8,128)}), f32[256,768]{1,0:T(8,128)}) %reduce-scatter.27.cloned.1.call-update) | async-done | bytes 786448 | tf_op jit(solution)/shard_map/while/body/eval_jaxpr/reduce_scatter | solution.py:191
  797.9 37.1 %all-gather.19.cloned.1.call-done = bf16[1024,768]{1,0:T(8,128)(2,1)} async-done(((bf16[256,768]{1,0:T(8,128)(2,1)}), bf16[1024,768]{1,0:T(8,128)(2,1)}) %all-gather.19.cloned.1.call-update) | async-done | bytes 1572880 | tf_op jit(solution)/shard_map/while/body/eval_jaxpr/all_gather | solution.py:214
  835.0 5.5 fusion.272
  841.7 3.1 fusion.273
  844.8 59.2 %reduce-scatter.29.cloned.1.call-done = f32[256,768]{1,0:T(8,128)} async-done(((f32[1024,768]{1,0:T(8,128)}), f32[256,768]{1,0:T(8,128)}) %reduce-scatter.29.cloned.1.call-update) | async-done | bytes 786448 | tf_op jit(solution)/shard_map/while/body/eval_jaxpr/reduce_scatter | solution.py:222
  904.1 2.2 multiply_reduce_fusion.12
  911.7 33.4 %all-gather.21.cloned.1.call-done = bf16[1024,768]{1,0:T(8,128)(2,1)} async-done(((bf16[256,768]{1,0:T(8,128)(2,1)}), bf16[1024,768]{1,0:T(8,128)(2,1)}) %all-gather.21.cloned.1.call-update) | async-done | bytes 1572880 | tf_op jit(solution)/shard_map/while/body/eval_jaxpr/all_gather | solution.py:228
  945.0 2.1 convolution_convert_fusion.2
  947.2 20.7 %while.97 = (s32[]{:T(128)}, f32[1024,3,64]{0,2,1:T(8,128)S(1)}, f32[1024,3,64]{0,2,1:T(8,128)}, f32[2,512,192]{1,2,0:T(8,128)}, bf16[2,512,192]{1,2,0:T(8,128)(...) while((s32[]{:T(128)}, f32[1024,3,64]{0,2,1:T(8,128)S(1)}, ...), condition=%wide.region_18.18_spmd.clone, body=%wide.region_16.17_spmd.clone.sunk | while | flops 1031306752 | bytes 66894084 | solution.py:90
  968.0 2.2 fusion.275
  974.1 5.6 select_add_fusion.20
  979.8 4.6 select_add_fusion.19
  985.8 2.9 convolution_add_fusion.2
  991.0 2.4 fusion.276
  993.4 14.9 %reduce-scatter.31.cloned.1.call-done = bf16[256,768]{1,0:T(8,128)(2,1)} async-done(((bf16[1024,768]{1,0:T(8,128)(2,1)}), bf16[256,768]{1,0:T(8,128)(2,1)}) %reduce-scatter.31.cloned.1.call-update) | async-done | bytes 393232 | tf_op jit(solution)/shard_map/while/body/eval_jaxpr/reduce_scatter | solution.py:248
  1013.2 2.3 copy.61
  1015.6 2.2 copy.57
  1025.2 13.6 %all-reduce.29 = (f32[192]{0:T(256)S(1)}, f32[192]{0:T(256)S(1)}, f32[768]{0:T(1024)S(1)}) all-reduce(f32[192]{0:T(256)S(1)} %copy-done.70, f32[192]{0:T(256)S(1)} %copy-done.67, f32[768]{0:T(1024)S(1)} %copy-done.43), channel_id=13, replica_groups=mesh['fsdp'=8,'tensor'=4] {'fsdp'}, use_global_device_ids=true, to_apply=%region_36.37.clone | all-reduce | flops 1152 | bytes 9216
  1040.0 38.9 %all-reduce.28 = (f32[768]{0:T(1024)S(1)}, f32[768]{0:T(1024)S(1)}, f32[768]{0:T(1024)S(1)}, f32[768]{0:T(1024)S(1)}, f32[768]{0:T(1024)S(1)}, /*index=5*/f32[768]{0:T(1024)S(1)}) all-reduce(f32[768]{0:T(1024)S(1)} %copy-done.57, f32[768]{0:T(1024)S(1)} %copy-done.54, ...), channel_id=16, replica_groups=mesh['fsdp'=8,'tensor'=4] {'fsdp','tensor'}, use_global_device_ids=true, to_apply=%region_39.40.clone | all-reduce | flops 4608 | bytes 36864
  1084.6 5.2 reduce-scatter.13.cloned.1.call-done
  1089.8 38.8 %reduce-scatter.15.cloned.1.call-done = f32[96,192]{1,0:T(8,128)} async-done(((f32[768,192]{1,0:T(8,128)}), f32[96,192]{1,0:T(8,128)}) %reduce-scatter.15.cloned.1.call-update) | async-done | bytes 73744 | tf_op jit(solution)/shard_map/reduce_scatter | solution.py:296
  1128.5 38.6 %reduce-scatter.17.cloned.1.call-done = f32[96,192]{1,0:T(8,128)} async-done(((f32[768,192]{1,0:T(8,128)}), f32[96,192]{1,0:T(8,128)}) %reduce-scatter.17.cloned.1.call-update) | async-done | bytes 73744 | tf_op jit(solution)/shard_map/reduce_scatter | solution.py:297
  1167.1 46.4 %reduce-scatter.19.cloned.1.call-done = f32[96,768]{1,0:T(8,128)} async-done(((f32[768,768]{1,0:T(8,128)}), f32[96,768]{1,0:T(8,128)}) %reduce-scatter.19.cloned.1.call-update) | async-done | bytes 294928 | tf_op jit(solution)/shard_map/reduce_scatter | solution.py:299
  1213.6 46.6 %reduce-scatter.21.cloned.1.call-done = f32[768,96]{0,1:T(8,128)} async-done(((f32[768,768]{0,1:T(8,128)}), f32[768,96]{0,1:T(8,128)}) %reduce-scatter.21.cloned.1.call-update) | async-done | bytes 294928 | tf_op jit(solution)/shard_map/reduce_scatter | solution.py:300
  (605 shorter events, 162.5 us)
Async XLA Ops:
  9.7 77.2 %all-gather.11.cloned.1.call-start = ((), (), s32[]{:S(2)}) async-start(), calls=%async_computation.16 | async-start | bytes 1966080 | tf_op jit(solution)/shard_map/while/body/eval_jaxpr/all_gather | solution.py:173
  11.5 153.1 %reduce-scatter.25.cloned.1.call-start = ((), (), s32[]{:S(2)}) async-start(), calls=%async_computation.17 | async-start | bytes 3932160 | tf_op jit(solution)/shard_map/while/body/eval_jaxpr/reduce_scatter | solution.py:183
  59.4 42.1 %copy-start.6 = (bf16[192,768]{0,1:T(8,128)(2,1)}, bf16[192,768]{0,1:T(8,128)(2,1)S(1)}, u32[]{:S(2)}) copy-start(bf16[192,768]{0,1:T(8,128)(2,1)S(1)} %all_gather.124) | copy-start | bytes 884740 | tf_op jit(solution)/shard_map/while
  68.7 21.2 %copy-start.2 = (bf16[768,192]{1,0:T(8,128)(2,1)}, bf16[768,192]{1,0:T(8,128)(2,1)S(1)}, u32[]{:S(2)}) copy-start(bf16[768,192]{1,0:T(8,128)(2,1)S(1)} %all_gather.123) | copy-start | bytes 884740 | tf_op jit(solution)/shard_map/while
  77.6 11.6 copy-start.4
  101.6 63.0 %copy-start.27 = (bf16[2,256,768]{2,1,0:T(8,128)(2,1)S(1)}, bf16[2,256,768]{2,1,0:T(8,128)(2,1)}, u32[]{:S(2)}) copy-start(bf16[2,256,768]{2,1,0:T(8,128)(2,1)} %get-tuple-element.1628) | copy-start | bytes 2359300 | tf_op jit(solution)/shard_map/while
  103.9 63.9 %copy-start.64 = (bf16[768]{0:T(1024)(128)(2,1)S(1)}, bf16[768]{0:T(1024)(128)(2,1)}, u32[]{:S(2)}) copy-start(bf16[768]{0:T(1024)(128)(2,1)} %get-tuple-element.1395) | copy-start | bytes 4612 | tf_op jit(solution)/shard_map/while
  103.9 63.9 %all-gather.13.cloned.1.call-start = ((), (), s32[]{:S(2)}) async-start(), calls=%async_computation.18 | async-start | bytes 1327104 | tf_op jit(solution)/shard_map/while/body/eval_jaxpr/all_gather | solution.py:166
  104.5 99.7 %all-gather.15.cloned.1.call-start = ((), (), s32[]{:S(2)}) async-start(), calls=%async_computation.19 | async-start | bytes 1966080 | tf_op jit(solution)/shard_map/while/body/eval_jaxpr/all_gather | solution.py:187
  166.2 48.7 %copy-start.32 = (f32[256]{0:T(256)}, f32[256]{0:T(256)S(1)}, u32[]{:S(2)}) copy-start(f32[256]{0:T(256)S(1)} %add_rsqrt_fusion.4) | copy-start | bytes 3076 | tf_op jit(solution)/shard_map/while
  167.2 61.6 %all-gather.17.cloned.1.call-start = ((), (), s32[]{:S(2)}) async-start(), calls=%async_computation.20 | async-start | bytes 1327104 | tf_op jit(solution)/shard_map/while/body/eval_jaxpr/all_gather | solution.py:167
  167.7 126.3 %reduce-scatter.27.cloned.1.call-start = ((), (), s32[]{:S(2)}) async-start(), calls=%async_computation.21 | async-start | bytes 3932160 | tf_op jit(solution)/shard_map/while/body/eval_jaxpr/reduce_scatter | solution.py:191
  167.8 47.1 %copy-start.59 = (f32[768]{0:T(1024)}, f32[768]{0:T(1024)S(1)}, u32[]{:S(2)}) copy-start(f32[768]{0:T(1024)S(1)} %convert_element_type.279) | copy-start | bytes 9220 | tf_op jit(solution)/shard_map/while
  233.6 62.2 %copy-start.24 = (bf16[2,256,768]{2,1,0:T(8,128)(2,1)S(1)}, bf16[2,256,768]{2,1,0:T(8,128)(2,1)}, u32[]{:S(2)}) copy-start(bf16[2,256,768]{2,1,0:T(8,128)(2,1)} %get-tuple-element.1643) | copy-start | bytes 2359300 | tf_op jit(solution)/shard_map/while
  233.7 103.1 %all-gather.19.cloned.1.call-start = ((), (), s32[]{:S(2)}) async-start(), calls=%async_computation.22 | async-start | bytes 1966080 | tf_op jit(solution)/shard_map/while/body/eval_jaxpr/all_gather | solution.py:214
  234.3 64.4 %copy-start.31 = (f32[768]{0:T(1024)}, f32[768]{0:T(1024)S(1)}, u32[]{:S(2)}) copy-start(f32[768]{0:T(1024)S(1)} %convert_element_type.282) | copy-start | bytes 9220 | tf_op jit(solution)/shard_map/while
  295.5 41.2 %copy-start.60 = (f32[768]{0:T(1024)S(1)}, f32[768]{0:T(1024)}, u32[]{:S(2)}) copy-start(f32[768]{0:T(1024)} %copy-done.59) | copy-start | bytes 9220 | tf_op jit(solution)/shard_map/while
  299.6 106.2 %reduce-scatter.29.cloned.1.call-start = ((), (), s32[]{:S(2)}) async-start(), calls=%async_computation.23 | async-start | bytes 3932160 | tf_op jit(solution)/shard_map/while/body/eval_jaxpr/reduce_scatter | solution.py:222
  336.7 6.7 copy-start.72
  346.5 59.3 %copy-start.33 = (f32[256]{0:T(256)S(1)}, f32[256]{0:T(256)}, u32[]{:S(2)}) copy-start(f32[256]{0:T(256)} %copy-done.32) | copy-start | bytes 3076 | tf_op jit(solution)/shard_map/while
  346.5 100.2 %all-gather.21.cloned.1.call-start = ((), (), s32[]{:S(2)}) async-start(), calls=%async_computation.24 | async-start | bytes 1966080 | tf_op jit(solution)/shard_map/while/body/eval_jaxpr/all_gather | solution.py:228
  408.9 40.1 %copy-start.29 = (f32[2,3,512]{2,1,0:T(4,128)S(1)}, f32[2,3,512]{2,1,0:T(4,128)}, u32[]{:S(2)}) copy-start(f32[2,3,512]{2,1,0:T(4,128)} %copy-done.28) | copy-start | bytes 36868 | tf_op jit(solution)/shard_map/while
  409.7 100.3 %reduce-scatter.31.cloned.1.call-start = ((), (), s32[]{:S(2)}) async-start(), calls=%async_computation.25 | async-start | bytes 1966080 | tf_op jit(solution)/shard_map/while/body/eval_jaxpr/reduce_scatter | solution.py:248
  511.9 75.3 %all-gather.11.cloned.1.call-start = ((), (), s32[]{:S(2)}) async-start(), calls=%async_computation.16 | async-start | bytes 1966080 | tf_op jit(solution)/shard_map/while/body/eval_jaxpr/all_gather | solution.py:173
  513.7 149.2 %reduce-scatter.25.cloned.1.call-start = ((), (), s32[]{:S(2)}) async-start(), calls=%async_computation.17 | async-start | bytes 3932160 | tf_op jit(solution)/shard_map/while/body/eval_jaxpr/reduce_scatter | solution.py:183
  559.8 42.1 %copy-start.6 = (bf16[192,768]{0,1:T(8,128)(2,1)}, bf16[192,768]{0,1:T(8,128)(2,1)S(1)}, u32[]{:S(2)}) copy-start(bf16[192,768]{0,1:T(8,128)(2,1)S(1)} %all_gather.124) | copy-start | bytes 884740 | tf_op jit(solution)/shard_map/while
  569.1 21.2 %copy-start.2 = (bf16[768,192]{1,0:T(8,128)(2,1)}, bf16[768,192]{1,0:T(8,128)(2,1)S(1)}, u32[]{:S(2)}) copy-start(bf16[768,192]{1,0:T(8,128)(2,1)S(1)} %all_gather.123) | copy-start | bytes 884740 | tf_op jit(solution)/shard_map/while
  577.9 11.6 copy-start.4
  601.9 61.0 %copy-start.27 = (bf16[2,256,768]{2,1,0:T(8,128)(2,1)S(1)}, bf16[2,256,768]{2,1,0:T(8,128)(2,1)}, u32[]{:S(2)}) copy-start(bf16[2,256,768]{2,1,0:T(8,128)(2,1)} %get-tuple-element.1628) | copy-start | bytes 2359300 | tf_op jit(solution)/shard_map/while
  604.2 61.9 %copy-start.64 = (bf16[768]{0:T(1024)(128)(2,1)S(1)}, bf16[768]{0:T(1024)(128)(2,1)}, u32[]{:S(2)}) copy-start(bf16[768]{0:T(1024)(128)(2,1)} %get-tuple-element.1395) | copy-start | bytes 4612 | tf_op jit(solution)/shard_map/while
  604.3 61.9 %all-gather.13.cloned.1.call-start = ((), (), s32[]{:S(2)}) async-start(), calls=%async_computation.18 | async-start | bytes 1327104 | tf_op jit(solution)/shard_map/while/body/eval_jaxpr/all_gather | solution.py:166
  604.9 97.7 %all-gather.15.cloned.1.call-start = ((), (), s32[]{:S(2)}) async-start(), calls=%async_computation.19 | async-start | bytes 1966080 | tf_op jit(solution)/shard_map/while/body/eval_jaxpr/all_gather | solution.py:187
  664.5 48.7 %copy-start.32 = (f32[256]{0:T(256)}, f32[256]{0:T(256)S(1)}, u32[]{:S(2)}) copy-start(f32[256]{0:T(256)S(1)} %add_rsqrt_fusion.4) | copy-start | bytes 3076 | tf_op jit(solution)/shard_map/while
  665.5 61.6 %all-gather.17.cloned.1.call-start = ((), (), s32[]{:S(2)}) async-start(), calls=%async_computation.20 | async-start | bytes 1327104 | tf_op jit(solution)/shard_map/while/body/eval_jaxpr/all_gather | solution.py:167
  666.0 126.3 %reduce-scatter.27.cloned.1.call-start = ((), (), s32[]{:S(2)}) async-start(), calls=%async_computation.21 | async-start | bytes 3932160 | tf_op jit(solution)/shard_map/while/body/eval_jaxpr/reduce_scatter | solution.py:191
  666.1 47.1 %copy-start.59 = (f32[768]{0:T(1024)}, f32[768]{0:T(1024)S(1)}, u32[]{:S(2)}) copy-start(f32[768]{0:T(1024)S(1)} %convert_element_type.279) | copy-start | bytes 9220 | tf_op jit(solution)/shard_map/while
  731.9 62.2 %copy-start.24 = (bf16[2,256,768]{2,1,0:T(8,128)(2,1)S(1)}, bf16[2,256,768]{2,1,0:T(8,128)(2,1)}, u32[]{:S(2)}) copy-start(bf16[2,256,768]{2,1,0:T(8,128)(2,1)} %get-tuple-element.1643) | copy-start | bytes 2359300 | tf_op jit(solution)/shard_map/while
  732.0 103.1 %all-gather.19.cloned.1.call-start = ((), (), s32[]{:S(2)}) async-start(), calls=%async_computation.22 | async-start | bytes 1966080 | tf_op jit(solution)/shard_map/while/body/eval_jaxpr/all_gather | solution.py:214
  732.6 64.4 %copy-start.31 = (f32[768]{0:T(1024)}, f32[768]{0:T(1024)S(1)}, u32[]{:S(2)}) copy-start(f32[768]{0:T(1024)S(1)} %convert_element_type.282) | copy-start | bytes 9220 | tf_op jit(solution)/shard_map/while
  793.8 41.2 %copy-start.60 = (f32[768]{0:T(1024)S(1)}, f32[768]{0:T(1024)}, u32[]{:S(2)}) copy-start(f32[768]{0:T(1024)} %copy-done.59) | copy-start | bytes 9220 | tf_op jit(solution)/shard_map/while
  797.9 106.2 %reduce-scatter.29.cloned.1.call-start = ((), (), s32[]{:S(2)}) async-start(), calls=%async_computation.23 | async-start | bytes 3932160 | tf_op jit(solution)/shard_map/while/body/eval_jaxpr/reduce_scatter | solution.py:222
  835.0 6.7 copy-start.72
  844.8 59.3 %copy-start.33 = (f32[256]{0:T(256)S(1)}, f32[256]{0:T(256)}, u32[]{:S(2)}) copy-start(f32[256]{0:T(256)} %copy-done.32) | copy-start | bytes 3076 | tf_op jit(solution)/shard_map/while
  844.8 100.2 %all-gather.21.cloned.1.call-start = ((), (), s32[]{:S(2)}) async-start(), calls=%async_computation.24 | async-start | bytes 1966080 | tf_op jit(solution)/shard_map/while/body/eval_jaxpr/all_gather | solution.py:228
  907.1 40.1 %copy-start.29 = (f32[2,3,512]{2,1,0:T(4,128)S(1)}, f32[2,3,512]{2,1,0:T(4,128)}, u32[]{:S(2)}) copy-start(f32[2,3,512]{2,1,0:T(4,128)} %copy-done.28) | copy-start | bytes 36868 | tf_op jit(solution)/shard_map/while
  908.0 100.3 %reduce-scatter.31.cloned.1.call-start = ((), (), s32[]{:S(2)}) async-start(), calls=%async_computation.25 | async-start | bytes 1966080 | tf_op jit(solution)/shard_map/while/body/eval_jaxpr/reduce_scatter | solution.py:248
  974.0 5.7 copy-start.47
  974.1 5.6 copy-start.42
  974.1 5.6 copy-start.71
  974.1 5.6 copy-start.75
  979.8 6.0 copy-start.10
  1013.1 69.9 %reduce-scatter.23.cloned.1.call-start = ((), (), s32[]{:S(2)}) async-start(), calls=%async_computation.15 | async-start | bytes 884736
  1013.2 5.9 copy-start.17
  1015.5 74.3 %reduce-scatter.13.cloned.1.call-start = ((), (), s32[]{:S(2)}) async-start(), calls=%async_computation.10 | async-start | bytes 884736 | tf_op jit(solution)/shard_map/reduce_scatter | solution.py:295
  1017.8 110.7 %reduce-scatter.15.cloned.1.call-start = ((), (), s32[]{:S(2)}) async-start(), calls=%async_computation.11 | async-start | bytes 884736 | tf_op jit(solution)/shard_map/reduce_scatter | solution.py:296
  1019.1 148.1 %reduce-scatter.17.cloned.1.call-start = ((), (), s32[]{:S(2)}) async-start(), calls=%async_computation.12 | async-start | bytes 884736 | tf_op jit(solution)/shard_map/reduce_scatter | solution.py:297
  1020.4 193.2 %reduce-scatter.19.cloned.1.call-start = ((), (), s32[]{:S(2)}) async-start(), calls=%async_computation.13 | async-start | bytes 2654208 | tf_op jit(solution)/shard_map/reduce_scatter | solution.py:299
  1021.1 239.1 %reduce-scatter.21.cloned.1.call-start = ((), (), s32[]{:S(2)}) async-start(), calls=%async_computation.14 | async-start | bytes 2654208 | tf_op jit(solution)/shard_map/reduce_scatter | solution.py:300
  1021.2 18.8 %copy-start.44 = (f32[768]{0:T(1024)S(1)}, f32[768]{0:T(1024)}, u32[]{:S(2)}) copy-start(f32[768]{0:T(1024)} %get-tuple-element.554) | copy-start | bytes 9220
  1021.2 18.8 %copy-start.45 = (f32[768]{0:T(1024)S(1)}, f32[768]{0:T(1024)}, u32[]{:S(2)}) copy-start(f32[768]{0:T(1024)} %get-tuple-element.553) | copy-start | bytes 9220
  1021.2 18.8 %copy-start.48 = (f32[768]{0:T(1024)S(1)}, f32[768]{0:T(1024)}, u32[]{:S(2)}) copy-start(f32[768]{0:T(1024)} %get-tuple-element.552) | copy-start | bytes 9220
  1021.2 18.8 %copy-start.51 = (f32[768]{0:T(1024)S(1)}, f32[768]{0:T(1024)}, u32[]{:S(2)}) copy-start(f32[768]{0:T(1024)} %get-tuple-element.551) | copy-start | bytes 9220
  1021.2 18.7 %copy-start.54 = (f32[768]{0:T(1024)S(1)}, f32[768]{0:T(1024)}, u32[]{:S(2)}) copy-start(f32[768]{0:T(1024)} %get-tuple-element.550) | copy-start | bytes 9220
  1021.3 18.7 %copy-start.57 = (f32[768]{0:T(1024)S(1)}, f32[768]{0:T(1024)}, u32[]{:S(2)}) copy-start(f32[768]{0:T(1024)} %get-tuple-element.549) | copy-start | bytes 9220
  (109 other events, 282.8 us)
Sparse Core Ops, SparseCore 0:
  12.1 39.8 all-gather.10
  104.0 60.5 reduce-scatter.24
  299.7 36.9 all-gather.18
  346.6 59.1 reduce-scatter.28
  514.0 35.9 all-gather.10
  604.4 58.4 reduce-scatter.24
  798.0 36.9 all-gather.18
  844.9 59.1 reduce-scatter.28
  1017.1 33.8 reduce-scatter.22
  1054.6 35.1 reduce-scatter.12
  1093.5 34.9 reduce-scatter.14
  1132.1 34.9 reduce-scatter.16
  1171.1 42.4 reduce-scatter.18
  1217.7 42.4 reduce-scatter.20
Sparse Core Ops, SparseCore 1:
  106.3 24.1 all-gather.12
  167.2 37.0 all-gather.14
  206.0 22.7 all-gather.16
  233.8 60.2 reduce-scatter.26
  409.8 36.9 all-gather.20
  475.8 34.1 reduce-scatter.30
  606.6 22.0 all-gather.12
  665.5 36.9 all-gather.14
  704.3 22.7 all-gather.16
  732.0 60.2 reduce-scatter.26
  908.0 36.9 all-gather.20
  974.1 34.1 reduce-scatter.30
where the time goes:
time: 1290 us; the launch traced here: 1270 us
  waiting for transfers between devices  806 us (62%)
  blocking collectives  179 us (14%)
  matrix products  138 us (11%)
  other arithmetic  61.7 us (5%)
  local copies, waits for them, and re-layouts  56.9 us (4%)
  between operations  17.3 us (1%)
    dot_general x64, matrix products, contract(): return jnp.einsum(form, left, right, preferred_element_type=jnp.float32)  138 us
    reduce_scatter x2, waiting for transfers between devices, micro_step(): lax.psum_scatter(normed_part, 'tensor', scatter_dimension=0, tiled=True)  118 us
    reduce_scatter x2, waiting for transfers between devices, micro_step(): lax.psum_scatter(attn_part, 'tensor', scatter_dimension=0, tiled=True)  118 us
    reduce_scatter x2, waiting for transfers between devices, micro_step(): lax.psum_scatter(ffn_part, 'tensor', scatter_dimension=0, tiled=True)  116 us
    all_gather x2, waiting for transfers between devices, micro_step(): lax.all_gather(second_grad.astype(jnp.bfloat16), 'tensor', axis=0, tiled=...  74.2 us
    all_gather x2, waiting for transfers between devices, micro_step(): lax.all_gather(normed.astype(jnp.bfloat16), 'tensor', axis=0, tiled=True)  72.8 us
    all_gather x2, waiting for transfers between devices, micro_step(): lax.all_gather(first_grad.astype(jnp.bfloat16), 'tensor', axis=0, tiled=T...  66.7 us
    while x2, blocking collectives  53.5 us
  transfers between devices with their start and end apart: 26, of which 21 were waited for; matrix products, arithmetic and copies ran while one was open for 8% of the time, Pallas kernels for 0%

commit v1 on v0

v1 whole, which is shorter than its diff:
```python
import jax
import jax.numpy as jnp
from jax import lax
from jax.sharding import PartitionSpec as P

HD = 64
EPS = 1e-05
NEG = -1000000000.0
ROOT_HALF = 0.7071067811865476
DENSITY = 0.3989422804014327
BOTH = ("fsdp", "tensor")
LOW = jnp.bfloat16
FULL = jnp.float32


def contract(left, right, form):
    return jnp.einsum(form, left, right, preferred_element_type=FULL)


def normalize(summed):
    center = summed - jnp.mean(summed, axis=-1, keepdims=True)
    spread = jnp.mean(center * center, axis=-1, keepdims=True)
    inv_scale = lax.rsqrt(spread + EPS)
    return (center * inv_scale, inv_scale)


def norm_back(grad, gain, unit, inv_scale):
    scaled = grad * gain
    return inv_scale * (
        scaled
        - jnp.mean(scaled, axis=-1, keepdims=True)
        - unit * jnp.mean(scaled * unit, axis=-1, keepdims=True)
    )


def pick(value, where, own, axis):
    return jnp.concatenate(
        [
            lax.dynamic_slice_in_dim(value, where[n ^ own], 1, axis)
            for n in range(value.shape[axis])
        ],
        axis=axis,
    )


class Plan:
    def __init__(self):
        self.parts = lax.axis_size("tensor")
        self.owners = lax.axis_size("fsdp")
        self.place = lax.axis_index("tensor")
        self.owner = lax.axis_index("fsdp")
        self.core = self.owner % 2
        self.outer = self.owner // 2
        self.outers = self.owners // 2
        self.bits = [1 << n for n in range((self.outers - 1).bit_length())]

    def swap(self, value, bit):
        return lax.ppermute(value, "fsdp", [(n, n ^ bit) for n in range(self.owners)])

    def turn(self, value, by):
        n = self.parts
        return lax.ppermute(value, "tensor", [(i, (i + by) % n) for i in range(n)])

    def trade(self, turn, back):
        pairs = []
        half = self.parts // 2
        for owner in range(self.owners):
            for place in range(self.parts):
                micro = (place + turn) % 2
                there = (owner - owner % 2 + place // half) * self.parts + 2 * micro + owner % 2
                here = owner * self.parts + place
                pairs.append((there, here) if back else (here, there))
        return pairs

    def collect(self, value):
        return [
            lax.ppermute(
                lax.dynamic_index_in_dim(value, (self.place + turn) % 2, 0, False),
                BOTH,
                self.trade(turn, False),
            )
            for turn in range(2)
        ]

    def release(self, blocks):
        first, second = [
            lax.ppermute(block, BOTH, self.trade(turn, True)) for turn, block in enumerate(blocks)
        ]
        even = self.place % 2 == 0
        return jnp.stack([jnp.where(even, first, second), jnp.where(even, second, first)])

    def gather(self, shard):
        slices = [shard] + [self.turn(shard, by) for by in range(1, self.parts)]
        half = self.parts // 2
        whole = []
        for lot, bits in ((slices[:half], self.bits), (slices[half:], self.bits[::-1])):
            held = jnp.stack(lot)[None]
            order = [0]
            for bit in bits:
                held = jnp.concatenate([held, self.swap(held, 2 * bit)])
                order = order + [n ^ bit for n in order]
            other = self.swap(held, 1)
            where = jnp.array([order.index(n) for n in range(self.outers)])
            mine, other = pick(held, where, self.outer, 0), pick(other, where, self.outer, 0)
            first = jnp.where(self.core == 0, mine, other)
            second = jnp.where(self.core == 0, other, mine)
            joined = jnp.stack([first, second], axis=1)
            for n in range(half):
                whole.append(joined[:, :, n].reshape(-1, shard.shape[1]))
        return whole

    def reduce(self, terms):
        half = self.parts // 2
        rows = terms[0].shape[0] // self.owners
        total = None
        for first, bits in ((0, self.bits), (half, self.bits[::-1])):
            lot = jnp.stack([t.reshape(self.outers, 2, rows, -1) for t in terms[first : first + half]])
            lot = pick(lot, jnp.arange(self.outers), self.outer, 1)
            away = lax.dynamic_index_in_dim(lot, 1 - self.core, 2, False)
            kept = lax.dynamic_index_in_dim(lot, self.core, 2, False)
            kept = kept + self.swap(away.astype(LOW), 1).astype(FULL)
            names = list(range(self.outers))
            for bit in bits:
                stay = [i for i, n in enumerate(names) if not n & bit]
                leave = [names.index(names[i] ^ bit) for i in stay]
                away = jnp.concatenate([kept[:, i : i + 1] for i in leave], axis=1)
                here = jnp.concatenate([kept[:, i : i + 1] for i in stay], axis=1)
                kept = here + self.swap(away.astype(LOW), 2 * bit).astype(FULL)
                names = [names[i] for i in stay]
            kept = kept[:, 0]
            for n in range(half):
                by = first + n
                term = kept[n] if by == 0 else self.turn(kept[n].astype(LOW), -by).astype(FULL)
                total = term if total is None else total + term
        return total


def head_blocks(width):
    return width // HD


def attend_forward(query, keys, values, live):
    rows, width = query.shape
    heads = head_blocks(width)
    q = query.reshape(rows, heads, HD)
    k = keys.reshape(-1, heads, HD)
    v = values.reshape(-1, heads, HD)
    scores = contract(q, k, "qhd,khd->hqk") * 0.125
    scores = jnp.where(live[None, None, :], scores, NEG)
    top = jnp.max(scores, axis=-1, keepdims=True)
    raised = jnp.exp(scores - top)
    denom = jnp.sum(raised, axis=-1, keepdims=True)
    probs_low = (raised / denom).astype(LOW)
    attended = contract(probs_low, v, "hqk,khd->qhd").astype(LOW)
    return (attended.reshape(rows, width), top + jnp.log(denom))


def attend_backward(query, keys, values, live, log_total, grad):
    rows, width = query.shape
    heads = head_blocks(width)
    q = query.reshape(rows, heads, HD)
    g = grad.reshape(rows, heads, HD)
    k = keys.reshape(-1, heads, HD)
    v = values.reshape(-1, heads, HD)
    scores = contract(q, k, "qhd,khd->hqk") * 0.125
    scores = jnp.where(live[None, None, :], scores, NEG)
    probs = jnp.exp(scores - log_total)
    prob_grad = contract(g, v, "qhd,khd->hqk")
    inner = jnp.sum(probs * prob_grad, axis=-1, keepdims=True)
    score_grad = (probs * (prob_grad - inner)).astype(LOW)
    query_grad = contract(score_grad, k, "hqk,khd->qhd") * 0.125
    key_grad = contract(score_grad, q, "hqk,qhd->khd") * 0.125
    value_grad = contract(probs.astype(LOW), g, "hqk,qhd->khd")
    return (
        query_grad.reshape(rows, width),
        key_grad.reshape(-1, width),
        value_grad.reshape(-1, width),
    )


def column(vector, rows):
    return jnp.pad(vector, (0, rows - vector.shape[0]))[:, None]


def shards(
    tokens, lengths, cotangent, query_proj, key_proj, value_proj, output_proj, expand_proj,
    shrink_proj, query_bias, value_bias, expand_bias, output_bias, attn_gain, attn_shift,
    shrink_bias, ffn_gain, ffn_shift,
):
    plan = Plan()
    parts = plan.parts
    rows, width = query_proj.shape
    hidden = expand_proj.shape[1]
    few = query_bias.shape[0]
    block = tokens.shape[2]

    head_biases = jnp.concatenate([query_bias, value_bias])
    smalls = [output_bias, attn_gain, attn_shift, shrink_bias, ffn_gain, ffn_shift, expand_bias]
    pack_one = jnp.concatenate(
        [query_proj, key_proj, value_proj]
        + [column(v, rows) for v in smalls]
        + [column(head_biases, rows)],
        axis=1,
    )
    pack_two = jnp.concatenate([output_proj.T, expand_proj, shrink_proj.T], axis=1)
    ones = plan.gather(pack_one)
    own_tokens = plan.collect(tokens[:, 0])
    twos = plan.gather(pack_two)
    three = 3 * width
    wide = [w[:, three : three + 6].astype(FULL).T for w in ones[:1]][0]
    output_b, gain_one, shift_one, shrink_b, gain_two, shift_two = [wide[n] for n in range(6)]
    expand_b = [w[:, three + 6].astype(FULL) for w in ones]
    query_b, value_b = [], []
    for w in ones:
        both = w[:, three + 7].astype(FULL).reshape(plan.owners, rows)
        query_b.append(both[:, :few].reshape(width))
        value_b.append(both[:, few : 2 * few].reshape(width))
    qkv_w = [w[:, :three] for w in ones]
    output_w = jnp.concatenate([w[:, :width] for w in twos], axis=1)
    expand_w = [w[:, width : width + hidden] for w in twos]
    shrink_w = [w[:, width + hidden :] for w in twos]

    micro, parity = plan.place // 2, plan.place % 2
    other_lengths = plan.swap(lengths, 1)
    mine = jnp.where(parity == plan.core, lengths, other_lengths)[:, 0]
    length = lax.dynamic_index_in_dim(mine, micro, 0, False)

    def slots_of(core):
        return jnp.concatenate(
            [block * (2 * core + (micro + n) % 2) + jnp.arange(block) for n in range(2)]
        )

    row_slots = slots_of(plan.core)
    live_rows = (row_slots < length).astype(FULL)[:, None]
    live = jnp.concatenate([row_slots, slots_of(1 - plan.core)]) < length

    x = jnp.concatenate(own_tokens)
    query, keys, values = [], [], []
    for n in range(parts):
        y = contract(x, qkv_w[n], "rd,dk->rk")
        query.append((y[:, :width] + query_b[n]).astype(LOW))
        keys.append(y[:, width : 2 * width].astype(LOW))
        values.append((y[:, 2 * width :] + value_b[n]).astype(LOW))
    other = plan.swap(jnp.concatenate(keys + values, axis=1), 1)
    full = parts * width
    attended, logs = [], []
    for n in range(parts):
        keys[n] = jnp.concatenate([keys[n], other[:, n * width : (n + 1) * width]])
        values[n] = jnp.concatenate([values[n], other[:, full + n * width : full + (n + 1) * width]])
        a, log_total = attend_forward(query[n], keys[n], values[n], live)
        attended.append(a)
        logs.append(log_total)
    attended_all = jnp.concatenate(attended, axis=1)
    attn = contract(attended_all, output_w, "rk,dk->rd")
    first_sum = x.astype(FULL) + attn + output_b
    first_unit, first_scale = normalize(first_sum)
    normed = first_unit * gain_one + shift_one
    ffn_in = normed.astype(LOW)
    active, slope = [], []
    ffn = 0.0
    for n in range(parts):
        upper = contract(ffn_in, expand_w[n], "rd,dk->rk") + expand_b[n]
        below = 0.5 * (1.0 + lax.erf(upper * ROOT_HALF))
        active.append((upper * below).astype(LOW))
        slope.append(below + upper * jnp.exp(-0.5 * upper * upper) * DENSITY)
        ffn = ffn + contract(active[n], shrink_w[n], "rk,dk->rd")
    second_sum = normed + ffn + shrink_b
    second_unit, second_scale = normalize(second_sum)
    layer_rows = (second_unit * gain_two + shift_two).astype(LOW)
    layer_out = plan.release([layer_rows[:block], layer_rows[block:]])

    cot = jnp.concatenate(plan.collect(cotangent[:, 0]))
    out_grad = cot.astype(FULL) * live_rows
    grad_gain_two = jnp.sum(out_grad * second_unit, axis=0)
    grad_shift_two = jnp.sum(out_grad, axis=0)
    second_grad = norm_back(out_grad, gain_two, second_unit, second_scale)
    grad_shrink_b = jnp.sum(second_grad, axis=0)
    second_low = second_grad.astype(LOW)
    grad_two, grad_expand_b = [], []
    normed_grad = second_grad
    upper_low = []
    for n in range(parts):
        upper_grad = contract(second_low, shrink_w[n], "rd,dk->rk") * slope[n]
        grad_expand_b.append(jnp.sum(upper_grad, axis=0))
        upper_low.append(upper_grad.astype(LOW))
        normed_grad = normed_grad + contract(upper_low[n], expand_w[n], "rk,dk->rd")
    grad_gain_one = jnp.sum(normed_grad * first_unit, axis=0)
    grad_shift_one = jnp.sum(normed_grad, axis=0)
    first_grad = norm_back(normed_grad, gain_one, first_unit, first_scale)
    grad_output_b = jnp.sum(first_grad, axis=0)
    first_low = first_grad.astype(LOW)
    for n in range(parts):
        grad_two.append(
            jnp.concatenate(
                [
                    contract(first_low, attended[n], "rd,rk->dk"),
                    contract(ffn_in, upper_low[n], "rd,rk->dk"),
                    contract(second_low, active[n], "rd,rk->dk"),
                ],
                axis=1,
            )
        )
    sums_two = plan.reduce(grad_two)
    attended_grad = contract(first_low, output_w, "rd,dk->rk").astype(LOW)
    query_grad, key_grad, value_grad = [], [], []
    for n in range(parts):
        q, k, v = attend_backward(
            query[n], keys[n], values[n], live, logs[n], attended_grad[:, n * width : (n + 1) * width]
        )
        query_grad.append(q)
        key_grad.append(k)
        value_grad.append(v)
    here = 2 * block
    away = jnp.concatenate([g[here:] for g in key_grad + value_grad], axis=1).astype(LOW)
    added = plan.swap(away, 1).astype(FULL)
    grad_one = []
    rows_grad = first_grad
    vectors = [grad_output_b, grad_gain_one, grad_shift_one, grad_shrink_b, grad_gain_two, grad_shift_two]
    for n in range(parts):
        k = key_grad[n][:here] + added[:, n * width : (n + 1) * width]
        v = value_grad[n][:here] + added[:, full + n * width : full + (n + 1) * width]
        low = jnp.concatenate([query_grad[n], k, v], axis=1).astype(LOW)
        rows_grad = rows_grad + contract(low, qkv_w[n], "rk,dk->rd")
        biases = jnp.concatenate(
            [jnp.sum(g, axis=0).reshape(plan.owners, few) for g in (query_grad[n], v)], axis=1
        )
        biases = jnp.pad(biases, ((0, 0), (0, rows - 2 * few))).reshape(-1)
        cols = jnp.stack(vectors + [grad_expand_b[n], biases], axis=1)
        grad_one.append(jnp.concatenate([contract(x, low, "rd,rk->dk"), cols], axis=1))
    input_low = rows_grad.astype(LOW)
    input_grad = plan.release([input_low[:block], input_low[block:]]).astype(FULL)
    sums_one = plan.reduce(grad_one)
    quarter = rows // parts
    own = lax.dynamic_slice_in_dim(sums_one[:, three : three + 6], plan.place * quarter, quarter, 0)
    return (
        layer_out[:, None],
        input_grad[:, None],
        sums_one[:, :width],
        sums_one[:, width : 2 * width],
        sums_one[:, 2 * width : three],
        sums_two[:, :width].T,
        sums_two[:, width : width + hidden],
        sums_two[:, width + hidden :].T,
        sums_one[:few, three + 7],
        sums_one[few : 2 * few, three + 7],
        sums_one[:, three + 6],
        own[:, 0],
        own[:, 1],
        own[:, 2],
        own[:, 3],
        own[:, 4],
        own[:, 5],
    )


def solution(mesh):
    rows = P(None, "fsdp", "tensor", None)
    split = P("fsdp", "tensor")
    turned = P("tensor", "fsdp")
    heads = P(("tensor", "fsdp"))
    model = P("fsdp")
    spread = P(("fsdp", "tensor"))
    return jax.shard_map(
        shards,
        mesh=mesh,
        in_specs=(rows, P(None, "fsdp"), rows, split, split, split, turned, split, turned)
        + (heads,) * 3
        + (model,) * 6,
        out_specs=(rows, rows, split, split, split, turned, split, turned)
        + (heads,) * 3
        + (spread,) * 6,
        check_vma=False,
    )
```

time: 1290 us -> 570 us (0.44); the launches traced: 1270 us -> 562 us
  waiting for transfers between devices: 806 us -> 94.1 us
  blocking collectives: 179 us -> 0 us
  starting transfers between devices: 1.05 us -> 86.2 us
  local copies, waits for them, and re-layouts: 56.9 us -> 137 us
  other arithmetic: 61.7 us -> 106 us
    reduce_scatter x13 -> x0, waiting for transfers between devices: 561 us -> none  [the longest x2 118 us: micro_step(): lax.psum_scatter(normed_part, 'tensor', scatter_dimension=0, tiled=True)]
    all_gather x12 -> x0, waiting for transfers between devices: 242 us -> none  [the longest x2 74.2 us: micro_step(): lax.all_gather(second_grad.astype(jnp.bfloat16), 'tensor', axis=0, tiled=...]
    ppermute x0 -> x47, waiting for transfers between devices: none -> 94.1 us  [the longest x27 62 us: swap(): lax.ppermute(value, 'fsdp', [(n, n ^ bit) for n in range(self.owners)])]
    ppermute x0 -> x47, starting transfers between devices: none -> 86.2 us  [the longest x27 33.4 us: swap(): lax.ppermute(value, 'fsdp', [(n, n ^ bit) for n in range(self.owners)])]
    all_gather x8 -> x0, blocking collectives: 72.6 us -> none  [the longest x2 18.6 us: micro_step(): lax.all_gather(value_proj, 'fsdp', axis=0, tiled=True)]
    concatenate x0 -> x52, local copies, waits for them, and re-layouts: none -> 70.3 us  [the longest x34 39.3 us: shards(): jnp.concatenate([contract(x, low, 'rd,rk->dk'), cols], axis=1)]
    while x2 -> x0, blocking collectives: 53.5 us -> none
    unnamed x2 -> x0, blocking collectives: 52.5 us -> none
  transfers between devices with their start and end apart: 26 -> 47, of which waited for: 21 -> 10; matrix products, arithmetic and copies ran while one was open for 8% -> 35% of each run, Pallas kernels for 0% -> 0%
where the time goes in v1:
time: 570 us; the launch traced here: 562 us
  local copies, waits for them, and re-layouts  137 us (24%)
  matrix products  127 us (22%)
  other arithmetic  106 us (19%)
  waiting for transfers between devices  94.1 us (17%)
  starting transfers between devices  86.2 us (15%)
  between operations  11.4 us (2%)
    dot_general x66, matrix products, contract(): return jnp.einsum(form, left, right, preferred_element_type=FULL)  127 us
    ppermute x27, waiting for transfers between devices, swap(): lax.ppermute(value, 'fsdp', [(n, n ^ bit) for n in range(self.owners)])  62 us
    concatenate x34, local copies, waits for them, and re-layouts, shards(): jnp.concatenate([contract(x, low, 'rd,rk->dk'), cols], axis=1)  39.3 us
    ppermute x27, starting transfers between devices, swap(): lax.ppermute(value, 'fsdp', [(n, n ^ bit) for n in range(self.owners)])  33.4 us
    unnamed x288, local copies, waits for them, and re-layouts  26.9 us
    concatenate x4, local copies, waits for them, and re-layouts, shards(): jnp.concatenate([contract(first_low, attended[n], 'rd,rk->dk'), contract(...  24.8 us
    ppermute x12, waiting for transfers between devices, turn(): return lax.ppermute(value, 'tensor', [(i, (i + by) % n) for i in range(n)])  22 us
    ppermute x12, starting transfers between devices, turn(): return lax.ppermute(value, 'tensor', [(i, (i + by) % n) for i in range(n)])  21.8 us
  transfers between devices with their start and end apart: 47, of which 10 were waited for; matrix products, arithmetic and copies ran while one was open for 35% of the time, Pallas kernels for 0%

profile of v1, /device:TPU:0, one launch (start us, length us, event | category | flops | bytes accessed | tf_op | source)
XLA Modules:
  0.0 561.9 jit_solution(6270660107556102299)
XLA Ops:
  8.1 4.1 collective-permute-start.6
  30.2 2.2 collective-permute-start.17
  37.0 2.8 collective-permute-start.1
  41.4 6.5 %collective-permute-done.3 = bf16[1,2,96,584]{3,2,1,0:T(8,128)(2,1)S(1)} collective-permute-done((bf16[1,2,96,584]{3,2,1,0:T(8,128)(2,1)S(1)}, bf16[1,2,96,584]{3,2,1,0:T(8,128)(2,1)S(1)}, u32[]{:S(2)}, u32[]{:S(2)}) %collective-permute-start.3) | collective-permute-done | bytes 224288 | tf_op jit(solution)/shard_map/ppermute | solution.py:58
  48.0 4.5 collective-permute-start.24
  54.7 6.8 %collective-permute-done.8 = bf16[1,2,96,584]{3,2,1,0:T(8,128)(2,1)S(1)} collective-permute-done((bf16[1,2,96,584]{3,2,1,0:T(8,128)(2,1)S(1)}, bf16[1,2,96,584]{3,2,1,0:T(8,128)(2,1)S(1)}, u32[]{:S(2)}, u32[]{:S(2)}) %collective-permute-start.8) | collective-permute-done | bytes 224288 | tf_op jit(solution)/shard_map/ppermute | solution.py:58
  65.3 3.4 collective-permute-done.4
  68.9 6.6 %collective-permute-start.5 = (bf16[4,2,96,584]{3,2,1,0:T(8,128)(2,1)S(1)}, bf16[4,2,96,584]{3,2,1,0:T(8,128)(2,1)S(1)}, u32[]{:S(2)}, u32[]{:S(2)}) collective-permute-start(bf16[4,2,96,584]{3,2,1,0:T(8,128)(2,1)S(1)} %pad_maximum_fusion.22), channel_id=1, source_target_pairs={{0,4},{4,0},{8,12},{12,8},{16,20},{20,16},{24,28},{28,24},{1,5},{5... | collective-permute-start | bytes 2691080 | tf_op jit(solution)/shard_map/ppermute | solution.py:58
  75.6 5.7 %collective-permute-done.9 = bf16[2,2,96,584]{3,2,1,0:T(8,128)(2,1)S(1)} collective-permute-done((bf16[2,2,96,584]{3,2,1,0:T(8,128)(2,1)S(1)}, bf16[2,2,96,584]{3,2,1,0:T(8,128)(2,1)S(1)}, u32[]{:S(2)}, u32[]{:S(2)}) %collective-permute-start.9) | collective-permute-done | bytes 448544 | tf_op jit(solution)/shard_map/ppermute | solution.py:58
  81.3 12.1 %collective-permute-start.25 = (bf16[256,768]{1,0:T(8,128)(2,1)}, bf16[256,768]{1,0:T(8,128)(2,1)}, u32[]{:S(2)}, u32[]{:S(2)}) collective-permute-start(bf16[256,768]{1,0:T(8,128)(2,1)} %get-tuple-element.224), channel_id=1, source_target_pairs={{0,2},{1,0},{2,6},{3,4},{4,3},{5,1},{6,7},{7,5},{8,10},{9,8},{10,1... | collective-permute-start | bytes 1179656 | tf_op jit(solution)/shard_map/ppermute | solution.py:77
  93.7 6.7 %collective-permute-start.10 = (bf16[4,2,96,584]{3,2,1,0:T(8,128)(2,1)S(1)}, bf16[4,2,96,584]{3,2,1,0:T(8,128)(2,1)S(1)}, u32[]{:S(2)}, u32[]{:S(2)}) collective-permute-start(bf16[4,2,96,584]{3,2,1,0:T(8,128)(2,1)S(1)} %pad_maximum_fusion.25), channel_id=1, source_target_pairs={{0,4},{4,0},{8,12},{12,8},{16,20},{20,16},{24,28},{28,24},{1,5},{5... | collective-permute-start | bytes 2691080 | tf_op jit(solution)/shard_map/ppermute | solution.py:58
  180.0 2.6 multiply_reduce_fusion.4
  182.6 3.3 fusion.206
  186.0 2.1 fusion.239
  188.1 2.2 fusion.203
  193.2 2.2 fusion.163
  195.4 2.3 fusion.242
  197.7 2.2 fusion.160
  205.5 2.2 multiply_reduce_fusion.5
  211.5 2.2 fusion.241
  213.7 2.2 fusion.166
  218.2 2.3 fusion.169
  220.5 2.2 fusion.240
  224.8 3.9 multiply_reduce_fusion
  230.9 2.4 fusion.220
  234.1 4.1 fusion.67
  238.2 6.3 %multiply_reduce_fusion.1 = (f32[3,512]{1,0:T(4,128)}, f32[3,512,1024]{2,1,0:T(8,128)}) fusion(f32[3,512,1024]{2,1,0:T(8,128)} %copy-done.2, f32[3,512]{1,0:T(4,128)S(1)} %log_add_fusion.1, bf16[512,3,64]{0,2,1:T(8,128)(2,1)S(1)} %bitcast.441, bf16[1024,3,64]{0,2,1:T(8,128)(2,1)S(1)} %bitcast.449), kind=kOutput, calls=%fused_computation.22 | convolution fusion | flops 206043648 | bytes 13185024 | tf_op jit(solution)/shard_map/qhd,khd->hqk/dot_general | solution.py:17
  244.7 4.0 fusion.64
  248.7 6.4 %multiply_reduce_fusion.2 = (f32[3,512]{1,0:T(4,128)}, f32[3,512,1024]{2,1,0:T(8,128)}) fusion(f32[3,512,1024]{2,1,0:T(8,128)} %copy-done, f32[3,512]{1,0:T(4,128)S(1)} %log_add_fusion.2, bf16[512,3,64]{0,2,1:T(8,128)(2,1)S(1)} %bitcast.443, bf16[1024,3,64]{0,2,1:T(8,128)(2,1)S(1)} %bitcast.447), kind=kOutput, calls=%fused_computation.25 | convolution fusion | flops 206043648 | bytes 13185024 | tf_op jit(solution)/shard_map/qhd,khd->hqk/dot_general | solution.py:17
  256.2 4.1 fusion.61
  260.3 4.1 multiply_reduce_fusion.3
  269.4 3.7 multiply_convert_fusion.1
  275.2 2.4 fusion.221
  280.6 2.3 fusion.222
  299.8 3.5 fusion.223
  303.2 4.3 pad_maximum_fusion.5
  307.6 6.3 %copy.185 = f32[768,1728]{1,0:T(8,128)} copy(f32[768,1728]{0,1:T(8,128)} %pad_maximum_fusion.5) | data formatting | bytes 10616832 | tf_op jit(solution)/shard_map/concatenate | solution.py:294
  313.8 4.3 pad_maximum_fusion.4
  318.1 6.1 %copy.184 = f32[768,1728]{1,0:T(8,128)} copy(f32[768,1728]{0,1:T(8,128)} %pad_maximum_fusion.4) | data formatting | bytes 10616832 | tf_op jit(solution)/shard_map/concatenate | solution.py:294
  324.2 4.6 fusion.29
  330.2 4.0 copy-done.4
  337.7 2.7 pad_maximum_fusion.3
  340.4 6.3 %copy.183 = f32[768,1728]{1,0:T(8,128)} copy(f32[768,1728]{0,1:T(8,128)} %pad_maximum_fusion.3) | data formatting | bytes 10616832 | tf_op jit(solution)/shard_map/concatenate | solution.py:294
  346.7 4.3 pad_maximum_fusion.2
  351.1 6.2 %copy.182 = f32[768,1728]{1,0:T(8,128)} copy(f32[768,1728]{0,1:T(8,128)} %pad_maximum_fusion.2) | data formatting | bytes 10616832 | tf_op jit(solution)/shard_map/concatenate | solution.py:294
  369.4 4.5 collective-permute-start.22
  373.9 4.6 fusion.33
  395.0 2.2 fusion.177
  405.9 3.4 concatenate.531
  409.3 4.6 concatenate.526
  420.0 3.2 add_convert_fusion
  426.3 4.5 collective-permute-start.27
  430.8 3.3 concatenate.518
  434.1 4.5 concatenate.513
  444.6 10.1 %collective-permute-done.28 = bf16[256,768]{1,0:T(8,128)(2,1)S(1)} collective-permute-done((bf16[256,768]{1,0:T(8,128)(2,1)S(1)}, bf16[256,768]{1,0:T(8,128)(2,1)S(1)}, u32[]{:S(2)}, u32[]{:S(2)}) %collective-permute-start.28) | collective-permute-done | bytes 393248 | tf_op jit(solution)/shard_map/ppermute | solution.py:87
  461.8 2.6 bitcast_add_fusion
  467.2 4.2 fusion.204
  478.2 30.2 %collective-permute-done.35 = bf16[2,1,96,584]{3,2,1,0:T(8,128)(2,1)S(1)} collective-permute-done((bf16[2,1,96,584]{3,2,1,0:T(8,128)(2,1)S(1)}, bf16[2,1,96,584]{3,2,1,0:T(8,128)(2,1)S(1)}, u32[]{:S(2)}, u32[]{:S(2)}) %collective-permute-start.35) | collective-permute-done | bytes 224288 | tf_op jit(solution)/shard_map/ppermute | solution.py:58
  510.4 2.2 collective-permute-start.32
  512.9 4.3 collective-permute-done.36
  523.7 9.3 %collective-permute-done.44 = bf16[2,1,96,1728]{3,2,1,0:T(8,128)(2,1)S(1)} collective-permute-done((bf16[2,1,96,1728]{3,2,1,0:T(8,128)(2,1)S(1)}, bf16[2,1,96,1728]{3,2,1,0:T(8,128)(2,1)S(1)}, u32[]{:S(2)}, u32[]{:S(2)}) %collective-permute-start.44) | collective-permute-done | bytes 663584 | tf_op jit(solution)/shard_map/ppermute | solution.py:58
  533.2 3.7 collective-permute-start.45
  537.6 3.3 collective-permute-start.41
  542.4 17.1 %collective-permute-done.45 = bf16[96,1728]{1,0:T(8,128)(2,1)S(1)} collective-permute-done((bf16[96,1728]{1,0:T(8,128)(2,1)S(1)}, bf16[96,1728]{1,0:T(8,128)(2,1)S(1)}, u32[]{:S(2)}, u32[]{:S(2)}) %collective-permute-start.45) | collective-permute-done | bytes 331808 | tf_op jit(solution)/shard_map/ppermute | solution.py:62
  (648 shorter events, 242.7 us)
Async XLA Ops:
  0.7 25.9 %copy-start.87 = (bf16[2,1,256,768]{3,2,1,0:T(8,128)(2,1)S(1)}, bf16[2,1,256,768]{3,2,1,0:T(8,128)(2,1)}, u32[]{:S(2)}) copy-start(bf16[2,1,256,768]{3,2,1,0:T(8,128)(2,1)} %param.24) | copy-start | bytes 2359300
  7.0 25.4 %copy-start.118 = (s32[2,1]{0,1:T(1,128)S(1)}, s32[2,1]{0,1:T(1,128)}, u32[]{:S(2)}) copy-start(s32[2,1]{0,1:T(1,128)} %param.23) | copy-start | bytes 28
  8.1 26.9 %collective-permute-start.6 = (bf16[96,584]{1,0:T(8,128)(2,1)S(1)}, bf16[96,584]{1,0:T(8,128)(2,1)S(1)}, u32[]{:S(2)}, u32[]{:S(2)}) collective-permute-start(bf16[96,584]{1,0:T(8,128)(2,1)S(1)} %concatenate.434), channel_id=1, source_target_pairs={{0,2},{1,3},{2,0},{3,1},{4,6},{5,7},{6,4},{7,5},{8,10},{9,11},{10,... | collective-permute-start | bytes 336392 | tf_op jit(solution)/shard_map/ppermute | solution.py:62
  12.2 23.1 %collective-permute-start.7 = (bf16[96,584]{1,0:T(8,128)(2,1)S(1)}, bf16[96,584]{1,0:T(8,128)(2,1)S(1)}, u32[]{:S(2)}, u32[]{:S(2)}) collective-permute-start(bf16[96,584]{1,0:T(8,128)(2,1)S(1)} %concatenate.434), channel_id=1, source_target_pairs={{0,3},{1,0},{2,1},{3,2},{4,7},{5,4},{6,5},{7,6},{8,11},{9,8},{10,9... | collective-permute-start | bytes 336392 | tf_op jit(solution)/shard_map/ppermute | solution.py:62
  13.5 23.4 %collective-permute-start.2 = (bf16[96,584]{1,0:T(8,128)(2,1)S(1)}, bf16[96,584]{1,0:T(8,128)(2,1)S(1)}, u32[]{:S(2)}, u32[]{:S(2)}) collective-permute-start(bf16[96,584]{1,0:T(8,128)(2,1)S(1)} %concatenate.434), channel_id=1, source_target_pairs={{0,1},{1,2},{2,3},{3,0},{4,5},{5,6},{6,7},{7,4},{8,9},{9,10},{10,1... | collective-permute-start | bytes 336392 | tf_op jit(solution)/shard_map/ppermute | solution.py:62
  14.2 16.0 %collective-permute-start.12 = (s32[2,1]{0,1:T(1,128)}, s32[2,1]{0,1:T(1,128)S(1)}, u32[]{:S(2)}, u32[]{:S(2)}) collective-permute-start(s32[2,1]{0,1:T(1,128)} %param.23), channel_id=1, source_target_pairs={{0,4},{4,0},{8,12},{12,8},{16,20},{20,16},{24,28},{28,24},{1,5},{5... | collective-permute-start | bytes 32 | tf_op jit(solution)/shard_map/ppermute | solution.py:58
  16.3 23.5 %collective-permute-start.13 = (bf16[96,1728]{1,0:T(8,128)(2,1)S(1)}, bf16[96,1728]{1,0:T(8,128)(2,1)S(1)}, u32[]{:S(2)}, u32[]{:S(2)}) collective-permute-start(bf16[96,1728]{1,0:T(8,128)(2,1)S(1)} %concatenate.470), channel_id=1, source_target_pairs={{0,1},{1,2},{2,3},{3,0},{4,5},{5,6},{6,7},{7,4},{8,9},{9,10},{10,1... | collective-permute-start | bytes 995336 | tf_op jit(solution)/shard_map/ppermute | solution.py:62
  30.2 22.3 %collective-permute-start.17 = (bf16[96,1728]{1,0:T(8,128)(2,1)S(1)}, bf16[96,1728]{1,0:T(8,128)(2,1)S(1)}, u32[]{:S(2)}, u32[]{:S(2)}) collective-permute-start(bf16[96,1728]{1,0:T(8,128)(2,1)S(1)} %concatenate.470), channel_id=1, source_target_pairs={{0,2},{1,3},{2,0},{3,1},{4,6},{5,7},{6,4},{7,5},{8,10},{9,11},{10,... | collective-permute-start | bytes 995336 | tf_op jit(solution)/shard_map/ppermute | solution.py:62
  34.9 115.1 %copy-start.97 = (pred[1024]{0:T(1024)(128)(4,1)}, pred[1024]{0:T(1024)(128)(4,1)S(1)}, u32[]{:S(2)}) copy-start(pred[1024]{0:T(1024)(128)(4,1)S(1)} %add_compare_fusion) | copy-start | bytes 3076
  34.9 19.2 %collective-permute-start.18 = (bf16[96,1728]{1,0:T(8,128)(2,1)S(1)}, bf16[96,1728]{1,0:T(8,128)(2,1)S(1)}, u32[]{:S(2)}, u32[]{:S(2)}) collective-permute-start(bf16[96,1728]{1,0:T(8,128)(2,1)S(1)} %concatenate.470), channel_id=1, source_target_pairs={{0,3},{1,0},{2,1},{3,2},{4,7},{5,4},{6,5},{7,6},{8,11},{9,8},{10,9... | collective-permute-start | bytes 995336 | tf_op jit(solution)/shard_map/ppermute | solution.py:62
  35.3 27.8 %collective-permute-start = (bf16[256,768]{1,0:T(8,128)(2,1)}, bf16[256,768]{1,0:T(8,128)(2,1)S(1)}, u32[]{:S(2)}, u32[]{:S(2)}) collective-permute-start(bf16[256,768]{1,0:T(8,128)(2,1)} %get-tuple-element.230), channel_id=1, source_target_pairs={{0,0},{1,2},{2,4},{3,6},{4,1},{5,3},{6,5},{7,7},{8,8},{9,10},{10,1... | collective-permute-start | bytes 1179656 | tf_op jit(solution)/shard_map/ppermute | solution.py:77
  37.0 26.7 %collective-permute-start.1 = (bf16[256,768]{1,0:T(8,128)(2,1)S(1)}, bf16[256,768]{1,0:T(8,128)(2,1)S(1)}, u32[]{:S(2)}, u32[]{:S(2)}) collective-permute-start(bf16[256,768]{1,0:T(8,128)(2,1)S(1)} %get-tuple-element.229), channel_id=1, source_target_pairs={{0,2},{1,0},{2,6},{3,4},{4,3},{5,1},{6,7},{7,5},{8,10},{9,8},{10,1... | collective-permute-start | bytes 1179656 | tf_op jit(solution)/shard_map/ppermute | solution.py:77
  39.8 8.1 %collective-permute-start.3 = (bf16[1,2,96,584]{3,2,1,0:T(8,128)(2,1)S(1)}, bf16[1,2,96,584]{3,2,1,0:T(8,128)(2,1)S(1)}, u32[]{:S(2)}, u32[]{:S(2)}) collective-permute-start(bf16[1,2,96,584]{3,2,1,0:T(8,128)(2,1)S(1)} %maximum_bitcast_fusion.3), channel_id=1, source_target_pairs={{0,8},{4,12},{8,0},{12,4},{16,24},{20,28},{24,16},{28,20},{1,9},{5... | collective-permute-start | bytes 672776 | tf_op jit(solution)/shard_map/ppermute | solution.py:58
  48.0 132.1 %collective-permute-start.24 = (bf16[256,768]{1,0:T(8,128)(2,1)}, bf16[256,768]{1,0:T(8,128)(2,1)}, u32[]{:S(2)}, u32[]{:S(2)}) collective-permute-start(bf16[256,768]{1,0:T(8,128)(2,1)} %get-tuple-element.223), channel_id=1, source_target_pairs={{0,0},{1,2},{2,4},{3,6},{4,1},{5,3},{6,5},{7,7},{8,8},{9,10},{10,1... | collective-permute-start | bytes 1179656 | tf_op jit(solution)/shard_map/ppermute | solution.py:77
  52.5 9.0 %collective-permute-start.8 = (bf16[1,2,96,584]{3,2,1,0:T(8,128)(2,1)S(1)}, bf16[1,2,96,584]{3,2,1,0:T(8,128)(2,1)S(1)}, u32[]{:S(2)}, u32[]{:S(2)}) collective-permute-start(bf16[1,2,96,584]{3,2,1,0:T(8,128)(2,1)S(1)} %maximum_bitcast_fusion.4), channel_id=1, source_target_pairs={{0,16},{4,20},{8,24},{12,28},{16,0},{20,4},{24,8},{28,12},{1,17},{... | collective-permute-start | bytes 672776 | tf_op jit(solution)/shard_map/ppermute | solution.py:58
  54.1 14.6 %collective-permute-start.4 = (bf16[2,2,96,584]{3,2,1,0:T(8,128)(2,1)S(1)}, bf16[2,2,96,584]{3,2,1,0:T(8,128)(2,1)S(1)}, u32[]{:S(2)}, u32[]{:S(2)}) collective-permute-start(bf16[2,2,96,584]{3,2,1,0:T(8,128)(2,1)S(1)} %pad_maximum_fusion.33), channel_id=1, source_target_pairs={{0,16},{4,20},{8,24},{12,28},{16,0},{20,4},{24,8},{28,12},{1,17},{... | collective-permute-start | bytes 1345544 | tf_op jit(solution)/shard_map/ppermute | solution.py:58
  61.5 32.2 %collective-permute-start.14 = (bf16[1,2,96,1728]{3,2,1,0:T(8,128)(2,1)S(1)}, bf16[1,2,96,1728]{3,2,1,0:T(8,128)(2,1)S(1)}, u32[]{:S(2)}, u32[]{:S(2)}) collective-permute-start(bf16[1,2,96,1728]{3,2,1,0:T(8,128)(2,1)S(1)} %maximum_bitcast_fusion.1), channel_id=1, source_target_pairs={{0,8},{4,12},{8,0},{12,4},{16,24},{20,28},{24,16},{28,20},{1,9},{5... | collective-permute-start | bytes 1990664 | tf_op jit(solution)/shard_map/ppermute | solution.py:58
  63.1 18.2 %collective-permute-start.9 = (bf16[2,2,96,584]{3,2,1,0:T(8,128)(2,1)S(1)}, bf16[2,2,96,584]{3,2,1,0:T(8,128)(2,1)S(1)}, u32[]{:S(2)}, u32[]{:S(2)}) collective-permute-start(bf16[2,2,96,584]{3,2,1,0:T(8,128)(2,1)S(1)} %pad_maximum_fusion.34), channel_id=1, source_target_pairs={{0,8},{4,12},{8,0},{12,4},{16,24},{20,28},{24,16},{28,20},{1,9},{5... | collective-permute-start | bytes 1345544 | tf_op jit(solution)/shard_map/ppermute | solution.py:58
  63.7 38.0 %collective-permute-start.19 = (bf16[1,2,96,1728]{3,2,1,0:T(8,128)(2,1)S(1)}, bf16[1,2,96,1728]{3,2,1,0:T(8,128)(2,1)S(1)}, u32[]{:S(2)}, u32[]{:S(2)}) collective-permute-start(bf16[1,2,96,1728]{3,2,1,0:T(8,128)(2,1)S(1)} %maximum_bitcast_fusion.2), channel_id=1, source_target_pairs={{0,16},{4,20},{8,24},{12,28},{16,0},{20,4},{24,8},{28,12},{1,17},{... | collective-permute-start | bytes 1990664 | tf_op jit(solution)/shard_map/ppermute | solution.py:58
  65.3 103.9 %copy-start.11 = (bf16[512,768]{1,0:T(8,128)(2,1)}, bf16[512,768]{1,0:T(8,128)(2,1)S(1)}, u32[]{:S(2)}) copy-start(bf16[512,768]{1,0:T(8,128)(2,1)S(1)} %constant_dynamic-update-slice_fusion) | copy-start | bytes 2359300
  68.9 35.6 %collective-permute-start.5 = (bf16[4,2,96,584]{3,2,1,0:T(8,128)(2,1)S(1)}, bf16[4,2,96,584]{3,2,1,0:T(8,128)(2,1)S(1)}, u32[]{:S(2)}, u32[]{:S(2)}) collective-permute-start(bf16[4,2,96,584]{3,2,1,0:T(8,128)(2,1)S(1)} %pad_maximum_fusion.22), channel_id=1, source_target_pairs={{0,4},{4,0},{8,12},{12,8},{16,20},{20,16},{24,28},{28,24},{1,5},{5... | collective-permute-start | bytes 2691080 | tf_op jit(solution)/shard_map/ppermute | solution.py:58
  81.3 98.7 %collective-permute-start.25 = (bf16[256,768]{1,0:T(8,128)(2,1)}, bf16[256,768]{1,0:T(8,128)(2,1)}, u32[]{:S(2)}, u32[]{:S(2)}) collective-permute-start(bf16[256,768]{1,0:T(8,128)(2,1)} %get-tuple-element.224), channel_id=1, source_target_pairs={{0,2},{1,0},{2,6},{3,4},{4,3},{5,1},{6,7},{7,5},{8,10},{9,8},{10,1... | collective-permute-start | bytes 1179656 | tf_op jit(solution)/shard_map/ppermute | solution.py:77
  93.7 10.8 %copy-start.42 = (bf16[1,2,96,1728]{3,2,1,0:T(8,128)(2,1)}, bf16[1,2,96,1728]{3,2,1,0:T(8,128)(2,1)S(1)}, u32[]{:S(2)}) copy-start(bf16[1,2,96,1728]{3,2,1,0:T(8,128)(2,1)S(1)} %collective-permute-done.14) | copy-start | bytes 1990660
  93.7 17.5 %collective-permute-start.10 = (bf16[4,2,96,584]{3,2,1,0:T(8,128)(2,1)S(1)}, bf16[4,2,96,584]{3,2,1,0:T(8,128)(2,1)S(1)}, u32[]{:S(2)}, u32[]{:S(2)}) collective-permute-start(bf16[4,2,96,584]{3,2,1,0:T(8,128)(2,1)S(1)} %pad_maximum_fusion.25), channel_id=1, source_target_pairs={{0,4},{4,0},{8,12},{12,8},{16,20},{20,16},{24,28},{28,24},{1,5},{5... | collective-permute-start | bytes 2691080 | tf_op jit(solution)/shard_map/ppermute | solution.py:58
  101.8 36.1 %collective-permute-start.15 = (bf16[2,2,96,1728]{3,2,1,0:T(8,128)(2,1)}, bf16[2,2,96,1728]{3,2,1,0:T(8,128)(2,1)}, u32[]{:S(2)}, u32[]{:S(2)}) collective-permute-start(bf16[2,2,96,1728]{3,2,1,0:T(8,128)(2,1)} %pad_maximum_fusion.16), channel_id=1, source_target_pairs={{0,16},{4,20},{8,24},{12,28},{16,0},{20,4},{24,8},{28,12},{1,17},{... | collective-permute-start | bytes 3981320 | tf_op jit(solution)/shard_map/ppermute | solution.py:58
  104.5 35.7 %collective-permute-start.20 = (bf16[2,2,96,1728]{3,2,1,0:T(8,128)(2,1)}, bf16[2,2,96,1728]{3,2,1,0:T(8,128)(2,1)}, u32[]{:S(2)}, u32[]{:S(2)}) collective-permute-start(bf16[2,2,96,1728]{3,2,1,0:T(8,128)(2,1)} %pad_maximum_fusion.17), channel_id=1, source_target_pairs={{0,8},{4,12},{8,0},{12,4},{16,24},{20,28},{24,16},{28,20},{1,9},{5... | collective-permute-start | bytes 3981320 | tf_op jit(solution)/shard_map/ppermute | solution.py:58
  106.9 26.2 %copy-start.19 = (bf16[4,2,1,96,584]{4,3,2,1,0:T(8,128)(2,1)}, bf16[4,2,1,96,584]{4,3,2,1,0:T(8,128)(2,1)S(1)}, u32[]{:S(2)}) copy-start(bf16[4,2,1,96,584]{4,3,2,1,0:T(8,128)(2,1)S(1)} %get-tuple-element.185) | copy-start | bytes 2691076
  131.6 10.7 %collective-permute-start.11 = (bf16[512,1536]{0,1:T(8,128)(2,1)}, bf16[512,1536]{0,1:T(8,128)(2,1)}, u32[]{:S(2)}, u32[]{:S(2)}) collective-permute-start(bf16[512,1536]{0,1:T(8,128)(2,1)} %get-tuple-element.110), channel_id=1, source_target_pairs={{0,4},{4,0},{8,12},{12,8},{16,20},{20,16},{24,28},{28,24},{1,5},{5... | collective-permute-start | bytes 4718600 | tf_op jit(solution)/shard_map/ppermute | solution.py:58
  137.8 20.5 %copy-start.56 = (bf16[512,192]{0,1:T(8,128)(2,1)}, bf16[512,192]{0,1:T(8,128)(2,1)S(1)}, u32[]{:S(2)}) copy-start(bf16[512,192]{0,1:T(8,128)(2,1)S(1)} %fusion.152) | copy-start | bytes 589828
  139.6 26.0 %collective-permute-start.16 = (bf16[4,2,96,1728]{3,2,1,0:T(8,128)(2,1)S(1)}, bf16[4,2,96,1728]{3,2,1,0:T(8,128)(2,1)S(1)}, u32[]{:S(2)}, u32[]{:S(2)}) collective-permute-start(bf16[4,2,96,1728]{3,2,1,0:T(8,128)(2,1)S(1)} %pad_maximum_fusion.10), channel_id=1, source_target_pairs={{0,4},{4,0},{8,12},{12,8},{16,20},{20,16},{24,28},{28,24},{1,5},{5... | collective-permute-start | bytes 7962632 | tf_op jit(solution)/shard_map/ppermute | solution.py:58
  141.8 25.5 %collective-permute-start.21 = (bf16[4,2,96,1728]{3,2,1,0:T(8,128)(2,1)S(1)}, bf16[4,2,96,1728]{3,2,1,0:T(8,128)(2,1)S(1)}, u32[]{:S(2)}, u32[]{:S(2)}) collective-permute-start(bf16[4,2,96,1728]{3,2,1,0:T(8,128)(2,1)S(1)} %pad_maximum_fusion.13), channel_id=1, source_target_pairs={{0,4},{4,0},{8,12},{12,8},{16,20},{20,16},{24,28},{28,24},{1,5},{5... | collective-permute-start | bytes 7962632 | tf_op jit(solution)/shard_map/ppermute | solution.py:58
  233.9 35.4 %copy-start.46 = (f32[1024,3,64]{0,2,1:T(8,128)}, f32[1024,3,64]{0,2,1:T(8,128)S(1)}, u32[]{:S(2)}) copy-start(f32[1024,3,64]{0,2,1:T(8,128)S(1)} %fusion.73) | copy-start | bytes 2359300
  238.2 28.2 %copy-start.31 = (f32[1024,3,64]{0,2,1:T(8,128)}, f32[1024,3,64]{0,2,1:T(8,128)S(1)}, u32[]{:S(2)}) copy-start(f32[1024,3,64]{0,2,1:T(8,128)S(1)} %fusion.67) | copy-start | bytes 2359300
  248.6 18.5 %copy-start.32 = (f32[1024,3,64]{0,2,1:T(8,128)}, f32[1024,3,64]{0,2,1:T(8,128)S(1)}, u32[]{:S(2)}) copy-start(f32[1024,3,64]{0,2,1:T(8,128)S(1)} %fusion.64) | copy-start | bytes 2359300
  256.2 13.2 %slice-start.4 = ((s8[6291456]{0:T(1024)(128)(4,1)}), s8[4194304]{0:T(1024)(128)(4,1)S(1)}, s32[]{:S(2)}) async-start(s8[6291456]{0:T(1024)(128)(4,1)} %bitcast.365), calls=%async_computation.4 | async-start | bytes 8388608
  264.5 13.1 %slice-start = ((s8[6291456]{0:T(1024)(128)(4,1)}), s8[4194304]{0:T(1024)(128)(4,1)S(1)}, s32[]{:S(2)}) async-start(s8[6291456]{0:T(1024)(128)(4,1)} %bitcast.361), calls=%async_computation | async-start | bytes 8388608
  286.4 11.4 %copy-start.100 = (f32[768]{0:T(1024)S(1)}, f32[768]{0:T(1024)}, u32[]{:S(2)}) copy-start(f32[768]{0:T(1024)} %get-tuple-element.87) | copy-start | bytes 9220
  336.0 125.7 %collective-permute-start.42 = (bf16[2,4,96,1728]{3,2,1,0:T(8,128)(2,1)}, bf16[2,4,96,1728]{3,2,1,0:T(8,128)(2,1)}, u32[]{:S(2)}, u32[]{:S(2)}) collective-permute-start(bf16[2,4,96,1728]{3,2,1,0:T(8,128)(2,1)} %fusion.27), channel_id=1, source_target_pairs={{0,4},{4,0},{8,12},{12,8},{16,20},{20,16},{24,28},{28,24},{1,5},{5... | collective-permute-start | bytes 7962632 | tf_op jit(solution)/shard_map/ppermute | solution.py:58
  357.3 10.1 %copy-start.112 = (f32[768]{0:T(1024)S(1)}, f32[768]{0:T(1024)}, u32[]{:S(2)}) copy-start(f32[768]{0:T(1024)} %get-tuple-element.291) | copy-start | bytes 9220
  357.4 11.0 %copy-start.41 = (bf16[512,768]{1,0:T(8,128)(2,1)S(1)}, bf16[512,768]{1,0:T(8,128)(2,1)}, u32[]{:S(2)}) copy-start(bf16[512,768]{1,0:T(8,128)(2,1)} %get-tuple-element.188) | copy-start | bytes 2359300
  363.0 18.8 %collective-permute-start.26 = (bf16[512,1536]{0,1:T(8,128)(2,1)}, bf16[512,1536]{0,1:T(8,128)(2,1)S(1)}, u32[]{:S(2)}, u32[]{:S(2)}) collective-permute-start(bf16[512,1536]{0,1:T(8,128)(2,1)} %constant_dynamic-update-slice_fusion.10), channel_id=1, source_target_pairs={{0,4},{4,0},{8,12},{12,8},{16,20},{20,16},{24,28},{28,24},{1,5},{5... | collective-permute-start | bytes 4718600 | tf_op jit(solution)/shard_map/ppermute | solution.py:58
  369.4 71.5 %collective-permute-start.22 = (bf16[256,768]{1,0:T(8,128)(2,1)}, bf16[256,768]{1,0:T(8,128)(2,1)}, u32[]{:S(2)}, u32[]{:S(2)}) collective-permute-start(bf16[256,768]{1,0:T(8,128)(2,1)} %get-tuple-element.227), channel_id=1, source_target_pairs={{0,0},{2,1},{4,2},{6,3},{1,4},{3,5},{5,6},{7,7},{8,8},{10,9},{12,1... | collective-permute-start | bytes 1179656 | tf_op jit(solution)/shard_map/ppermute | solution.py:87
  373.9 67.5 %collective-permute-start.23 = (bf16[256,768]{1,0:T(8,128)(2,1)}, bf16[256,768]{1,0:T(8,128)(2,1)}, u32[]{:S(2)}, u32[]{:S(2)}) collective-permute-start(bf16[256,768]{1,0:T(8,128)(2,1)} %get-tuple-element.228), channel_id=1, source_target_pairs={{2,0},{0,1},{6,2},{4,3},{3,4},{1,5},{7,6},{5,7},{10,8},{8,9},{14,1... | collective-permute-start | bytes 1179656 | tf_op jit(solution)/shard_map/ppermute | solution.py:87
  419.2 37.8 %collective-permute-start.33 = (bf16[2,4,96,584]{3,2,1,0:T(8,128)(2,1)}, bf16[2,4,96,584]{3,2,1,0:T(8,128)(2,1)}, u32[]{:S(2)}, u32[]{:S(2)}) collective-permute-start(bf16[2,4,96,584]{3,2,1,0:T(8,128)(2,1)} %fusion.108), channel_id=1, source_target_pairs={{0,4},{4,0},{8,12},{12,8},{16,20},{20,16},{24,28},{28,24},{1,5},{5... | collective-permute-start | bytes 2691080 | tf_op jit(solution)/shard_map/ppermute | solution.py:58
  426.3 15.2 %collective-permute-start.27 = (bf16[256,768]{1,0:T(8,128)(2,1)}, bf16[256,768]{1,0:T(8,128)(2,1)}, u32[]{:S(2)}, u32[]{:S(2)}) collective-permute-start(bf16[256,768]{1,0:T(8,128)(2,1)} %get-tuple-element.217), channel_id=1, source_target_pairs={{0,0},{2,1},{4,2},{6,3},{1,4},{3,5},{5,6},{7,7},{8,8},{10,9},{12,1... | collective-permute-start | bytes 1179656 | tf_op jit(solution)/shard_map/ppermute | solution.py:87
  440.9 26.3 %collective-permute-start.38 = (bf16[2,4,96,1728]{3,2,1,0:T(8,128)(2,1)}, bf16[2,4,96,1728]{3,2,1,0:T(8,128)(2,1)}, u32[]{:S(2)}, u32[]{:S(2)}) collective-permute-start(bf16[2,4,96,1728]{3,2,1,0:T(8,128)(2,1)} %fusion.24), channel_id=1, source_target_pairs={{0,4},{4,0},{8,12},{12,8},{16,20},{20,16},{24,28},{28,24},{1,5},{5... | collective-permute-start | bytes 7962632 | tf_op jit(solution)/shard_map/ppermute | solution.py:58
  441.4 18.5 %collective-permute-start.29 = (bf16[2,4,96,584]{3,2,1,0:T(8,128)(2,1)S(1)}, bf16[2,4,96,584]{3,2,1,0:T(8,128)(2,1)S(1)}, u32[]{:S(2)}, u32[]{:S(2)}) collective-permute-start(bf16[2,4,96,584]{3,2,1,0:T(8,128)(2,1)S(1)} %fusion.107), channel_id=1, source_target_pairs={{0,4},{4,0},{8,12},{12,8},{16,20},{20,16},{24,28},{28,24},{1,5},{5... | collective-permute-start | bytes 2691080 | tf_op jit(solution)/shard_map/ppermute | solution.py:58
  441.5 13.1 %collective-permute-start.28 = (bf16[256,768]{1,0:T(8,128)(2,1)S(1)}, bf16[256,768]{1,0:T(8,128)(2,1)S(1)}, u32[]{:S(2)}, u32[]{:S(2)}) collective-permute-start(bf16[256,768]{1,0:T(8,128)(2,1)S(1)} %copy-done.88), channel_id=1, source_target_pairs={{2,0},{0,1},{6,2},{4,3},{3,4},{1,5},{7,6},{5,7},{10,8},{8,9},{14,1... | collective-permute-start | bytes 1179656 | tf_op jit(solution)/shard_map/ppermute | solution.py:87
  443.6 13.4 %copy-start.16 = (f32[2,4,2,96,584]{4,3,1,0,2:T(8,128)S(1)}, f32[2,4,2,96,584]{4,3,1,0,2:T(8,128)}, u32[]{:S(2)}) copy-start(f32[2,4,2,96,584]{4,3,1,0,2:T(8,128)} %copy-done.15) | copy-start | bytes 10764292
  443.6 18.1 %slice-start.10 = ((s8[11010048]{0:T(1024)(128)(4,1)}), s8[4194304]{0:T(1024)(128)(4,1)S(1)}, s32[]{:S(2)}) async-start(s8[11010048]{0:T(1024)(128)(4,1)} %bitcast.371), calls=%async_computation.10 | async-start | bytes 8388608
  459.4 15.3 %collective-permute-start.34 = (bf16[2,2,96,584]{3,2,1,0:T(8,128)(2,1)}, bf16[2,2,96,584]{3,2,1,0:T(8,128)(2,1)}, u32[]{:S(2)}, u32[]{:S(2)}) collective-permute-start(bf16[2,2,96,584]{3,2,1,0:T(8,128)(2,1)} %concatenate.558), channel_id=1, source_target_pairs={{0,16},{4,20},{8,24},{12,28},{16,0},{20,4},{24,8},{28,12},{1,17},{... | collective-permute-start | bytes 1345544 | tf_op jit(solution)/shard_map/ppermute | solution.py:58
  461.1 15.3 %collective-permute-start.30 = (bf16[2,2,96,584]{3,2,1,0:T(8,128)(2,1)}, bf16[2,2,96,584]{3,2,1,0:T(8,128)(2,1)}, u32[]{:S(2)}, u32[]{:S(2)}) collective-permute-start(bf16[2,2,96,584]{3,2,1,0:T(8,128)(2,1)} %pad_maximum_fusion.35), channel_id=1, source_target_pairs={{0,8},{4,12},{8,0},{12,4},{16,24},{20,28},{24,16},{28,20},{1,9},{5... | collective-permute-start | bytes 1345544 | tf_op jit(solution)/shard_map/ppermute | solution.py:58
  465.7 53.1 %collective-permute-start.43 = (bf16[2,2,96,1728]{3,2,1,0:T(8,128)(2,1)}, bf16[2,2,96,1728]{3,2,1,0:T(8,128)(2,1)}, u32[]{:S(2)}, u32[]{:S(2)}) collective-permute-start(bf16[2,2,96,1728]{3,2,1,0:T(8,128)(2,1)} %concatenate.557), channel_id=1, source_target_pairs={{0,16},{4,20},{8,24},{12,28},{16,0},{20,4},{24,8},{28,12},{1,17},{... | collective-permute-start | bytes 3981320 | tf_op jit(solution)/shard_map/ppermute | solution.py:58
  473.1 49.6 %collective-permute-start.39 = (bf16[2,2,96,1728]{3,2,1,0:T(8,128)(2,1)S(1)}, bf16[2,2,96,1728]{3,2,1,0:T(8,128)(2,1)S(1)}, u32[]{:S(2)}, u32[]{:S(2)}) collective-permute-start(bf16[2,2,96,1728]{3,2,1,0:T(8,128)(2,1)S(1)} %pad_maximum_fusion.18), channel_id=1, source_target_pairs={{0,8},{4,12},{8,0},{12,4},{16,24},{20,28},{24,16},{28,20},{1,9},{5... | collective-permute-start | bytes 3981320 | tf_op jit(solution)/shard_map/ppermute | solution.py:58
  475.9 32.6 %collective-permute-start.35 = (bf16[2,1,96,584]{3,2,1,0:T(8,128)(2,1)S(1)}, bf16[2,1,96,584]{3,2,1,0:T(8,128)(2,1)S(1)}, u32[]{:S(2)}, u32[]{:S(2)}) collective-permute-start(bf16[2,1,96,584]{3,2,1,0:T(8,128)(2,1)S(1)} %slice.991), channel_id=1, source_target_pairs={{0,8},{4,12},{8,0},{12,4},{16,24},{20,28},{24,16},{28,20},{1,9},{5... | collective-permute-start | bytes 672776 | tf_op jit(solution)/shard_map/ppermute | solution.py:58
  477.7 32.7 %collective-permute-start.31 = (bf16[2,1,96,584]{3,2,1,0:T(8,128)(2,1)S(1)}, bf16[2,1,96,584]{3,2,1,0:T(8,128)(2,1)S(1)}, u32[]{:S(2)}, u32[]{:S(2)}) collective-permute-start(bf16[2,1,96,584]{3,2,1,0:T(8,128)(2,1)S(1)} %slice.992), channel_id=1, source_target_pairs={{0,16},{4,20},{8,24},{12,28},{16,0},{20,4},{24,8},{28,12},{1,17},{... | collective-permute-start | bytes 672776 | tf_op jit(solution)/shard_map/ppermute | solution.py:58
  508.6 8.6 %collective-permute-start.36 = (bf16[96,584]{1,0:T(8,128)(2,1)S(1)}, bf16[96,584]{1,0:T(8,128)(2,1)S(1)}, u32[]{:S(2)}, u32[]{:S(2)}) collective-permute-start(bf16[96,584]{1,0:T(8,128)(2,1)S(1)} %get-tuple-element.246), channel_id=1, source_target_pairs={{0,2},{1,3},{2,0},{3,1},{4,6},{5,7},{6,4},{7,5},{8,10},{9,11},{10,... | collective-permute-start | bytes 336392 | tf_op jit(solution)/shard_map/ppermute | solution.py:62
  508.6 8.5 %collective-permute-start.37 = (bf16[96,584]{1,0:T(8,128)(2,1)S(1)}, bf16[96,584]{1,0:T(8,128)(2,1)S(1)}, u32[]{:S(2)}, u32[]{:S(2)}) collective-permute-start(bf16[96,584]{1,0:T(8,128)(2,1)S(1)} %get-tuple-element.247), channel_id=1, source_target_pairs={{0,1},{1,2},{2,3},{3,0},{4,5},{5,6},{6,7},{7,4},{8,9},{9,10},{10,1... | collective-permute-start | bytes 336392 | tf_op jit(solution)/shard_map/ppermute | solution.py:62
  510.4 7.3 %collective-permute-start.32 = (bf16[96,584]{1,0:T(8,128)(2,1)S(1)}, bf16[96,584]{1,0:T(8,128)(2,1)S(1)}, u32[]{:S(2)}, u32[]{:S(2)}) collective-permute-start(bf16[96,584]{1,0:T(8,128)(2,1)S(1)} %fusion.188), channel_id=1, source_target_pairs={{0,3},{1,0},{2,1},{3,2},{4,7},{5,4},{6,5},{7,6},{8,11},{9,8},{10,9... | collective-permute-start | bytes 336392 | tf_op jit(solution)/shard_map/ppermute | solution.py:62
  520.5 12.5 %collective-permute-start.44 = (bf16[2,1,96,1728]{3,2,1,0:T(8,128)(2,1)S(1)}, bf16[2,1,96,1728]{3,2,1,0:T(8,128)(2,1)S(1)}, u32[]{:S(2)}, u32[]{:S(2)}) collective-permute-start(bf16[2,1,96,1728]{3,2,1,0:T(8,128)(2,1)S(1)} %slice.989), channel_id=1, source_target_pairs={{0,8},{4,12},{8,0},{12,4},{16,24},{20,28},{24,16},{28,20},{1,9},{5... | collective-permute-start | bytes 1990664 | tf_op jit(solution)/shard_map/ppermute | solution.py:58
  523.1 14.3 %collective-permute-start.40 = (bf16[2,1,96,1728]{3,2,1,0:T(8,128)(2,1)S(1)}, bf16[2,1,96,1728]{3,2,1,0:T(8,128)(2,1)S(1)}, u32[]{:S(2)}, u32[]{:S(2)}) collective-permute-start(bf16[2,1,96,1728]{3,2,1,0:T(8,128)(2,1)S(1)} %slice.990), channel_id=1, source_target_pairs={{0,16},{4,20},{8,24},{12,28},{16,0},{20,4},{24,8},{28,12},{1,17},{... | collective-permute-start | bytes 1990664 | tf_op jit(solution)/shard_map/ppermute | solution.py:58
  533.2 26.3 %collective-permute-start.45 = (bf16[96,1728]{1,0:T(8,128)(2,1)S(1)}, bf16[96,1728]{1,0:T(8,128)(2,1)S(1)}, u32[]{:S(2)}, u32[]{:S(2)}) collective-permute-start(bf16[96,1728]{1,0:T(8,128)(2,1)S(1)} %get-tuple-element.233), channel_id=1, source_target_pairs={{0,2},{1,3},{2,0},{3,1},{4,6},{5,7},{6,4},{7,5},{8,10},{9,11},{10,... | collective-permute-start | bytes 995336 | tf_op jit(solution)/shard_map/ppermute | solution.py:62
  536.8 22.6 %collective-permute-start.46 = (bf16[96,1728]{1,0:T(8,128)(2,1)S(1)}, bf16[96,1728]{1,0:T(8,128)(2,1)S(1)}, u32[]{:S(2)}, u32[]{:S(2)}) collective-permute-start(bf16[96,1728]{1,0:T(8,128)(2,1)S(1)} %get-tuple-element.234), channel_id=1, source_target_pairs={{0,1},{1,2},{2,3},{3,0},{4,5},{5,6},{6,7},{7,4},{8,9},{9,10},{10,1... | collective-permute-start | bytes 995336 | tf_op jit(solution)/shard_map/ppermute | solution.py:62
  537.6 21.9 %collective-permute-start.41 = (bf16[96,1728]{1,0:T(8,128)(2,1)S(1)}, bf16[96,1728]{1,0:T(8,128)(2,1)S(1)}, u32[]{:S(2)}, u32[]{:S(2)}) collective-permute-start(bf16[96,1728]{1,0:T(8,128)(2,1)S(1)} %fusion.172), channel_id=1, source_target_pairs={{0,3},{1,0},{2,1},{3,2},{4,7},{5,4},{6,5},{7,6},{8,11},{9,8},{10,9... | collective-permute-start | bytes 995336 | tf_op jit(solution)/shard_map/ppermute | solution.py:62
  (126 other events, 543.4 us)

commit v2 on v1

v2 whole, which is shorter than its diff:
```python
import functools
import math

import jax
import jax.numpy as jnp
from jax import lax
from jax.experimental import pallas as pl
from jax.experimental.pallas import tpu as pltpu
from jax.sharding import PartitionSpec as P

HD = 64
EPS = 1e-05
DEAD = -8000000000.0
ROOT_HALF = 0.7071067811865476
DENSITY = 0.3989422804014327
LOG2E = 1.4426950408889634
SCALE2 = 0.125 * LOG2E
BOTH = ("fsdp", "tensor")
LOW = jnp.bfloat16
FULL = jnp.float32
LANES = 128
CHUNK = 256
QUERIES = 256
ROWS = 128
MIB = 1 << 20
NT = (((1,), (1,)), ((), ()))
SMALL = 64

IN_VMEM = pl.BlockSpec(memory_space=pltpu.VMEM)
IN_SMEM = pl.BlockSpec(memory_space=pltpu.SMEM)
ANYWHERE = pl.BlockSpec(memory_space=pl.ANY)


def shape(dims, dtype):
    return jax.ShapeDtypeStruct(dims, dtype)


def fixed(dims):
    return pl.BlockSpec(dims, lambda i: (0,) * len(dims))


def params(grid=0, vmem=56):
    return pltpu.CompilerParams(
        vmem_limit_bytes=vmem * MIB, dimension_semantics=("arbitrary",) * grid if grid else None
    )


def cost(flops, touched, exps=0):
    return pl.CostEstimate(flops=int(flops), bytes_accessed=int(touched), transcendentals=int(exps))


def mm(left, right):
    return jnp.dot(left, right, preferred_element_type=FULL)


def mm_nt(left, right):
    return lax.dot_general(left, right, NT, preferred_element_type=FULL)


def flip(value):
    return value.astype(FULL).T.astype(value.dtype)


class Blocks:
    def __init__(self, arrays, slices, table_rows):
        self.arrays, self.slices, self.table_rows = arrays, slices, table_rows

    def count(self):
        return sum(a.shape[0] * a.shape[1] for a in self.arrays)

    def width(self):
        return self.arrays[0].shape[3]

    def copies(self, table, refs, scratch, sems):
        found = {}
        at = 0
        for ref, slices, row in zip(refs, self.slices, self.table_rows):
            n, _, rows, _ = ref.shape
            for place, s in enumerate(slices):
                for i in range(n):
                    start = pl.multiple_of(table[row, i], 16) if n > 1 else 0
                    found.setdefault(s, []).append(
                        pltpu.make_async_copy(
                            ref.at[i, place], scratch.at[s, pl.ds(start, rows), :], sems.at[at]
                        )
                    )
                    at += 1
        return found


def begin(copies):
    for group in copies.values():
        for copy in group:
            copy.start()


def finish(group):
    for copy in group:
        copy.wait()


def project_kernel(blocks, rows_few, table, x_ref, pick_ref, *rest):
    n = len(blocks.arrays)
    refs, (q_ref, kv_ref, small_ref, w, sems) = rest[:n], rest[n:]
    copies = blocks.copies(table, refs, w, sems)
    begin(copies)
    parts = len(copies)
    third = q_ref.shape[1] // parts
    base = 3 * third // LANES * LANES
    skip = 3 * third - base
    small_ref[...] = jnp.zeros_like(small_ref)
    queries, keys, values = [], [], []
    for s in range(parts):
        finish(copies[s])
        turned = w[s, :, base:].astype(FULL).T
        few = turned[skip : skip + 8]
        if s == 0:
            small_ref[0:8] = few
        small_ref[8 + s : 9 + s] = few[6:7]
        bias = mm(few.astype(LOW), pick_ref[...])[7:8]
        y = mm(x_ref[...], w[s])
        queries.append(y[:, :third] + bias[:, :third])
        keys.append(y[:, third : 2 * third])
        values.append(y[:, 2 * third : 3 * third] + bias[:, third:])
    q_ref[...] = jnp.concatenate(queries, axis=1).astype(LOW)
    width = q_ref.shape[1]
    kv_ref[:, :width] = jnp.concatenate(keys, axis=1).astype(LOW)
    kv_ref[:, width:] = jnp.concatenate(values, axis=1).astype(LOW)


def attend_kernel(q_ref, ko, ke, vo, ve, xk_ref, xq_ref, att_ref, lse_ref):
    pair = pl.program_id(0)
    k = jnp.concatenate([ko[...], ke[...]], axis=0)
    v_t = flip(jnp.concatenate([vo[...], ve[...]], axis=0))
    q = q_ref[...]
    rows = q.shape[0]
    ones = jnp.ones((16, k.shape[0]), LOW)
    outs = []
    for h in range(2):
        side = slice(HD * h, HD * h + HD)
        kh = jnp.concatenate([k[:, side], xk_ref[...]], axis=1)
        qh = jnp.concatenate([q[:, side], xq_ref[...]], axis=1)
        vt = jnp.concatenate([v_t[side], ones], axis=0)
        got = []
        for start in range(0, rows, QUERIES):
            span = slice(start, start + QUERIES)
            scores = mm_nt(kh, qh[span])
            top = jnp.max(scores, axis=0, keepdims=True)
            raised = jnp.exp2((scores - top) * SCALE2).astype(LOW)
            o = mm(vt, raised)
            denom = o[HD : HD + 1]
            got.append(o[:HD] * (1.0 / denom))
            lse_ref[pl.ds(2 * pair + h, 1), span] = top * SCALE2 + jnp.log2(denom)
        outs.append(jnp.concatenate(got, axis=1))
    att_ref[...] = jnp.concatenate(outs, axis=0).T.astype(LOW)


def attend_back_kernel(
    first, q_ref, g_ref, att_ref, ko, ke, vo, ve, xk_ref, xq_ref, lse_ref,
    dq_ref, sum_ref, dk_ref, dv_ref, ak_ref, av_ref,
):
    pair = pl.program_id(0) + first
    k = jnp.concatenate([ko[...], ke[...]], axis=0)
    v = jnp.concatenate([vo[...], ve[...]], axis=0)
    k_t = flip(k)
    q, g = q_ref[...], g_ref[...]
    rows = q.shape[0]
    product = (g.astype(FULL) * att_ref[...].astype(FULL)).T
    dqs, dks, dvs = [], [], []
    for h in range(2):
        side = slice(HD * h, HD * h + HD)
        kh = jnp.concatenate([k[:, side], xk_ref[...]], axis=1)
        qh = jnp.concatenate([q[:, side], xq_ref[...]], axis=1)
        inner = jnp.sum(product[side], axis=0, keepdims=True)
        lse = lse_ref[pl.ds(2 * pair + h, 1), :]
        vh, gh, qs = v[:, side], g[:, side], q[:, side]
        dk = dv = None
        got = []
        for start in range(0, rows, QUERIES):
            span = slice(start, start + QUERIES)
            probs = jnp.exp2(mm_nt(kh, qh[span]) * SCALE2 - lse[:, span])
            prob_grad = mm_nt(vh, gh[span])
            score_grad = (probs * (prob_grad - inner[:, span])).astype(LOW)
            more_v = mm(probs.astype(LOW), gh[span])
            more_k = mm(score_grad, qs[span])
            dv = more_v if dv is None else dv + more_v
            dk = more_k if dk is None else dk + more_k
            got.append(mm(k_t[side], score_grad))
        dqs.append(jnp.concatenate(got, axis=1))
        dks.append(dk)
        dvs.append(dv)
    dq = jnp.concatenate(dqs, axis=0).T * 0.125
    dq_ref[...] = dq.astype(LOW)
    sum_ref[...] = jnp.broadcast_to(jnp.sum(dq, axis=0, keepdims=True), sum_ref.shape)
    dk = jnp.concatenate(dks, axis=1) * 0.125
    dv = jnp.concatenate(dvs, axis=1)
    dk_ref[...] = dk[:rows]
    dv_ref[...] = dv[:rows]
    ak_ref[...] = dk[rows:].astype(LOW)
    av_ref[...] = dv[rows:].astype(LOW)


def means(value):
    return jnp.mean(value, axis=-1, keepdims=True)


def normalize(summed):
    center = summed - means(summed)
    inv = lax.rsqrt(means(center * center) + EPS)
    return center * inv, inv


def norm_back(grad, gain, unit, inv):
    scaled = grad * gain
    return inv * (scaled - means(scaled) - unit * means(scaled * unit))


def total(value):
    return jnp.sum(value, axis=0, keepdims=True)


def expand_kernel(blocks, table, x_ref, att_ref, small_ref, *rest):
    n = len(blocks.arrays)
    refs = rest[:n]
    normed_ref, unit_ref, inv_ref, low_ref, act_ref, slope_ref, w, attn, sems = rest[n:]
    copies = blocks.copies(table, refs, w, sems)
    parts = len(copies)
    step = pl.program_id(0)
    hidden = x_ref.shape[1]
    width = hidden // parts

    @pl.when(step == 0)
    def _():
        begin(copies)
        for s in range(parts):
            finish(copies[s])
        value = None
        for s in range(parts):
            more = mm_nt(att_ref[:, width * s : width * s + width], w[s, :, hidden : hidden + width])
            value = more if value is None else value + more
        attn[...] = value

        @pl.loop(0, x_ref.shape[0] // ROWS)
        def _(i):
            span = pl.ds(pl.multiple_of(i * ROWS, ROWS), ROWS)
            summed = x_ref[span].astype(FULL) + attn[span] + small_ref[0:1]
            unit, inv = normalize(summed)
            normed = unit * small_ref[1:2] + small_ref[2:3]
            normed_ref[span] = normed
            unit_ref[span] = unit
            inv_ref[span] = jnp.broadcast_to(inv, (ROWS, LANES))
            low_ref[span] = normed.astype(LOW)

    per = hidden // CHUNK
    s, lanes = step // per, pl.ds(pl.multiple_of(step % per * CHUNK, CHUNK), CHUNK)
    bias = small_ref[pl.ds(8 + s, 1), lanes]
    upper = mm(low_ref[...], w[s, :, lanes]) + bias
    below = 0.5 * (1.0 + lax.erf(upper * ROOT_HALF))
    act_ref[...] = (upper * below).astype(LOW)
    slope_ref[...] = (below + upper * jnp.exp(-0.5 * upper * upper) * DENSITY).astype(LOW)


def shrink_kernel(blocks, table, act_ref, normed_ref, small_ref, cot_ref, live_ref, *rest):
    n = len(blocks.arrays)
    refs = rest[:n]
    out_ref, grad_ref, low_ref, vec_ref, w, acc, sems = rest[n:]
    copies = blocks.copies(table, refs, w, sems)
    step = pl.program_id(0)
    hidden = normed_ref.shape[1]
    per = hidden // CHUNK
    s, lanes = step // per, pl.ds(pl.multiple_of(step % per * CHUNK, CHUNK), CHUNK)

    @pl.when(step == 0)
    def _():
        begin(copies)

    for part, group in copies.items():

        @pl.when(step == part * per)
        def _(group=group):
            finish(group)

    more = mm_nt(act_ref[...], w[s, :, lanes])

    @pl.when(step == 0)
    def _():
        acc[...] = more

    @pl.when(step > 0)
    def _():
        acc[...] += more

    @pl.when(step == pl.num_programs(0) - 1)
    def _():
        vec_ref[...] = jnp.zeros_like(vec_ref)

        @pl.loop(0, normed_ref.shape[0] // ROWS)
        def _(i):
            span = pl.ds(pl.multiple_of(i * ROWS, ROWS), ROWS)
            summed = normed_ref[span] + acc[span] + small_ref[3:4]
            unit, inv = normalize(summed)
            out_ref[span] = (unit * small_ref[4:5] + small_ref[5:6]).astype(LOW)
            arriving = cot_ref[span].astype(FULL) * live_ref[span, 0:1]
            grad = norm_back(arriving, small_ref[4:5], unit, inv)
            grad_ref[span] = grad
            low_ref[span] = grad.astype(LOW)
            vec_ref[0:1] += total(grad)
            vec_ref[1:2] += total(arriving * unit)
            vec_ref[2:3] += total(arriving)


class Exits:
    def __init__(self, flat, outers, rows, table_rows):
        self.flat, self.outers, self.rows, self.table_rows = flat, outers, rows, table_rows

    def shapes(self, slices, width):
        dims = (self.outers, slices, self.rows, width)
        if self.flat:
            return [shape((slices, 2 * self.outers * self.rows, width), LOW)]
        return [shape(dims, LOW)] * 2

    def emit(self, table, value_ref, refs, s, lanes):
        if self.flat:
            refs[0][s, :, lanes] = value_ref[...].astype(LOW)
            return
        for ref, row in zip(refs, self.table_rows):
            for i in range(self.outers):
                start = pl.multiple_of(table[row, i], 8)
                ref[i, s, :, lanes] = value_ref[pl.ds(start, self.rows), :].astype(LOW)


def shrink_grad_kernel(exits, table, low_ref, act_ref, *rest):
    outs, (turned, stage) = rest[:-2], rest[-2:]

    @pl.when(pl.program_id(0) == 0)
    def _():
        turned[...] = flip(low_ref[...])

    stage[...] = mm(turned[...], act_ref[...])
    exits.emit(table, stage, outs, 0, slice(None))


def middle_kernel(
    ups, downs, exits, table, low_ref, normed_low_ref, slope_ref, grad_ref, unit_ref, inv_ref,
    small_ref, att_ref, *rest,
):
    n, m = len(ups.arrays), len(downs.arrays)
    up_refs, down_refs, rest = rest[:n], rest[n : n + m], rest[n + m :]
    first_ref, first_low_ref, att_grad_ref, vec_ref, expand_ref = rest[:5]
    outs = rest[5:-8]
    up_w, down_w, up_sems, down_sems, turned, acc, stage, stage_o = rest[-8:]
    up_copies = ups.copies(table, up_refs, up_w, up_sems)
    down_copies = downs.copies(table, down_refs, down_w, down_sems)
    parts = len(up_copies)
    step = pl.program_id(0)
    hidden = unit_ref.shape[1]
    width = hidden // parts
    per = hidden // CHUNK
    s, lanes = step // per, pl.ds(pl.multiple_of(step % per * CHUNK, CHUNK), CHUNK)

    @pl.when(step == 0)
    def _():
        for part in range(parts):
            begin({0: down_copies[part], 1: up_copies[part]})
        turned[...] = flip(normed_low_ref[...])
        expand_ref[...] = jnp.zeros_like(expand_ref)

    for part in range(parts):

        @pl.when(step == part * per)
        def _(part=part):
            finish(down_copies[part])
            finish(up_copies[part])

    upper_grad = mm(low_ref[...], down_w[s, :, lanes]) * slope_ref[...].astype(FULL)
    expand_ref[pl.ds(s, 1), lanes] = total(upper_grad)
    upper_low = upper_grad.astype(LOW)
    stage[...] = mm(turned[...], upper_low)
    exits.emit(table, stage, outs, s, lanes)
    more = mm_nt(upper_low, up_w[s, :, lanes])

    @pl.when(step == 0)
    def _():
        acc[...] = more

    @pl.when(step > 0)
    def _():
        acc[...] += more

    @pl.when(step == pl.num_programs(0) - 1)
    def _():
        vec_ref[...] = jnp.zeros_like(vec_ref)

        @pl.loop(0, unit_ref.shape[0] // ROWS)
        def _(i):
            span = pl.ds(pl.multiple_of(i * ROWS, ROWS), ROWS)
            grad = acc[span] + grad_ref[span]
            unit = unit_ref[span]
            first = norm_back(grad, small_ref[1:2], unit, inv_ref[span, 0:1])
            first_ref[span] = first
            first_low_ref[span] = first.astype(LOW)
            vec_ref[0:1] += total(first)
            vec_ref[1:2] += total(grad * unit)
            vec_ref[2:3] += total(grad)

        turned[...] = flip(first_low_ref[...])
        grads = []
        for part in range(parts):
            o = up_w[part, :, hidden : hidden + width]
            grads.append(mm(first_low_ref[...], o))
            stage_o[...] = mm(turned[...], att_ref[:, width * part : width * part + width])
            exits.emit(table, stage_o, outs, part, slice(hidden, hidden + width))
        att_grad_ref[...] = jnp.concatenate(grads, axis=1).astype(LOW)


def input_kernel(
    blocks, exits, slices, table, x_ref, dq_ref, dqs_ref, dk_ref, dv_ref, add_ref, sofar_ref,
    one_ref, two_ref, expand_ref, pick_ref, *rest,
):
    n = len(blocks.arrays)
    refs, rest = rest[:n], rest[n:]
    grad_ref, outs = rest[0], rest[1:-4]
    w, vecs, stage, sems = rest[-4:]
    copies = blocks.copies(table, refs, w, sems)
    begin(copies)
    turned = flip(x_ref[...])
    rows = x_ref.shape[0]
    wide = dq_ref.shape[1]
    width = wide // len(slices)
    dq = dq_ref[...]
    dk = (dk_ref[...] + add_ref[:, :wide].astype(FULL)).astype(LOW)
    dv_full = dv_ref[...] + add_ref[:, wide:].astype(FULL)
    dv = dv_full.astype(LOW)
    dvs = total(dv_full)
    base = 3 * width // LANES * LANES
    skip = 3 * width - base
    vecs[...] = jnp.zeros_like(vecs)
    vecs[skip : skip + 3] = one_ref[0:3]
    vecs[skip + 3 : skip + 6] = two_ref[0:3]
    grad = sofar_ref[...]
    for i, s in enumerate(slices):
        side = slice(width * i, width * i + width)
        low = jnp.concatenate([dq[:, side], dk[:, side], dv[:, side], jnp.zeros((rows, SMALL), LOW)], axis=1)
        stage[...] = mm(turned, low)
        sums = jnp.concatenate([dqs_ref[:, side], jnp.broadcast_to(dvs[:, side], (8, width))], axis=1)
        high = sums.astype(LOW)
        rest_of = (sums - high.astype(FULL)).astype(LOW)
        heads = mm_nt(high, pick_ref[...]) + mm_nt(rest_of, pick_ref[...])
        vecs[skip + 6 : skip + 7] = expand_ref[s : s + 1]
        vecs[skip + 7 : skip + 8] = heads[0:1]
        stage[:, base:] += vecs[...].T
        exits.emit(table, stage, outs, i, slice(None))
        finish(copies[s])
        grad = grad + mm_nt(low, w[s])
    grad_ref[...] = grad.astype(grad_ref.dtype)


class Plan:
    def __init__(self, rows):
        self.parts = lax.axis_size("tensor")
        self.owners = lax.axis_size("fsdp")
        self.place = lax.axis_index("tensor")
        self.owner = lax.axis_index("fsdp")
        self.core = self.owner % 2
        self.outer = self.owner // 2
        self.outers = self.owners // 2
        self.rows = rows
        self.flat = rows % 16 != 0
        self.bits = [1 << n for n in range((self.outers - 1).bit_length())]
        rising = list(range(self.outers))
        falling = [0]
        for bit in self.bits[::-1]:
            falling = falling + [n ^ bit for n in falling]
        self.orders = (rising, falling)
        own = jnp.array([rising, rising, falling, falling], jnp.int32) ^ self.outer
        core = jnp.array([0, 1, 0, 1], jnp.int32)[:, None] ^ self.core
        self.table = ((own * 2 + core) * rows).astype(jnp.int32)

    def swap(self, value, bit):
        return lax.ppermute(value, "fsdp", [(n, n ^ bit) for n in range(self.owners)])

    def turn(self, value, by):
        n = self.parts
        return lax.ppermute(value, "tensor", [(i, (i + by) % n) for i in range(n)])

    def trade(self, turn, back):
        pairs = []
        half = self.parts // 2
        for owner in range(self.owners):
            for place in range(self.parts):
                micro = (place + turn) % 2
                there = (owner - owner % 2 + place // half) * self.parts + 2 * micro + owner % 2
                here = owner * self.parts + place
                pairs.append((there, here) if back else (here, there))
        return pairs

    def collect(self, value):
        return [
            lax.ppermute(
                lax.dynamic_index_in_dim(value, (self.place + turn) % 2, 0, False),
                BOTH,
                self.trade(turn, False),
            )
            for turn in range(2)
        ]

    def release(self, blocks):
        first, second = [
            lax.ppermute(block, BOTH, self.trade(turn, True)) for turn, block in enumerate(blocks)
        ]
        even = self.place % 2 == 0
        return jnp.stack([jnp.where(even, first, second), jnp.where(even, second, first)])

    def around(self, shard):
        return [shard] + [self.turn(shard, by) for by in range(1, self.parts)]

    def gather(self, lots):
        arrays, numbers, table_rows = [], [], []
        for lot, names, falling in lots:
            held = jnp.stack(lot)[None]
            for bit in self.bits[::-1] if falling else self.bits:
                held = jnp.concatenate([held, self.swap(held, 2 * bit)])
            other = self.swap(held, 1)
            if self.flat:
                arrays.append(self.natural(held, other, self.orders[falling]))
                numbers.append(names)
                table_rows.append(0)
            else:
                arrays += [held, other]
                numbers += [names, names]
                table_rows += [2 * falling, 2 * falling + 1]
        return Blocks(arrays, numbers, table_rows)

    def natural(self, mine, other, order):
        where = jnp.array([order.index(n) for n in range(self.outers)])
        both = []
        for n in range(self.outers):
            at = where[n ^ self.outer]
            pair = [lax.dynamic_index_in_dim(v, at, 0, False) for v in (mine, other)]
            both.append(jnp.where(self.core == 0, pair[0], pair[1]))
            both.append(jnp.where(self.core == 0, pair[1], pair[0]))
        return jnp.concatenate(both, axis=1)[None]

    def exits(self, falling):
        row = 0 if falling else 2
        return Exits(self.flat, self.outers, self.rows, (row, row + 1))

    def reduce(self, blocks, names, falling):
        if self.flat:
            order = self.orders[not falling]
            value = blocks[0].reshape(len(names), self.outers, 2, self.rows, -1)
            pair = [
                jnp.concatenate(
                    [
                        lax.dynamic_slice(
                            value,
                            (0, n ^ self.outer, core, 0, 0),
                            (len(names), 1, 1, self.rows, value.shape[-1]),
                        )[:, 0]
                        for n in order
                    ],
                    axis=1,
                ).swapaxes(0, 1)
                for core in (self.core, 1 - self.core)
            ]
            blocks = pair
        keep, send = blocks
        terms = [keep, self.swap(send, 1)]
        n = self.outers
        for bit in self.bits[::-1] if falling else self.bits:
            n //= 2
            away = sum(t[n:].astype(FULL) for t in terms).astype(LOW)
            terms = [t[:n] for t in terms] + [self.swap(away, 2 * bit)]
        value = 0.0
        for i, by in enumerate(names):
            term = sum(t[0, i].astype(FULL) for t in terms)
            value = value + (self.turn(term.astype(LOW), -by).astype(FULL) if by else term)
        return value


def column(vector, rows):
    return jnp.pad(vector, (0, rows - vector.shape[0]))[:, None]


def shards(
    tokens, lengths, cotangent, query_proj, key_proj, value_proj, output_proj, expand_proj,
    shrink_proj, query_bias, value_bias, expand_bias, output_bias, attn_gain, attn_shift,
    shrink_bias, ffn_gain, ffn_shift,
):
    rows, width = query_proj.shape
    plan = Plan(rows)
    parts = plan.parts
    hidden = expand_proj.shape[1]
    few = query_bias.shape[0]
    block = tokens.shape[2]
    mine = 2 * block
    model = tokens.shape[3]
    three = 3 * width
    table = plan.table

    smalls = [output_bias, attn_gain, attn_shift, shrink_bias, ffn_gain, ffn_shift, expand_bias]
    pack_one = jnp.concatenate(
        [query_proj, key_proj, value_proj]
        + [column(v, rows) for v in smalls]
        + [column(jnp.concatenate([query_bias, value_bias]), rows)]
        + [jnp.zeros((rows, SMALL - 8), LOW)],
        axis=1,
    )
    pack_two = jnp.concatenate([expand_proj, output_proj.T, shrink_proj.T], axis=1)
    wide_one, wide_two, wide_three = pack_one.shape[1], hidden + width, hidden
    ones = plan.around(pack_one)
    own_tokens = plan.collect(tokens[:, 0])
    twos = plan.around(pack_two)
    half = parts // 2
    low_names, high_names, names = list(range(half)), list(range(half, parts)), list(range(parts))
    qkv_w = plan.gather([(ones[:half], low_names, False), (ones[half:], high_names, True)])
    up_w = plan.gather([([t[:, :wide_two] for t in twos], names, False)])
    down_w = plan.gather([([t[:, wide_two:] for t in twos], names, True)])
    place = jnp.arange(model)[:, None]
    head = jnp.arange(2 * width)[None, :]
    inside = head % width
    pick = (place == inside // few * rows + inside % few + few * (head // width)).astype(LOW)

    micro, parity = plan.place // 2, plan.place % 2
    seen = jnp.where(parity == plan.core, lengths, plan.swap(lengths, 1))[:, 0]
    length = jnp.where(micro == 0, seen[0], seen[1])

    def slots_of(core):
        return jnp.concatenate(
            [block * (2 * core + (micro + n) % 2) + jnp.arange(block) for n in range(2)]
        )

    row_slots = slots_of(plan.core)
    live_rows = jnp.broadcast_to((row_slots < length).astype(FULL)[:, None], (mine, LANES))
    live = jnp.concatenate([row_slots, slots_of(1 - plan.core)]) < length
    lead = jnp.arange(HD)[None, :] == 0
    extra_k = jnp.where(lead & ~live[:, None], DEAD, 0.0).astype(LOW)
    extra_q = jnp.broadcast_to(lead, (mine, HD)).astype(LOW)

    x = jnp.concatenate(own_tokens)
    dot_cost = 2 * mine * model * model
    query, key_value, small = pl.pallas_call(
        functools.partial(project_kernel, qkv_w, few),
        out_shape=[shape((mine, model), LOW), shape((mine, 2 * model), LOW), shape((16, model), FULL)],
        in_specs=[IN_SMEM, IN_VMEM, IN_VMEM] + [ANYWHERE] * len(qkv_w.arrays),
        out_specs=[IN_VMEM] * 3,
        scratch_shapes=[
            pltpu.VMEM((parts, model, wide_one), LOW),
            pltpu.SemaphoreType.DMA((qkv_w.count(),)),
        ],
        compiler_params=params(),
        cost_estimate=cost(3 * dot_cost, 8 * MIB),
        name="project",
    )(table, x, pick, *qkv_w.arrays)
    other = plan.swap(key_value, 1)
    pairs = model // LANES
    heads = 2 * pairs
    pad_heads = -(-heads // 8) * 8
    all_rows = 2 * mine

    def lane_block(offset):
        return pl.BlockSpec((mine, LANES), lambda i: (0, i + offset))

    score_cost = 2 * mine * all_rows * HD
    attended, log_total = pl.pallas_call(
        attend_kernel,
        out_shape=[shape((mine, model), LOW), shape((pad_heads, mine), FULL)],
        grid=(pairs,),
        in_specs=[
            lane_block(0), lane_block(0), lane_block(0), lane_block(pairs), lane_block(pairs),
            fixed((all_rows, HD)), fixed((mine, HD)),
        ],
        out_specs=[lane_block(0), fixed((pad_heads, mine))],
        compiler_params=params(1),
        cost_estimate=cost(6 * heads * score_cost, 6 * MIB, heads * mine * all_rows),
        name="attend",
    )(query, key_value, other, key_value, other, extra_k, extra_q)

    chunks = parts * hidden // CHUNK
    per = hidden // CHUNK
    chunk_block = pl.BlockSpec((mine, CHUNK), lambda i: (0, i))
    full_rows = fixed((mine, model))
    normed, unit, inv, normed_low, active, slope = pl.pallas_call(
        functools.partial(expand_kernel, up_w),
        out_shape=[
            shape((mine, model), FULL), shape((mine, model), FULL), shape((mine, LANES), FULL),
            shape((mine, model), LOW), shape((mine, parts * hidden), LOW), shape((mine, parts * hidden), LOW),
        ],
        grid=(chunks,),
        in_specs=[IN_SMEM, full_rows, full_rows, fixed((16, model))] + [ANYWHERE] * len(up_w.arrays),
        out_specs=[full_rows, full_rows, fixed((mine, LANES)), full_rows, chunk_block, chunk_block],
        scratch_shapes=[
            pltpu.VMEM((parts, model, wide_two), LOW),
            pltpu.VMEM((mine, model), FULL),
            pltpu.SemaphoreType.DMA((up_w.count(),)),
        ],
        compiler_params=params(1),
        cost_estimate=cost(8 * dot_cost, 20 * MIB),
        name="expand",
    )(table, x, attended, small, *up_w.arrays)
    cot = jnp.concatenate(plan.collect(cotangent[:, 0]))
    layer_rows, second_grad, second_low, vec_two = pl.pallas_call(
        functools.partial(shrink_kernel, down_w),
        out_shape=[
            shape((mine, model), LOW), shape((mine, model), FULL), shape((mine, model), LOW), shape((8, model), FULL),
        ],
        grid=(chunks,),
        in_specs=[
            IN_SMEM, chunk_block, full_rows, fixed((16, model)), full_rows, fixed((mine, LANES)),
        ] + [ANYWHERE] * len(down_w.arrays),
        out_specs=[full_rows, full_rows, full_rows, fixed((8, model))],
        scratch_shapes=[
            pltpu.VMEM((parts, model, wide_three), LOW),
            pltpu.VMEM((mine, model), FULL),
            pltpu.SemaphoreType.DMA((down_w.count(),)),
        ],
        compiler_params=params(1),
        cost_estimate=cost(5 * dot_cost, 16 * MIB),
        name="shrink",
    )(table, active, normed, small, cot, live_rows, *down_w.arrays)
    layer_out = plan.release([layer_rows[:block], layer_rows[block:]])

    exits = plan.exits(False)
    if plan.flat:
        grad_block = [pl.BlockSpec((1, model, CHUNK), lambda i: (i // per, 0, i % per))]
    else:
        grad_block = [
            pl.BlockSpec((plan.outers, 1, rows, CHUNK), lambda i: (0, i // per, 0, i % per))
        ] * 2
    blocks = pl.pallas_call(
        functools.partial(shrink_grad_kernel, exits),
        out_shape=exits.shapes(parts, hidden),
        grid=(chunks,),
        in_specs=[IN_SMEM, full_rows, chunk_block],
        out_specs=grad_block,
        scratch_shapes=[pltpu.VMEM((model, mine), LOW), pltpu.VMEM((model, CHUNK), FULL)],
        compiler_params=params(1),
        cost_estimate=cost(4 * dot_cost, 9 * MIB),
        name="shrink_grad",
    )(table, second_low, active)
    sums_three = plan.reduce(blocks, names, False)

    exits = plan.exits(True)
    grad_shapes = exits.shapes(parts, wide_two)
    first_grad, first_low, attended_grad, vec_one, expand_sums, *blocks = pl.pallas_call(
        functools.partial(middle_kernel, up_w, down_w, exits),
        out_shape=[
            shape((mine, model), FULL), shape((mine, model), LOW), shape((mine, model), LOW),
            shape((8, model), FULL), shape((8, model), FULL),
        ] + grad_shapes,
        grid=(chunks,),
        in_specs=[
            IN_SMEM, full_rows, full_rows, chunk_block, full_rows, full_rows, fixed((mine, LANES)),
            fixed((16, model)), full_rows,
        ] + [ANYWHERE] * (len(up_w.arrays) + len(down_w.arrays)),
        out_specs=[full_rows, full_rows, full_rows, fixed((8, model)), fixed((8, model))]
        + [fixed(g.shape) for g in grad_shapes],
        scratch_shapes=[
            pltpu.VMEM((parts, model, wide_two), LOW),
            pltpu.VMEM((parts, model, wide_three), LOW),
            pltpu.SemaphoreType.DMA((up_w.count(),)),
            pltpu.SemaphoreType.DMA((down_w.count(),)),
            pltpu.VMEM((model, mine), LOW),
            pltpu.VMEM((mine, model), FULL),
            pltpu.VMEM((model, CHUNK), FULL),
            pltpu.VMEM((model, width), FULL),
        ],
        compiler_params=params(1),
        cost_estimate=cost(14 * dot_cost, 30 * MIB),
        name="middle",
    )(
        table, second_low, normed_low, slope, second_grad, unit, inv, small, attended,
        *up_w.arrays, *down_w.arrays,
    )
    sums_two = plan.reduce(blocks, names, True)

    input_grad, sums_one = first_grad, 0.0
    few_pairs = pairs // 2
    for turn, lot in enumerate((high_names, low_names)):
        last = turn == 1
        first = lot[0] * width // LANES
        wide = len(lot) * width

        def from_block(offset, first=first):
            return pl.BlockSpec((mine, LANES), lambda i: (0, i + first + offset))

        lot_block = pl.BlockSpec((mine, LANES), lambda i: (0, i))
        dq, dq_sum, dk, dv, away_k, away_v = pl.pallas_call(
            functools.partial(attend_back_kernel, first),
            out_shape=[
                shape((mine, wide), LOW), shape((8, wide), FULL), shape((mine, wide), FULL),
                shape((mine, wide), FULL), shape((mine, wide), LOW), shape((mine, wide), LOW),
            ],
            grid=(few_pairs,),
            in_specs=[
                from_block(0), from_block(0), from_block(0), from_block(0), from_block(0),
                from_block(pairs), from_block(pairs), fixed((all_rows, HD)), fixed((mine, HD)),
                fixed((pad_heads, mine)),
            ],
            out_specs=[lot_block, pl.BlockSpec((8, LANES), lambda i: (0, i))] + [lot_block] * 4,
            compiler_params=params(1),
            cost_estimate=cost(10 * heads * score_cost, 8 * MIB, heads * mine * all_rows // 2),
            name="attend_back",
        )(
            query, attended_grad, attended, key_value, other, key_value, other, extra_k, extra_q,
            log_total,
        )
        added = plan.swap(jnp.concatenate([away_k, away_v], axis=1), 1)
        index = [i for i, names_here in enumerate(qkv_w.slices) if names_here == lot]
        part_w = Blocks(
            [qkv_w.arrays[i] for i in index], [lot] * len(index), [qkv_w.table_rows[i] for i in index]
        )
        exits = plan.exits(turn == 0)
        grad_shapes = exits.shapes(len(lot), wide_one)
        input_grad, *blocks = pl.pallas_call(
            functools.partial(input_kernel, part_w, exits, lot),
            out_shape=[shape((mine, model), LOW if last else FULL)] + grad_shapes,
            in_specs=[IN_SMEM] + [IN_VMEM] * 11 + [ANYWHERE] * len(part_w.arrays),
            out_specs=[IN_VMEM] * (1 + len(grad_shapes)),
            scratch_shapes=[
                pltpu.VMEM((parts, model, wide_one), LOW),
                pltpu.VMEM((LANES, model), FULL),
                pltpu.VMEM((model, wide_one), FULL),
                pltpu.SemaphoreType.DMA((part_w.count(),)),
            ],
            compiler_params=params(),
            cost_estimate=cost(3 * dot_cost, 12 * MIB),
            name="input_grad",
        )(table, x, dq, dq_sum, dk, dv, added, input_grad, vec_one, vec_two, expand_sums, pick, *part_w.arrays)
        sums_one = sums_one + plan.reduce(blocks, lot, turn == 0)
    input_rows = plan.release([input_grad[:block], input_grad[block:]]).astype(FULL)
    quarter = rows // parts
    own = lax.dynamic_slice_in_dim(sums_one[:, three : three + 6], plan.place * quarter, quarter, 0)
    return (
        layer_out[:, None],
        input_rows[:, None],
        sums_one[:, :width],
        sums_one[:, width : 2 * width],
        sums_one[:, 2 * width : three],
        sums_two[:, hidden:].T,
        sums_two[:, :hidden],
        sums_three.T,
        sums_one[:few, three + 7],
        sums_one[few : 2 * few, three + 7],
        sums_one[:, three + 6],
        own[:, 0],
        own[:, 1],
        own[:, 2],
        own[:, 3],
        own[:, 4],
        own[:, 5],
    )


def solution(mesh):
    rows = P(None, "fsdp", "tensor", None)
    split = P("fsdp", "tensor")
    turned = P("tensor", "fsdp")
    heads = P(("tensor", "fsdp"))
    model = P("fsdp")
    spread = P(("fsdp", "tensor"))
    return jax.shard_map(
        shards,
        mesh=mesh,
        in_specs=(rows, P(None, "fsdp"), rows, split, split, split, turned, split, turned)
        + (heads,) * 3
        + (model,) * 6,
        out_specs=(rows, rows, split, split, split, turned, split, turned)
        + (heads,) * 3
        + (spread,) * 6,
        check_vma=False,
    )
```

time: 570 us -> 443 us (0.78)
  Pallas kernels: 0 us -> 143 us
  matrix products: 127 us -> 0 us
  local copies, waits for them, and re-layouts: 137 us -> 16 us
  other arithmetic: 106 us -> 38.5 us
  waiting for transfers between devices: 94.1 us -> 158 us
  starting transfers between devices: 86.2 us -> 76.5 us
  between operations: 11.4 us -> 3.32 us
    pallas_call x0 -> x10, Pallas kernels: none -> 143 us  [the longest x1 28.4 us: shards(): pl.pallas_call(functools.partial(middle_kernel, up_w, down_w, exits), out...]
    dot_general x66 -> x0, matrix products: 127 us -> none  [contract(): return jnp.einsum(form, left, right, preferred_element_type=FULL)]
    concatenate x50 -> x1, local copies, waits for them, and re-layouts: 69.3 us -> 1.14 us  [shards(): jnp.concatenate([expand_proj, output_proj.T, shrink_proj.T], axis=1)]
    ppermute x12 -> x15, waiting for transfers between devices: 22 us -> 50.9 us  [turn(): return lax.ppermute(value, 'tensor', [(i, (i + by) % n) for i in range(n)])]
    ppermute x27 -> x28, waiting for transfers between devices: 62 us -> 85.4 us  [swap(): lax.ppermute(value, 'fsdp', [(n, n ^ bit) for n in range(self.owners)])]
    unnamed x288 -> x81, local copies, waits for them, and re-layouts: 26.9 us -> 5.55 us
    concatenate x19 -> x3, other arithmetic: 22.8 us -> 3.41 us  [the longest x2 2.43 us: shards(): added = plan.swap(jnp.concatenate([away_k, away_v], axis=1), 1)]
    another operation x13 -> x1, other arithmetic: 19.6 us -> 0.93 us  [gather(): held = jnp.stack(lot)[None]]
  transfers between devices with their start and end apart: 47 -> 51, of which waited for: 10 -> 18; matrix products, arithmetic and copies ran while one was open for 35% -> 11% of each run, Pallas kernels for 0% -> 27%
where the time goes in v2:
time: 443 us; the launch traced here: 435 us
  waiting for transfers between devices  158 us (36%)
  Pallas kernels  143 us (32%)
  starting transfers between devices  76.5 us (17%)
  other arithmetic  38.5 us (9%)
  local copies, waits for them, and re-layouts  16 us (4%)
    ppermute x28, waiting for transfers between devices, swap(): lax.ppermute(value, 'fsdp', [(n, n ^ bit) for n in range(self.owners)])  85.4 us
    ppermute x15, waiting for transfers between devices, turn(): return lax.ppermute(value, 'tensor', [(i, (i + by) % n) for i in range(n)])  50.9 us
    ppermute x28, starting transfers between devices, swap(): lax.ppermute(value, 'fsdp', [(n, n ^ bit) for n in range(self.owners)])  31.7 us
    pallas_call x1, Pallas kernels, shards(): pl.pallas_call(functools.partial(middle_kernel, up_w, down_w, exits), out...  28.4 us
    ppermute x15, starting transfers between devices, turn(): return lax.ppermute(value, 'tensor', [(i, (i + by) % n) for i in range(n)])  26.2 us
    pallas_call x2, Pallas kernels, shards(): pl.pallas_call(functools.partial(attend_back_kernel, first), out_shape=[s...  22.7 us
    pallas_call x1, Pallas kernels, shards(): pl.pallas_call(attend_kernel, out_shape=[shape((mine, model), LOW), shape...  21 us
    pallas_call x2, Pallas kernels, shards(): pl.pallas_call(functools.partial(input_kernel, part_w, exits, lot), out_s...  19.3 us
  transfers between devices with their start and end apart: 51, of which 18 were waited for; matrix products, arithmetic and copies ran while one was open for 11% of the time, Pallas kernels for 27%

profile of v2, /device:TPU:0, one launch (start us, length us, event | category | flops | bytes accessed | tf_op | source)
XLA Modules:
  0.0 434.9 jit_solution(4786987068898042029)
XLA Ops:
  2.8 5.1 %collective-permute-start.15 = (bf16[96,1728]{1,0:T(8,128)(2,1)S(1)}, bf16[96,1728]{1,0:T(8,128)(2,1)S(1)}, u32[]{:S(2)}, u32[]{:S(2)}) collective-permute-start(bf16[96,1728]{1,0:T(8,128)(2,1)S(1)} %concatenate.83), channel_id=1, source_target_pairs={{0,3},{1,0},{2,1},{3,2},{4,7},{5,4},{6,5},{7,6},{8,11},{9,8},{10,9... | collective-permute-start | bytes 995336 | tf_op jit(solution)/shard_map/ppermute | solution.py:484
  9.9 6.5 %collective-permute-done.15 = bf16[96,1728]{1,0:T(8,128)(2,1)S(1)} collective-permute-done((bf16[96,1728]{1,0:T(8,128)(2,1)S(1)}, bf16[96,1728]{1,0:T(8,128)(2,1)S(1)}, u32[]{:S(2)}, u32[]{:S(2)}) %collective-permute-start.15) | collective-permute-done | bytes 331808 | tf_op jit(solution)/shard_map/ppermute | solution.py:484
  16.4 20.8 %collective-permute-done.14 = bf16[96,1728]{1,0:T(8,128)(2,1)S(1)} collective-permute-done((bf16[96,1728]{1,0:T(8,128)(2,1)S(1)}, bf16[96,1728]{1,0:T(8,128)(2,1)S(1)}, u32[]{:S(2)}, u32[]{:S(2)}) %collective-permute-start.14) | collective-permute-done | bytes 331808 | tf_op jit(solution)/shard_map/ppermute | solution.py:484
  37.4 1.6 collective-permute-start.16
  40.3 2.8 collective-permute-start.6
  43.6 1.6 collective-permute-start.2
  45.2 6.3 %collective-permute-done.6 = bf16[96,640]{1,0:T(8,128)(2,1)S(1)} collective-permute-done((bf16[96,640]{1,0:T(8,128)(2,1)S(1)}, bf16[96,640]{1,0:T(8,128)(2,1)S(1)}, u32[]{:S(2)}, u32[]{:S(2)}) %collective-permute-start.6) | collective-permute-done | bytes 122912 | tf_op jit(solution)/shard_map/ppermute | solution.py:484
  52.1 1.6 collective-permute-start.8
  54.4 3.5 collective-permute-done.16
  58.0 1.4 pad_maximum_fusion.2
  59.4 1.5 collective-permute-start.17
  61.2 1.6 collective-permute-start.9
  64.3 1.5 collective-permute-start.4
  66.7 4.5 %collective-permute-start = (bf16[256,768]{1,0:T(8,128)(2,1)}, bf16[256,768]{1,0:T(8,128)(2,1)}, u32[]{:S(2)}, u32[]{:S(2)}) collective-permute-start(bf16[256,768]{1,0:T(8,128)(2,1)} %get-tuple-element.160), channel_id=1, source_target_pairs={{0,0},{1,2},{2,4},{3,6},{4,1},{5,3},{6,5},{7,7},{8,8},{9,10},{10,1... | collective-permute-start | bytes 1179656 | tf_op jit(solution)/shard_map/ppermute | solution.py:499
  73.0 42.3 %collective-permute-done.4 = bf16[2,2,96,640]{3,2,1,0:T(8,128)(2,1)} collective-permute-done((bf16[2,2,96,640]{3,2,1,0:T(8,128)(2,1)}, bf16[2,2,96,640]{3,2,1,0:T(8,128)(2,1)}, u32[]{:S(2)}, u32[]{:S(2)}) %collective-permute-start.4) | collective-permute-done | bytes 491552 | tf_op jit(solution)/shard_map/ppermute | solution.py:480
  115.3 1.1 pad_maximum_fusion.4.rest_0_
  116.6 1.6 pad_maximum_fusion.3
  118.2 1.4 collective-permute-start.22
  119.6 3.5 pad_maximum_fusion.rest_0_
  123.7 3.3 collective-permute-start.1
  129.1 5.7 %collective-permute-done.1 = bf16[256,768]{1,0:T(8,128)(2,1)S(1)} collective-permute-done((bf16[256,768]{1,0:T(8,128)(2,1)S(1)}, bf16[256,768]{1,0:T(8,128)(2,1)S(1)}, u32[]{:S(2)}, u32[]{:S(2)}) %collective-permute-start.1) | collective-permute-done | bytes 393248 | tf_op jit(solution)/shard_map/ppermute | solution.py:499
  137.0 8.0 %project.1 = (bf16[512,768]{1,0:T(8,128)(2,1)}, bf16[512,1536]{1,0:T(8,128)(2,1)}, f32[16,768]{1,0:T(8,128)}) custom-call(s32[4,4]{1,0:T(4,128)} %add_multiply_fusion.table, bf16[512,768]{1,0:T(8,128)(2,1)} %copy-done, bf16[768,384]{1,0:T(8,128)(2,1)} %fusion.pick_ref, bf16[4,2,96,640]{3,2,1,0:T(8,128)(2,1)} %copy-done.1, ...), custom_call_target="tpu_custom_call" | custom-call | flops 1811939328 | bytes 8388608 | tf_op jit(solution)/shard_map/project/pallas_call | solution.py:642
  145.1 2.4 collective-permute-start.11
  147.5 2.8 pad_maximum_fusion.1.rest_0_.rest_2_
  151.6 2.9 collective-permute-done.12
  154.5 1.9 collective-permute-start.20
  159.3 6.8 %collective-permute-done.20 = bf16[256,768]{1,0:T(8,128)(2,1)S(1)} collective-permute-done((bf16[256,768]{1,0:T(8,128)(2,1)S(1)}, bf16[256,768]{1,0:T(8,128)(2,1)S(1)}, u32[]{:S(2)}, u32[]{:S(2)}) %collective-permute-start.20) | collective-permute-done | bytes 393248 | tf_op jit(solution)/shard_map/ppermute | solution.py:499
  168.3 21.0 %attend.1 = (bf16[512,768]{1,0:T(8,128)(2,1)}, f32[16,512]{1,0:T(8,128)}) custom-call(bf16[512,768]{1,0:T(8,128)(2,1)} %get-tuple-element.58.q_ref, bf16[512,1536]{1,0:T(8,128)(2,1)} %get-tuple-element.59.ko.vo, bf16[512,1536]{1,0:T(8,128)(2,1)} %copy-done.35, bf16[512,1536]{1,0:T(8,128)(2,1)} %get-tuple-element.59.ko.vo, bf16[512,1536]{1,0:T(8,128)(2,1)} %copy-done.35, ...), custom_call_target="tpu_custom_call" | custom-call | flops 4831838208 | bytes 6291456 | tf_op jit(solution)/shard_map/attend/pallas_call | solution.py:665
  189.3 16.3 %expand.1 = (f32[512,768]{1,0:T(8,128)}, f32[512,768]{1,0:T(8,128)}, f32[512,128]{1,0:T(8,128)}, bf16[512,768]{1,0:T(8,128)(2,1)}, bf16[512,3072]{1,0:T(8,128)(2,1)}, /*index=5*/bf16[512,3072]{1,0:T(8,128)(2,1)}) custom-call(s32[4,4]{1,0:T(4,128)} %add_multiply_fusion.table, bf16[512,768]{1,0:T(8,128)(2,1)} %copy-done, ...), custom_call_target="tpu_custom_call" | custom-call | flops 4831838208 | bytes 20971520 | tf_op jit(solution)/shard_map/expand/pallas_call | solution.py:683
  206.5 16.1 %shrink.1 = (bf16[512,768]{1,0:T(8,128)(2,1)}, f32[512,768]{1,0:T(8,128)}, bf16[512,768]{1,0:T(8,128)(2,1)}, f32[8,768]{1,0:T(8,128)}) custom-call(s32[4,4]{1,0:T(4,128)} %add_multiply_fusion.table, bf16[512,3072]{1,0:T(8,128)(2,1)} %get-tuple-element.62.act_ref, f32[512,768]{1,0:T(8,128)} %get-tuple-element.63.normed_ref, ...), custom_call_target="tpu_custom_call" | custom-call | flops 3019898880 | bytes 16777216 | tf_op jit(solution)/shard_map/shrink/pallas_call | solution.py:702
  222.6 11.2 %shrink_grad.1 = (bf16[4,4,96,768]{3,2,1,0:T(8,128)(2,1)}, bf16[4,4,96,768]{3,2,1,0:T(8,128)(2,1)}) custom-call(s32[4,4]{1,0:T(4,128)} %add_multiply_fusion.table, bf16[512,768]{1,0:T(8,128)(2,1)} %get-tuple-element.65.low_ref, bf16[512,3072]{1,0:T(8,128)(2,1)} %get-tuple-element.62.act_ref), custom_call_target="tpu_custom_call" | custom-call | flops 2415919104 | bytes 9437184 | tf_op jit(solution)/shard_map/shrink_grad/pallas_call | solution.py:730
  233.7 7.3 %collective-permute-start.45 = (bf16[4,4,96,768]{3,2,1,0:T(8,128)(2,1)}, bf16[4,4,96,768]{3,2,1,0:T(8,128)(2,1)}, u32[]{:S(2)}, u32[]{:S(2)}) collective-permute-start(bf16[4,4,96,768]{3,2,1,0:T(8,128)(2,1)} %get-tuple-element.98), channel_id=1, source_target_pairs={{0,4},{4,0},{8,12},{12,8},{16,20},{20,16},{24,28},{28,24},{1,5},{5... | collective-permute-start | bytes 7077896 | tf_op jit(solution)/shard_map/ppermute | solution.py:480
  241.0 28.4 %middle.1 = (f32[512,768]{1,0:T(8,128)}, bf16[512,768]{1,0:T(8,128)(2,1)}, bf16[512,768]{1,0:T(8,128)(2,1)}, f32[8,768]{1,0:T(8,128)}, f32[8,768]{1,0:T(8,128)},...) custom-call(s32[4,4]{1,0:T(4,128)} %add_multiply_fusion.table, ...), custom_call_target="tpu_custom_call" | custom-call | flops 8455716864 | bytes 31457280 | tf_op jit(solution)/shard_map/middle/pallas_call | solution.py:745
  269.6 11.4 %attend_back.3 = (bf16[512,384]{1,0:T(8,128)(2,1)}, f32[8,384]{1,0:T(8,128)}, f32[512,384]{1,0:T(8,128)}, f32[512,384]{1,0:T(8,128)}, bf16[512,384]{1,0:T(8,128)(2,1)}, /*index=5*/bf16[512,384]{1,0:T(8,128)(2,1)}) custom-call(bf16[512,768]{1,0:T(8,128)(2,1)} %get-tuple-element.58.q_ref, bf16[512,768]{1,0:T(8,128)(2,1)} %get-tuple-element.71.g_ref, ...), custom_call_target="tpu_custom_call" | custom-call | flops 8053063680 | bytes 8388608 | tf_op jit(solution)/shard_map/attend_back/pallas_call | solution.py:788
  281.0 1.2 pad_maximum_fusion.8
  282.7 11.3 %attend_back.2 = (bf16[512,384]{1,0:T(8,128)(2,1)}, f32[8,384]{1,0:T(8,128)}, f32[512,384]{1,0:T(8,128)}, f32[512,384]{1,0:T(8,128)}, bf16[512,384]{1,0:T(8,128)(2,1)}, /*index=5*/bf16[512,384]{1,0:T(8,128)(2,1)}) custom-call(bf16[512,768]{1,0:T(8,128)(2,1)} %get-tuple-element.58.q_ref, bf16[512,768]{1,0:T(8,128)(2,1)} %get-tuple-element.71.g_ref, ...), custom_call_target="tpu_custom_call" | custom-call | flops 8053063680 | bytes 8388608 | tf_op jit(solution)/shard_map/attend_back/pallas_call | solution.py:788
  294.0 1.3 pad_maximum_fusion.7
  296.8 3.6 collective-permute-start.25
  300.5 9.8 %input_grad.2 = (f32[512,768]{1,0:T(8,128)}, bf16[4,2,96,640]{3,2,1,0:T(8,128)(2,1)}, bf16[4,2,96,640]{3,2,1,0:T(8,128)(2,1)}) custom-call(s32[4,4]{1,0:T(4,128)} %add_multiply_fusion.table, bf16[512,768]{1,0:T(8,128)(2,1)} %copy-done, bf16[512,384]{1,0:T(8,128)(2,1)} %get-tuple-element.79.dq_ref, f32[8,384]{1,0:T(8,128)} %get-tuple-element.80.dqs_ref, ...), custom_call_target="tpu_custom_call" | custom-call | flops 1811939328 | bytes 12582912 | tf_op jit(solution)/shard_map/input_grad/pallas_call | solution.py:815
  311.2 9.5 %input_grad.3 = (bf16[512,768]{1,0:T(8,128)(2,1)}, bf16[4,2,96,640]{3,2,1,0:T(8,128)(2,1)}, bf16[4,2,96,640]{3,2,1,0:T(8,128)(2,1)}) custom-call(s32[4,4]{1,0:T(4,128)} %add_multiply_fusion.table, bf16[512,768]{1,0:T(8,128)(2,1)} %copy-done, bf16[512,384]{1,0:T(8,128)(2,1)} %get-tuple-element.73.dq_ref, f32[8,384]{1,0:T(8,128)} %get-tuple-element.74.dqs_ref, ...), custom_call_target="tpu_custom_call" | custom-call | flops 1811939328 | bytes 12582912 | tf_op jit(solution)/shard_map/input_grad/pallas_call | solution.py:815
  324.6 3.1 collective-permute-start.29
  327.7 1.2 add_convert_fusion.5
  328.8 1.6 collective-permute-start.31
  330.4 1.2 add_convert_fusion.4
  331.9 1.7 add_convert_fusion.1
  333.7 1.8 collective-permute-start.46
  336.8 8.8 %collective-permute-done.29 = bf16[256,768]{1,0:T(8,128)(2,1)S(1)} collective-permute-done((bf16[256,768]{1,0:T(8,128)(2,1)S(1)}, bf16[256,768]{1,0:T(8,128)(2,1)S(1)}, u32[]{:S(2)}, u32[]{:S(2)}) %collective-permute-start.29) | collective-permute-done | bytes 393248 | tf_op jit(solution)/shard_map/ppermute | solution.py:509
  348.3 1.6 collective-permute-start.37
  349.9 1.2 maximum_convert_fusion
  351.2 24.6 %collective-permute-done.32 = bf16[1,2,96,640]{3,2,1,0:T(8,128)(2,1)S(1)} collective-permute-done((bf16[1,2,96,640]{3,2,1,0:T(8,128)(2,1)S(1)}, bf16[1,2,96,640]{3,2,1,0:T(8,128)(2,1)S(1)}, u32[]{:S(2)}, u32[]{:S(2)}) %collective-permute-start.32) | collective-permute-done | bytes 245792 | tf_op jit(solution)/shard_map/ppermute | solution.py:480
  376.9 1.7 collective-permute-start.34
  378.6 3.1 collective-permute-done.37
  382.7 1.5 collective-permute-start.38
  384.2 1.3 add_convert_fusion.3
  385.5 1.6 collective-permute-start.47
  392.9 6.8 %collective-permute-done.47 = bf16[1,4,96,768]{3,2,1,0:T(8,128)(2,1)S(1)} collective-permute-done((bf16[1,4,96,768]{3,2,1,0:T(8,128)(2,1)S(1)}, bf16[1,4,96,768]{3,2,1,0:T(8,128)(2,1)S(1)}, u32[]{:S(2)}, u32[]{:S(2)}) %collective-permute-start.47) | collective-permute-done | bytes 589856 | tf_op jit(solution)/shard_map/ppermute | solution.py:480
  399.7 1.3 fusion.10
  402.0 2.0 collective-permute-start.49
  404.0 1.6 collective-permute-done.41
  406.0 2.3 collective-permute-start.42
  409.1 5.9 %collective-permute-start.44 = (bf16[96,960]{1,0:T(8,128)(2,1)S(1)}, bf16[96,960]{1,0:T(8,128)(2,1)S(1)}, u32[]{:S(2)}, u32[]{:S(2)}) collective-permute-start(bf16[96,960]{1,0:T(8,128)(2,1)S(1)} %get-tuple-element.142), channel_id=1, source_target_pairs={{0,1},{1,2},{2,3},{3,0},{4,5},{5,6},{6,7},{7,4},{8,9},{9,10},{10,1... | collective-permute-start | bytes 552968 | tf_op jit(solution)/shard_map/ppermute | solution.py:484
  415.0 11.0 %collective-permute-done.49 = bf16[96,768]{1,0:T(8,128)(2,1)S(1)} collective-permute-done((bf16[96,768]{1,0:T(8,128)(2,1)S(1)}, bf16[96,768]{1,0:T(8,128)(2,1)S(1)}, u32[]{:S(2)}, u32[]{:S(2)}) %collective-permute-start.49) | collective-permute-done | bytes 147488 | tf_op jit(solution)/shard_map/ppermute | solution.py:484
  426.0 1.8 fusion.5
  427.8 4.9 %collective-permute-done.43 = bf16[96,960]{1,0:T(8,128)(2,1)S(1)} collective-permute-done((bf16[96,960]{1,0:T(8,128)(2,1)S(1)}, bf16[96,960]{1,0:T(8,128)(2,1)S(1)}, u32[]{:S(2)}, u32[]{:S(2)}) %collective-permute-start.43) | collective-permute-done | bytes 184352 | tf_op jit(solution)/shard_map/ppermute | solution.py:484
  (208 shorter events, 45.9 us)
Async XLA Ops:
  2.7 36.3 %copy-start.36 = (bf16[24]{0:T(256)(128)(2,1)S(1)}, bf16[24]{0:T(256)(128)(2,1)}, u32[]{:S(2)}) copy-start(bf16[24]{0:T(256)(128)(2,1)} %param.30) | copy-start | bytes 148
  2.7 36.3 %copy-start.37 = (bf16[24]{0:T(256)(128)(2,1)S(1)}, bf16[24]{0:T(256)(128)(2,1)}, u32[]{:S(2)}) copy-start(bf16[24]{0:T(256)(128)(2,1)} %param.29) | copy-start | bytes 148
  2.7 36.5 %copy-start.27 = (bf16[96]{0:T(256)(128)(2,1)S(1)}, bf16[96]{0:T(256)(128)(2,1)}, u32[]{:S(2)}) copy-start(bf16[96]{0:T(256)(128)(2,1)} %param.32) | copy-start | bytes 580
  2.7 36.6 %copy-start.28 = (bf16[96]{0:T(256)(128)(2,1)S(1)}, bf16[96]{0:T(256)(128)(2,1)}, u32[]{:S(2)}) copy-start(bf16[96]{0:T(256)(128)(2,1)} %param.33) | copy-start | bytes 580
  2.8 36.7 %copy-start.29 = (bf16[96]{0:T(256)(128)(2,1)S(1)}, bf16[96]{0:T(256)(128)(2,1)}, u32[]{:S(2)}) copy-start(bf16[96]{0:T(256)(128)(2,1)} %param.34) | copy-start | bytes 580
  2.8 36.8 %copy-start.30 = (bf16[96]{0:T(256)(128)(2,1)S(1)}, bf16[96]{0:T(256)(128)(2,1)}, u32[]{:S(2)}) copy-start(bf16[96]{0:T(256)(128)(2,1)} %param.35) | copy-start | bytes 580
  2.8 36.9 %copy-start.31 = (bf16[96]{0:T(256)(128)(2,1)S(1)}, bf16[96]{0:T(256)(128)(2,1)}, u32[]{:S(2)}) copy-start(bf16[96]{0:T(256)(128)(2,1)} %param.36) | copy-start | bytes 580
  2.8 37.0 %copy-start.32 = (bf16[96]{0:T(256)(128)(2,1)S(1)}, bf16[96]{0:T(256)(128)(2,1)}, u32[]{:S(2)}) copy-start(bf16[96]{0:T(256)(128)(2,1)} %param.37) | copy-start | bytes 580
  2.8 37.2 %copy-start.33 = (bf16[96]{0:T(256)(128)(2,1)S(1)}, bf16[96]{0:T(256)(128)(2,1)}, u32[]{:S(2)}) copy-start(bf16[96]{0:T(256)(128)(2,1)} %param.31) | copy-start | bytes 580
  2.8 13.6 %collective-permute-start.15 = (bf16[96,1728]{1,0:T(8,128)(2,1)S(1)}, bf16[96,1728]{1,0:T(8,128)(2,1)S(1)}, u32[]{:S(2)}, u32[]{:S(2)}) collective-permute-start(bf16[96,1728]{1,0:T(8,128)(2,1)S(1)} %concatenate.83), channel_id=1, source_target_pairs={{0,3},{1,0},{2,1},{3,2},{4,7},{5,4},{6,5},{7,6},{8,11},{9,8},{10,9... | collective-permute-start | bytes 995336 | tf_op jit(solution)/shard_map/ppermute | solution.py:484
  7.9 29.3 %collective-permute-start.14 = (bf16[96,1728]{1,0:T(8,128)(2,1)S(1)}, bf16[96,1728]{1,0:T(8,128)(2,1)S(1)}, u32[]{:S(2)}, u32[]{:S(2)}) collective-permute-start(bf16[96,1728]{1,0:T(8,128)(2,1)S(1)} %concatenate.83), channel_id=1, source_target_pairs={{0,2},{1,3},{2,0},{3,1},{4,6},{5,7},{6,4},{7,5},{8,10},{9,11},{10,... | collective-permute-start | bytes 995336 | tf_op jit(solution)/shard_map/ppermute | solution.py:484
  7.9 29.4 %collective-permute-start.13 = (bf16[96,1728]{1,0:T(8,128)(2,1)S(1)}, bf16[96,1728]{1,0:T(8,128)(2,1)S(1)}, u32[]{:S(2)}, u32[]{:S(2)}) collective-permute-start(bf16[96,1728]{1,0:T(8,128)(2,1)S(1)} %concatenate.83), channel_id=1, source_target_pairs={{0,1},{1,2},{2,3},{3,0},{4,5},{5,6},{6,7},{7,4},{8,9},{9,10},{10,1... | collective-permute-start | bytes 995336 | tf_op jit(solution)/shard_map/ppermute | solution.py:484
  9.9 30.2 %copy-start.23 = (bf16[96,192]{1,0:T(8,128)(2,1)S(1)}, bf16[96,192]{1,0:T(8,128)(2,1)}, u32[]{:S(2)}) copy-start(bf16[96,192]{1,0:T(8,128)(2,1)} %param.23) | copy-start | bytes 110596
  37.4 20.5 %collective-permute-start.16 = (bf16[1,4,96,960]{3,2,1,0:T(8,128)(2,1)S(1)}, bf16[1,4,96,960]{3,2,1,0:T(8,128)(2,1)S(1)}, u32[]{:S(2)}, u32[]{:S(2)}) collective-permute-start(bf16[1,4,96,960]{3,2,1,0:T(8,128)(2,1)S(1)} %maximum_bitcast_fusion), channel_id=1, source_target_pairs={{0,8},{4,12},{8,0},{12,4},{16,24},{20,28},{24,16},{28,20},{1,9},{5... | collective-permute-start | bytes 2211848 | tf_op jit(solution)/shard_map/ppermute | solution.py:480
  40.3 11.2 %collective-permute-start.6 = (bf16[96,640]{1,0:T(8,128)(2,1)S(1)}, bf16[96,640]{1,0:T(8,128)(2,1)S(1)}, u32[]{:S(2)}, u32[]{:S(2)}) collective-permute-start(bf16[96,640]{1,0:T(8,128)(2,1)S(1)} %concatenate.76), channel_id=1, source_target_pairs={{0,2},{1,3},{2,0},{3,1},{4,6},{5,7},{6,4},{7,5},{8,10},{9,11},{10,... | collective-permute-start | bytes 368648 | tf_op jit(solution)/shard_map/ppermute | solution.py:484
  43.1 8.9 %collective-permute-start.7 = (bf16[96,640]{1,0:T(8,128)(2,1)S(1)}, bf16[96,640]{1,0:T(8,128)(2,1)S(1)}, u32[]{:S(2)}, u32[]{:S(2)}) collective-permute-start(bf16[96,640]{1,0:T(8,128)(2,1)S(1)} %concatenate.76), channel_id=1, source_target_pairs={{0,3},{1,0},{2,1},{3,2},{4,7},{5,4},{6,5},{7,6},{8,11},{9,8},{10,9... | collective-permute-start | bytes 368648 | tf_op jit(solution)/shard_map/ppermute | solution.py:484
  43.6 10.1 %collective-permute-start.2 = (bf16[96,640]{1,0:T(8,128)(2,1)S(1)}, bf16[96,640]{1,0:T(8,128)(2,1)S(1)}, u32[]{:S(2)}, u32[]{:S(2)}) collective-permute-start(bf16[96,640]{1,0:T(8,128)(2,1)S(1)} %concatenate.76), channel_id=1, source_target_pairs={{0,1},{1,2},{2,3},{3,0},{4,5},{5,6},{6,7},{7,4},{8,9},{9,10},{10,1... | collective-permute-start | bytes 368648 | tf_op jit(solution)/shard_map/ppermute | solution.py:484
  52.1 9.1 %collective-permute-start.8 = (bf16[1,2,96,640]{3,2,1,0:T(8,128)(2,1)S(1)}, bf16[1,2,96,640]{3,2,1,0:T(8,128)(2,1)S(1)}, u32[]{:S(2)}, u32[]{:S(2)}) collective-permute-start(bf16[1,2,96,640]{3,2,1,0:T(8,128)(2,1)S(1)} %maximum_bitcast_fusion.4), channel_id=1, source_target_pairs={{0,16},{4,20},{8,24},{12,28},{16,0},{20,4},{24,8},{28,12},{1,17},{... | collective-permute-start | bytes 737288 | tf_op jit(solution)/shard_map/ppermute | solution.py:480
  53.7 9.7 %collective-permute-start.3 = (bf16[1,2,96,640]{3,2,1,0:T(8,128)(2,1)S(1)}, bf16[1,2,96,640]{3,2,1,0:T(8,128)(2,1)S(1)}, u32[]{:S(2)}, u32[]{:S(2)}) collective-permute-start(bf16[1,2,96,640]{3,2,1,0:T(8,128)(2,1)S(1)} %maximum_bitcast_fusion.3), channel_id=1, source_target_pairs={{0,8},{4,12},{8,0},{12,4},{16,24},{20,28},{24,16},{28,20},{1,9},{5... | collective-permute-start | bytes 737288 | tf_op jit(solution)/shard_map/ppermute | solution.py:480
  59.4 60.2 %collective-permute-start.17 = (bf16[2,4,96,960]{3,2,1,0:T(8,128)(2,1)}, bf16[2,4,96,960]{3,2,1,0:T(8,128)(2,1)}, u32[]{:S(2)}, u32[]{:S(2)}) collective-permute-start(bf16[2,4,96,960]{3,2,1,0:T(8,128)(2,1)} %pad_maximum_fusion.2), channel_id=1, source_target_pairs={{0,16},{4,20},{8,24},{12,28},{16,0},{20,4},{24,8},{28,12},{1,17},{... | collective-permute-start | bytes 4423688 | tf_op jit(solution)/shard_map/ppermute | solution.py:480
  61.2 10.6 %collective-permute-start.9 = (bf16[2,2,96,640]{3,2,1,0:T(8,128)(2,1)S(1)}, bf16[2,2,96,640]{3,2,1,0:T(8,128)(2,1)}, u32[]{:S(2)}, u32[]{:S(2)}) collective-permute-start(bf16[2,2,96,640]{3,2,1,0:T(8,128)(2,1)S(1)} %pad_maximum_fusion.10), channel_id=1, source_target_pairs={{0,8},{4,12},{8,0},{12,4},{16,24},{20,28},{24,16},{28,20},{1,9},{5... | collective-permute-start | bytes 1474568 | tf_op jit(solution)/shard_map/ppermute | solution.py:480
  62.8 53.7 %collective-permute-start.21 = (bf16[1,4,96,768]{3,2,1,0:T(8,128)(2,1)S(1)}, bf16[1,4,96,768]{3,2,1,0:T(8,128)(2,1)}, u32[]{:S(2)}, u32[]{:S(2)}) collective-permute-start(bf16[1,4,96,768]{3,2,1,0:T(8,128)(2,1)S(1)} %maximum_bitcast_fusion.2), channel_id=1, source_target_pairs={{0,16},{4,20},{8,24},{12,28},{16,0},{20,4},{24,8},{28,12},{1,17},{... | collective-permute-start | bytes 1769480 | tf_op jit(solution)/shard_map/ppermute | solution.py:480
  64.3 51.0 %collective-permute-start.4 = (bf16[2,2,96,640]{3,2,1,0:T(8,128)(2,1)}, bf16[2,2,96,640]{3,2,1,0:T(8,128)(2,1)}, u32[]{:S(2)}, u32[]{:S(2)}) collective-permute-start(bf16[2,2,96,640]{3,2,1,0:T(8,128)(2,1)} %pad_maximum_fusion.9), channel_id=1, source_target_pairs={{0,16},{4,20},{8,24},{12,28},{16,0},{20,4},{24,8},{28,12},{1,17},{... | collective-permute-start | bytes 1474568 | tf_op jit(solution)/shard_map/ppermute | solution.py:480
  66.7 57.0 %collective-permute-start = (bf16[256,768]{1,0:T(8,128)(2,1)}, bf16[256,768]{1,0:T(8,128)(2,1)}, u32[]{:S(2)}, u32[]{:S(2)}) collective-permute-start(bf16[256,768]{1,0:T(8,128)(2,1)} %get-tuple-element.160), channel_id=1, source_target_pairs={{0,0},{1,2},{2,4},{3,6},{4,1},{5,3},{6,5},{7,7},{8,8},{9,10},{10,1... | collective-permute-start | bytes 1179656 | tf_op jit(solution)/shard_map/ppermute | solution.py:499
  71.2 44.1 %copy-start.8 = (bf16[1,2,96,640]{3,2,1,0:T(8,128)(2,1)S(1)}, bf16[1,2,96,640]{3,2,1,0:T(8,128)(2,1)}, u32[]{:S(2)}) copy-start(bf16[1,2,96,640]{3,2,1,0:T(8,128)(2,1)} %copy-done.7) | copy-start | bytes 737284
  71.2 44.1 %copy-start.14 = (bf16[1,2,96,640]{3,2,1,0:T(8,128)(2,1)S(1)}, bf16[1,2,96,640]{3,2,1,0:T(8,128)(2,1)}, u32[]{:S(2)}) copy-start(bf16[1,2,96,640]{3,2,1,0:T(8,128)(2,1)} %copy-done.13) | copy-start | bytes 737284
  72.9 45.2 %copy-start.2 = (bf16[4,2,96,640]{3,2,1,0:T(8,128)(2,1)}, bf16[4,2,96,640]{3,2,1,0:T(8,128)(2,1)S(1)}, u32[]{:S(2)}) copy-start(bf16[4,2,96,640]{3,2,1,0:T(8,128)(2,1)S(1)} %pad_maximum_fusion.5.rest_2_.rest_0_) | copy-start | bytes 2949124
  73.0 61.9 %collective-permute-start.10 = (bf16[4,2,96,640]{3,2,1,0:T(8,128)(2,1)S(1)}, bf16[4,2,96,640]{3,2,1,0:T(8,128)(2,1)S(1)}, u32[]{:S(2)}, u32[]{:S(2)}) collective-permute-start(bf16[4,2,96,640]{3,2,1,0:T(8,128)(2,1)S(1)} %pad_maximum_fusion.5.rest_2_.rest_0_), channel_id=1, source_target_pairs={{0,4},{4,0},{8,12},{12,8},{16,20},{20,16},{24,28},{28,24},{1,5},{5... | collective-permute-start | bytes 2949128 | tf_op jit(solution)/shard_map/ppermute | solution.py:480
  116.5 18.4 %collective-permute-start.5 = (bf16[4,2,96,640]{3,2,1,0:T(8,128)(2,1)S(1)}, bf16[4,2,96,640]{3,2,1,0:T(8,128)(2,1)S(1)}, u32[]{:S(2)}, u32[]{:S(2)}) collective-permute-start(bf16[4,2,96,640]{3,2,1,0:T(8,128)(2,1)S(1)} %pad_maximum_fusion.4.rest_0_), channel_id=1, source_target_pairs={{0,4},{4,0},{8,12},{12,8},{16,20},{20,16},{24,28},{28,24},{1,5},{5... | collective-permute-start | bytes 2949128 | tf_op jit(solution)/shard_map/ppermute | solution.py:480
  118.2 29.3 %collective-permute-start.22 = (bf16[2,4,96,768]{3,2,1,0:T(8,128)(2,1)S(1)}, bf16[2,4,96,768]{3,2,1,0:T(8,128)(2,1)S(1)}, u32[]{:S(2)}, u32[]{:S(2)}) collective-permute-start(bf16[2,4,96,768]{3,2,1,0:T(8,128)(2,1)S(1)} %pad_maximum_fusion.3), channel_id=1, source_target_pairs={{0,8},{4,12},{8,0},{12,4},{16,24},{20,28},{24,16},{28,20},{1,9},{5... | collective-permute-start | bytes 3538952 | tf_op jit(solution)/shard_map/ppermute | solution.py:480
  123.1 66.3 %collective-permute-start.18 = (bf16[4,4,96,960]{3,2,1,0:T(8,128)(2,1)}, bf16[4,4,96,960]{3,2,1,0:T(8,128)(2,1)}, u32[]{:S(2)}, u32[]{:S(2)}) collective-permute-start(bf16[4,4,96,960]{3,2,1,0:T(8,128)(2,1)} %pad_maximum_fusion.rest_0_), channel_id=1, source_target_pairs={{0,4},{4,0},{8,12},{12,8},{16,20},{20,16},{24,28},{28,24},{1,5},{5... | collective-permute-start | bytes 8847368 | tf_op jit(solution)/shard_map/ppermute | solution.py:480
  123.7 11.1 %collective-permute-start.1 = (bf16[256,768]{1,0:T(8,128)(2,1)S(1)}, bf16[256,768]{1,0:T(8,128)(2,1)S(1)}, u32[]{:S(2)}, u32[]{:S(2)}) collective-permute-start(bf16[256,768]{1,0:T(8,128)(2,1)S(1)} %copy-done.22), channel_id=1, source_target_pairs={{0,2},{1,0},{2,6},{3,4},{4,3},{5,1},{6,7},{7,5},{8,10},{9,8},{10,1... | collective-permute-start | bytes 1179656 | tf_op jit(solution)/shard_map/ppermute | solution.py:499
  145.1 21.9 %collective-permute-start.11 = (bf16[512,1536]{1,0:T(8,128)(2,1)}, bf16[512,1536]{1,0:T(8,128)(2,1)S(1)}, u32[]{:S(2)}, u32[]{:S(2)}) collective-permute-start(bf16[512,1536]{1,0:T(8,128)(2,1)} %get-tuple-element.59.ko.vo), channel_id=1, source_target_pairs={{0,4},{4,0},{8,12},{12,8},{16,20},{20,16},{24,28},{28,24},{1,5},{5... | collective-permute-start | bytes 4718600 | tf_op jit(solution)/shard_map/ppermute | solution.py:480
  150.3 55.4 %collective-permute-start.23 = (bf16[4,4,96,768]{3,2,1,0:T(8,128)(2,1)}, bf16[4,4,96,768]{3,2,1,0:T(8,128)(2,1)}, u32[]{:S(2)}, u32[]{:S(2)}) collective-permute-start(bf16[4,4,96,768]{3,2,1,0:T(8,128)(2,1)} %pad_maximum_fusion.1.rest_0_.rest_2_), channel_id=1, source_target_pairs={{0,4},{4,0},{8,12},{12,8},{16,20},{20,16},{24,28},{28,24},{1,5},{5... | collective-permute-start | bytes 7077896 | tf_op jit(solution)/shard_map/ppermute | solution.py:480
  150.4 4.2 collective-permute-start.12
  150.8 8.4 %collective-permute-start.19 = (bf16[256,768]{1,0:T(8,128)(2,1)S(1)}, bf16[256,768]{1,0:T(8,128)(2,1)S(1)}, u32[]{:S(2)}, u32[]{:S(2)}) collective-permute-start(bf16[256,768]{1,0:T(8,128)(2,1)S(1)} %get-tuple-element.157), channel_id=1, source_target_pairs={{0,0},{1,2},{2,4},{3,6},{4,1},{5,3},{6,5},{7,7},{8,8},{9,10},{10,1... | collective-permute-start | bytes 1179656 | tf_op jit(solution)/shard_map/ppermute | solution.py:499
  154.5 11.5 %collective-permute-start.20 = (bf16[256,768]{1,0:T(8,128)(2,1)S(1)}, bf16[256,768]{1,0:T(8,128)(2,1)S(1)}, u32[]{:S(2)}, u32[]{:S(2)}) collective-permute-start(bf16[256,768]{1,0:T(8,128)(2,1)S(1)} %get-tuple-element.158), channel_id=1, source_target_pairs={{0,2},{1,0},{2,6},{3,4},{4,3},{5,1},{6,7},{7,5},{8,10},{9,8},{10,1... | collective-permute-start | bytes 1179656 | tf_op jit(solution)/shard_map/ppermute | solution.py:499
  233.7 97.9 %collective-permute-start.45 = (bf16[4,4,96,768]{3,2,1,0:T(8,128)(2,1)}, bf16[4,4,96,768]{3,2,1,0:T(8,128)(2,1)}, u32[]{:S(2)}, u32[]{:S(2)}) collective-permute-start(bf16[4,4,96,768]{3,2,1,0:T(8,128)(2,1)} %get-tuple-element.98), channel_id=1, source_target_pairs={{0,4},{4,0},{8,12},{12,8},{16,20},{20,16},{24,28},{28,24},{1,5},{5... | collective-permute-start | bytes 7077896 | tf_op jit(solution)/shard_map/ppermute | solution.py:480
  269.5 64.2 %collective-permute-start.39 = (bf16[4,4,96,960]{3,2,1,0:T(8,128)(2,1)}, bf16[4,4,96,960]{3,2,1,0:T(8,128)(2,1)S(1)}, u32[]{:S(2)}, u32[]{:S(2)}) collective-permute-start(bf16[4,4,96,960]{3,2,1,0:T(8,128)(2,1)} %get-tuple-element.96), channel_id=1, source_target_pairs={{0,4},{4,0},{8,12},{12,8},{16,20},{20,16},{24,28},{28,24},{1,5},{5... | collective-permute-start | bytes 8847368 | tf_op jit(solution)/shard_map/ppermute | solution.py:480
  282.1 14.7 %collective-permute-start.27 = (bf16[512,768]{1,0:T(8,128)(2,1)S(1)}, bf16[512,768]{1,0:T(8,128)(2,1)S(1)}, u32[]{:S(2)}, u32[]{:S(2)}) collective-permute-start(bf16[512,768]{1,0:T(8,128)(2,1)S(1)} %pad_maximum_fusion.8), channel_id=1, source_target_pairs={{0,4},{4,0},{8,12},{12,8},{16,20},{20,16},{24,28},{28,24},{1,5},{5... | collective-permute-start | bytes 2359304 | tf_op jit(solution)/shard_map/ppermute | solution.py:480
  295.2 15.1 %collective-permute-start.26 = (bf16[512,768]{1,0:T(8,128)(2,1)S(1)}, bf16[512,768]{1,0:T(8,128)(2,1)S(1)}, u32[]{:S(2)}, u32[]{:S(2)}) collective-permute-start(bf16[512,768]{1,0:T(8,128)(2,1)S(1)} %pad_maximum_fusion.7), channel_id=1, source_target_pairs={{0,4},{4,0},{8,12},{12,8},{16,20},{20,16},{24,28},{28,24},{1,5},{5... | collective-permute-start | bytes 2359304 | tf_op jit(solution)/shard_map/ppermute | solution.py:480
  296.1 24.6 %collective-permute-start.24 = (bf16[256,768]{1,0:T(8,128)(2,1)S(1)}, bf16[256,768]{1,0:T(8,128)(2,1)S(1)}, u32[]{:S(2)}, u32[]{:S(2)}) collective-permute-start(bf16[256,768]{1,0:T(8,128)(2,1)S(1)} %get-tuple-element.155), channel_id=1, source_target_pairs={{0,0},{2,1},{4,2},{6,3},{1,4},{3,5},{5,6},{7,7},{8,8},{10,9},{12,1... | collective-permute-start | bytes 1179656 | tf_op jit(solution)/shard_map/ppermute | solution.py:509
  296.8 24.8 %collective-permute-start.25 = (bf16[256,768]{1,0:T(8,128)(2,1)}, bf16[256,768]{1,0:T(8,128)(2,1)}, u32[]{:S(2)}, u32[]{:S(2)}) collective-permute-start(bf16[256,768]{1,0:T(8,128)(2,1)} %get-tuple-element.156), channel_id=1, source_target_pairs={{2,0},{0,1},{6,2},{4,3},{3,4},{1,5},{7,6},{5,7},{10,8},{8,9},{14,1... | collective-permute-start | bytes 1179656 | tf_op jit(solution)/shard_map/ppermute | solution.py:509
  310.3 14.3 %collective-permute-start.30 = (bf16[4,2,96,640]{3,2,1,0:T(8,128)(2,1)}, bf16[4,2,96,640]{3,2,1,0:T(8,128)(2,1)}, u32[]{:S(2)}, u32[]{:S(2)}) collective-permute-start(bf16[4,2,96,640]{3,2,1,0:T(8,128)(2,1)} %get-tuple-element.92), channel_id=1, source_target_pairs={{0,4},{4,0},{8,12},{12,8},{16,20},{20,16},{24,28},{28,24},{1,5},{5... | collective-permute-start | bytes 2949128 | tf_op jit(solution)/shard_map/ppermute | solution.py:480
  320.7 8.1 %collective-permute-start.35 = (bf16[4,2,96,640]{3,2,1,0:T(8,128)(2,1)}, bf16[4,2,96,640]{3,2,1,0:T(8,128)(2,1)}, u32[]{:S(2)}, u32[]{:S(2)}) collective-permute-start(bf16[4,2,96,640]{3,2,1,0:T(8,128)(2,1)} %get-tuple-element.94), channel_id=1, source_target_pairs={{0,4},{4,0},{8,12},{12,8},{16,20},{20,16},{24,28},{28,24},{1,5},{5... | collective-permute-start | bytes 2949128 | tf_op jit(solution)/shard_map/ppermute | solution.py:480
  323.8 12.5 %collective-permute-start.28 = (bf16[256,768]{1,0:T(8,128)(2,1)S(1)}, bf16[256,768]{1,0:T(8,128)(2,1)S(1)}, u32[]{:S(2)}, u32[]{:S(2)}) collective-permute-start(bf16[256,768]{1,0:T(8,128)(2,1)S(1)} %get-tuple-element.151), channel_id=1, source_target_pairs={{0,0},{2,1},{4,2},{6,3},{1,4},{3,5},{5,6},{7,7},{8,8},{10,9},{12,1... | collective-permute-start | bytes 1179656 | tf_op jit(solution)/shard_map/ppermute | solution.py:509
  324.6 21.0 %collective-permute-start.29 = (bf16[256,768]{1,0:T(8,128)(2,1)S(1)}, bf16[256,768]{1,0:T(8,128)(2,1)S(1)}, u32[]{:S(2)}, u32[]{:S(2)}) collective-permute-start(bf16[256,768]{1,0:T(8,128)(2,1)S(1)} %get-tuple-element.152), channel_id=1, source_target_pairs={{2,0},{0,1},{6,2},{4,3},{3,4},{1,5},{7,6},{5,7},{10,8},{8,9},{14,1... | collective-permute-start | bytes 1179656 | tf_op jit(solution)/shard_map/ppermute | solution.py:509
  328.8 16.8 %collective-permute-start.31 = (bf16[2,2,96,640]{3,2,1,0:T(8,128)(2,1)S(1)}, bf16[2,2,96,640]{3,2,1,0:T(8,128)(2,1)S(1)}, u32[]{:S(2)}, u32[]{:S(2)}) collective-permute-start(bf16[2,2,96,640]{3,2,1,0:T(8,128)(2,1)S(1)} %add_convert_fusion.5), channel_id=1, source_target_pairs={{0,16},{4,20},{8,24},{12,28},{16,0},{20,4},{24,8},{28,12},{1,17},{... | collective-permute-start | bytes 1474568 | tf_op jit(solution)/shard_map/ppermute | solution.py:480
  331.6 15.7 %collective-permute-start.36 = (bf16[2,2,96,640]{3,2,1,0:T(8,128)(2,1)S(1)}, bf16[2,2,96,640]{3,2,1,0:T(8,128)(2,1)S(1)}, u32[]{:S(2)}, u32[]{:S(2)}) collective-permute-start(bf16[2,2,96,640]{3,2,1,0:T(8,128)(2,1)S(1)} %add_convert_fusion.4), channel_id=1, source_target_pairs={{0,8},{4,12},{8,0},{12,4},{16,24},{20,28},{24,16},{28,20},{1,9},{5... | collective-permute-start | bytes 1474568 | tf_op jit(solution)/shard_map/ppermute | solution.py:480
  333.7 50.5 %collective-permute-start.46 = (bf16[2,4,96,768]{3,2,1,0:T(8,128)(2,1)S(1)}, bf16[2,4,96,768]{3,2,1,0:T(8,128)(2,1)S(1)}, u32[]{:S(2)}, u32[]{:S(2)}) collective-permute-start(bf16[2,4,96,768]{3,2,1,0:T(8,128)(2,1)S(1)} %add_convert_fusion.1), channel_id=1, source_target_pairs={{0,8},{4,12},{8,0},{12,4},{16,24},{20,28},{24,16},{28,20},{1,9},{5... | collective-permute-start | bytes 3538952 | tf_op jit(solution)/shard_map/ppermute | solution.py:480
  336.2 50.8 %collective-permute-start.40 = (bf16[2,4,96,960]{3,2,1,0:T(8,128)(2,1)S(1)}, bf16[2,4,96,960]{3,2,1,0:T(8,128)(2,1)S(1)}, u32[]{:S(2)}, u32[]{:S(2)}) collective-permute-start(bf16[2,4,96,960]{3,2,1,0:T(8,128)(2,1)S(1)} %add_convert_fusion), channel_id=1, source_target_pairs={{0,16},{4,20},{8,24},{12,28},{16,0},{20,4},{24,8},{28,12},{1,17},{... | collective-permute-start | bytes 4423688 | tf_op jit(solution)/shard_map/ppermute | solution.py:480
  346.7 29.1 %collective-permute-start.32 = (bf16[1,2,96,640]{3,2,1,0:T(8,128)(2,1)S(1)}, bf16[1,2,96,640]{3,2,1,0:T(8,128)(2,1)S(1)}, u32[]{:S(2)}, u32[]{:S(2)}) collective-permute-start(bf16[1,2,96,640]{3,2,1,0:T(8,128)(2,1)S(1)} %add_convert_fusion.7), channel_id=1, source_target_pairs={{0,8},{4,12},{8,0},{12,4},{16,24},{20,28},{24,16},{28,20},{1,9},{5... | collective-permute-start | bytes 737288 | tf_op jit(solution)/shard_map/ppermute | solution.py:480
  348.3 33.4 %collective-permute-start.37 = (bf16[1,2,96,640]{3,2,1,0:T(8,128)(2,1)S(1)}, bf16[1,2,96,640]{3,2,1,0:T(8,128)(2,1)S(1)}, u32[]{:S(2)}, u32[]{:S(2)}) collective-permute-start(bf16[1,2,96,640]{3,2,1,0:T(8,128)(2,1)S(1)} %add_convert_fusion.6), channel_id=1, source_target_pairs={{0,16},{4,20},{8,24},{12,28},{16,0},{20,4},{24,8},{28,12},{1,17},{... | collective-permute-start | bytes 737288 | tf_op jit(solution)/shard_map/ppermute | solution.py:480
  376.9 11.2 %collective-permute-start.33 = (bf16[96,640]{1,0:T(8,128)(2,1)S(1)}, bf16[96,640]{1,0:T(8,128)(2,1)S(1)}, u32[]{:S(2)}, u32[]{:S(2)}) collective-permute-start(bf16[96,640]{1,0:T(8,128)(2,1)S(1)} %get-tuple-element.147), channel_id=1, source_target_pairs={{0,2},{1,3},{2,0},{3,1},{4,6},{5,7},{6,4},{7,5},{8,10},{9,11},{10,... | collective-permute-start | bytes 368648 | tf_op jit(solution)/shard_map/ppermute | solution.py:484
  376.9 11.1 %collective-permute-start.34 = (bf16[96,640]{1,0:T(8,128)(2,1)S(1)}, bf16[96,640]{1,0:T(8,128)(2,1)S(1)}, u32[]{:S(2)}, u32[]{:S(2)}) collective-permute-start(bf16[96,640]{1,0:T(8,128)(2,1)S(1)} %get-tuple-element.148), channel_id=1, source_target_pairs={{0,1},{1,2},{2,3},{3,0},{4,5},{5,6},{6,7},{7,4},{8,9},{9,10},{10,1... | collective-permute-start | bytes 368648 | tf_op jit(solution)/shard_map/ppermute | solution.py:484
  382.7 6.1 %collective-permute-start.38 = (bf16[96,640]{1,0:T(8,128)(2,1)S(1)}, bf16[96,640]{1,0:T(8,128)(2,1)S(1)}, u32[]{:S(2)}, u32[]{:S(2)}) collective-permute-start(bf16[96,640]{1,0:T(8,128)(2,1)S(1)} %fusion.15), channel_id=1, source_target_pairs={{0,3},{1,0},{2,1},{3,2},{4,7},{5,4},{6,5},{7,6},{8,11},{9,8},{10,9... | collective-permute-start | bytes 368648 | tf_op jit(solution)/shard_map/ppermute | solution.py:484
  385.5 14.2 %collective-permute-start.47 = (bf16[1,4,96,768]{3,2,1,0:T(8,128)(2,1)S(1)}, bf16[1,4,96,768]{3,2,1,0:T(8,128)(2,1)S(1)}, u32[]{:S(2)}, u32[]{:S(2)}) collective-permute-start(bf16[1,4,96,768]{3,2,1,0:T(8,128)(2,1)S(1)} %add_convert_fusion.3), channel_id=1, source_target_pairs={{0,16},{4,20},{8,24},{12,28},{16,0},{20,4},{24,8},{28,12},{1,17},{... | collective-permute-start | bytes 1769480 | tf_op jit(solution)/shard_map/ppermute | solution.py:480
  387.5 18.1 %collective-permute-start.41 = (bf16[1,4,96,960]{3,2,1,0:T(8,128)(2,1)S(1)}, bf16[1,4,96,960]{3,2,1,0:T(8,128)(2,1)S(1)}, u32[]{:S(2)}, u32[]{:S(2)}) collective-permute-start(bf16[1,4,96,960]{3,2,1,0:T(8,128)(2,1)S(1)} %add_convert_fusion.2), channel_id=1, source_target_pairs={{0,8},{4,12},{8,0},{12,4},{16,24},{20,28},{24,16},{28,20},{1,9},{5... | collective-permute-start | bytes 2211848 | tf_op jit(solution)/shard_map/ppermute | solution.py:480
  400.9 8.2 %collective-permute-start.48 = (bf16[96,768]{1,0:T(8,128)(2,1)S(1)}, bf16[96,768]{1,0:T(8,128)(2,1)S(1)}, u32[]{:S(2)}, u32[]{:S(2)}) collective-permute-start(bf16[96,768]{1,0:T(8,128)(2,1)S(1)} %get-tuple-element.144), channel_id=1, source_target_pairs={{0,3},{1,0},{2,1},{3,2},{4,7},{5,4},{6,5},{7,6},{8,11},{9,8},{10,9... | collective-permute-start | bytes 442376 | tf_op jit(solution)/shard_map/ppermute | solution.py:484
  402.0 24.0 %collective-permute-start.49 = (bf16[96,768]{1,0:T(8,128)(2,1)S(1)}, bf16[96,768]{1,0:T(8,128)(2,1)S(1)}, u32[]{:S(2)}, u32[]{:S(2)}) collective-permute-start(bf16[96,768]{1,0:T(8,128)(2,1)S(1)} %get-tuple-element.146), channel_id=1, source_target_pairs={{0,2},{1,3},{2,0},{3,1},{4,6},{5,7},{6,4},{7,5},{8,10},{9,11},{10,... | collective-permute-start | bytes 442376 | tf_op jit(solution)/shard_map/ppermute | solution.py:484
  404.0 22.0 %collective-permute-start.50 = (bf16[96,768]{1,0:T(8,128)(2,1)S(1)}, bf16[96,768]{1,0:T(8,128)(2,1)S(1)}, u32[]{:S(2)}, u32[]{:S(2)}) collective-permute-start(bf16[96,768]{1,0:T(8,128)(2,1)S(1)} %get-tuple-element.145), channel_id=1, source_target_pairs={{0,1},{1,2},{2,3},{3,0},{4,5},{5,6},{6,7},{7,4},{8,9},{9,10},{10,1... | collective-permute-start | bytes 442376 | tf_op jit(solution)/shard_map/ppermute | solution.py:484
  406.0 21.7 %collective-permute-start.42 = (bf16[96,960]{1,0:T(8,128)(2,1)S(1)}, bf16[96,960]{1,0:T(8,128)(2,1)S(1)}, u32[]{:S(2)}, u32[]{:S(2)}) collective-permute-start(bf16[96,960]{1,0:T(8,128)(2,1)S(1)} %get-tuple-element.141), channel_id=1, source_target_pairs={{0,3},{1,0},{2,1},{3,2},{4,7},{5,4},{6,5},{7,6},{8,11},{9,8},{10,9... | collective-permute-start | bytes 552968 | tf_op jit(solution)/shard_map/ppermute | solution.py:484
  408.3 24.4 %collective-permute-start.43 = (bf16[96,960]{1,0:T(8,128)(2,1)S(1)}, bf16[96,960]{1,0:T(8,128)(2,1)S(1)}, u32[]{:S(2)}, u32[]{:S(2)}) collective-permute-start(bf16[96,960]{1,0:T(8,128)(2,1)S(1)} %get-tuple-element.143), channel_id=1, source_target_pairs={{0,2},{1,3},{2,0},{3,1},{4,6},{5,7},{6,4},{7,5},{8,10},{9,11},{10,... | collective-permute-start | bytes 552968 | tf_op jit(solution)/shard_map/ppermute | solution.py:484
  409.1 23.6 %collective-permute-start.44 = (bf16[96,960]{1,0:T(8,128)(2,1)S(1)}, bf16[96,960]{1,0:T(8,128)(2,1)S(1)}, u32[]{:S(2)}, u32[]{:S(2)}) collective-permute-start(bf16[96,960]{1,0:T(8,128)(2,1)S(1)} %get-tuple-element.142), channel_id=1, source_target_pairs={{0,1},{1,2},{2,3},{3,0},{4,5},{5,6},{6,7},{7,4},{8,9},{9,10},{10,1... | collective-permute-start | bytes 552968 | tf_op jit(solution)/shard_map/ppermute | solution.py:484
  (26 other events, 155.8 us)
